TPU v7x, 32 devices: a whole 2x2x4 slice. The times are simulated.
32 devices in a mesh: sec: 8 (over z, y), term: 4 (over x, core).
Axes of the slice: x: 2, y: 2, z: 4, core: 2. Of those that a mesh axis runs over, the one named last changes fastest.
Arguments:
- vector: bfloat16 [64, 2, 64, 1024], P('sec'), may hold values from -125 to 125
- right_sector: int32 [64, 2], P('sec'), may hold values from 0 to 63, as said below
- left_env: bfloat16 [64, 26, 4096], P('sec'), may hold values from -0.75 to 0.75
- right_env: bfloat16 [64, 26, 4096], P('sec'), may hold values from -0.21875 to 0.21875
- term_ops: bfloat16 [12, 8, 16, 16], P('term'), may hold values from -0.5 to 0.5
- term_left: int32 [12, 8], P('term'), may hold values from 0 to 25
- group_right: int32 [12], P('term'), may hold values from 0 to 25
Outputs:
- image_one: bfloat16 [64, 2, 64, 1024], P('sec', None, 'term')
- next_vector: bfloat16 [64, 2, 64, 1024], P('sec', None, 'term')
- image_two: bfloat16 [64, 2, 64, 1024], P('sec', None, 'term')
Inputs may be any that keep to these rules, and one draw needn't show every extreme that they name: right_sector[p, j] is a right sector. For every two devices d and e of sec, exactly 2 of the blocks with p in [d * 8, (d + 1) * 8) have right sectors in [e * 8, (e + 1) * 8).
All inputs are finite; a program needn't handle non-finite values.
Results may differ from a plain program's by a relative error of at most 0.0081.
Values may be sent and summed in bfloat16 or wider, within the bound.
No kernel may reach another device: no remote copies, remote signals or barrier semaphores. Data moves between devices by JAX's collectives and lax.ppermute only.
A program may use at most 192 MiB of HBM per device.

v0:
```python
import jax
import jax.numpy as jnp
from jax import lax
from jax.sharding import PartitionSpec as P


def body(vector, right_sector, left_env, right_env, term_ops, term_left, group_right):
    term_count = lax.axis_size("term")
    per_device, pair_count, block_rows, row_width = vector.shape
    phys_width = row_width // block_rows
    block_count = per_device * pair_count
    slab_rows = block_rows // term_count
    env_width = left_env.shape[1]
    left_square = left_env.reshape(per_device, env_width, block_rows, block_rows)
    row_count = left_square.shape[2]
    group_count = group_right.shape[0]
    destination = (right_sector // per_device).reshape(block_count)
    ordering = jnp.argsort(destination, stable=True)
    inverse = jnp.argsort(ordering, stable=True)
    sorted_sector = right_sector.reshape(block_count)[ordering]
    right_chosen = jnp.take(right_env, group_right, axis=1)
    sec_first = lax.axis_index("sec") * per_device

    def left_section(source):
        block_view = source.reshape(per_device, pair_count, block_rows, phys_width, block_rows)

        def one_group(inputs):
            operator, indices = inputs
            stacked = jnp.take(left_square, indices, axis=1)
            contracted = jnp.einsum(
                "ptxl,pjlsr->pjtxsr", stacked, block_view, preferred_element_type=jnp.float32
            ).astype(jnp.bfloat16)
            summed = jnp.einsum(
                "tys,pjtxsr->pjxyr", operator, contracted, preferred_element_type=jnp.float32
            )
            return summed.astype(jnp.bfloat16).reshape(
                block_count, row_count, phys_width, block_rows
            )

        pieces = lax.map(one_group, (term_ops, term_left))
        return jnp.moveaxis(pieces, 0, 1)

    def right_section(mixed_terms, environment):
        matrices = environment.reshape(environment.shape[0], group_count, block_rows, block_rows)
        return jnp.einsum(
            "ngxyr,ngzr->nxyz", mixed_terms, matrices, preferred_element_type=jnp.float32
        )

    def finish_rows(partial_value):
        return lax.psum_scatter(partial_value, "term", scatter_dimension=1, tiled=True).astype(
            jnp.bfloat16
        )

    def apply_operator(source):
        mixed_terms = left_section(source)[ordering]
        arrived, arrived_sector = (
            lax.all_to_all(mixed_terms, "sec", split_axis=0, concat_axis=0, tiled=True),
            lax.all_to_all(sorted_sector, "sec", split_axis=0, concat_axis=0, tiled=True),
        )
        environment = right_chosen[arrived_sector - sec_first]
        row_share = finish_rows(right_section(arrived, environment))
        returned = lax.all_to_all(row_share, "sec", split_axis=0, concat_axis=0, tiled=True)
        return returned[inverse]

    first_image = apply_operator(vector).reshape(per_device, pair_count, slab_rows, row_width)
    own_rows = lax.dynamic_slice_in_dim(
        vector, lax.axis_index("term") * slab_rows, slab_rows, 2
    ).astype(jnp.float32)
    image_rows = first_image.astype(jnp.float32)
    norm_sq, correlation = lax.psum(
        (jnp.sum(own_rows * own_rows), jnp.sum(own_rows * image_rows)), ("sec", "term")
    )
    ratio = correlation / norm_sq
    residual_rows = image_rows - ratio * own_rows
    residual_sq = lax.psum(jnp.sum(residual_rows * residual_rows), ("sec", "term"))
    next_rows = (residual_rows * jnp.sqrt(norm_sq / (residual_sq + 1e-06))).astype(jnp.bfloat16)
    next_full = lax.all_gather(next_rows, "term", axis=2, tiled=True)
    second_image = apply_operator(next_full).reshape(per_device, pair_count, slab_rows, row_width)
    return (first_image, next_rows, second_image)


def solution(mesh):
    in_specs = (
        P("sec", None, None, None),
        P("sec", None),
        P("sec", None, None),
        P("sec", None, None),
        P("term", None, None, None),
        P("term", None),
        P("term"),
    )
    out_specs = (
        P("sec", None, "term", None),
        P("sec", None, "term", None),
        P("sec", None, "term", None),
    )
    return jax.shard_map(body, mesh=mesh, in_specs=in_specs, out_specs=out_specs, check_vma=False)
```

profile of v0, /device:TPU:0, one launch (start us, length us, event | category | flops | bytes accessed | tf_op | source)
XLA Modules:
  0.0 1156.9 jit_solution(14313248477417615760)
XLA Ops:
  12.1 7.3 all-to-all-start.1
  19.4 5.9 reshape.68
  30.0 6.4 reshape.69
  36.4 5.2 copy.69
  41.6 7.4 broadcast.72.clone2
  49.1 187.6 %while.20 = (s32[]{:T(128)}, bf16[3,16,64,16,64]{4,3,2,0,1:T(8,128)(2,1)}, s32[3,8]{1,0:T(4,128)S(1)}, bf16[8,26,64,64]{3,2,1,0:T(8,128)(2,1)}, bf16[8,2,64,16,6...) while((s32[]{:T(128)}, bf16[3,16,64,16,64]{4,3,2,0,1:T(8,128)(2,1)}, ...), condition=%wide.region_1.3_spmd, body=%wide.region_0.2_spmd.sunk | while | flops 1351877632 | bytes 47747812 | solution.py:40
  52.2 16.3 %convert_bitcast_fusion.6 = bf16[8,2,8,64,16,64]{5,3,4,1,2,0:T(8,128)(2,1)} fusion(bf16[8,2,64,16,64]{4,2,3,1,0:T(8,128)(2,1)} %get-tuple-element.254, bf16[8,8,64,64]{3,2,1,0:T(8,128)(2,1)S(1)} %gather_fusion, pred[8]{0:T(512)(128)(4,1)S(1)} %get-tuple-element.227), kind=kOutput, calls=%fused_computation.11.clone.1 | convolution fusion | flops 1082392576 | bytes 19398664 | tf_op jit(solution)/shard_map/while/body/eval_jaxpr/ptxl,pjlsr->pjtxsr/dot_general | solution.py:30
  68.5 34.0 %bitcast_convert_fusion.4 = bf16[8,2,64,64,16]{3,4,2,1,0:T(8,128)(2,1)} fusion(bf16[8,2,8,64,16,64]{5,3,4,1,2,0:T(8,128)(2,1)} %convert_bitcast_fusion.6, bf16[3,8,16,16]{3,2,1,0:T(8,128)(2,1)S(1)} %get-tuple-element.255, s32[]{:T(128)} %get-tuple-element.243), kind=kOutput, calls=%fused_computation.12.clone.1 | convolution fusion | flops 269484032 | bytes 18907140 | tf_op jit(solution)/shard_map/while/body/eval_jaxpr/tys,pjtxsr->pjxyr/dot_general | solution.py:33
  110.3 16.3 %convert_bitcast_fusion.6 = bf16[8,2,8,64,16,64]{5,3,4,1,2,0:T(8,128)(2,1)} fusion(bf16[8,2,64,16,64]{4,2,3,1,0:T(8,128)(2,1)} %get-tuple-element.254, bf16[8,8,64,64]{3,2,1,0:T(8,128)(2,1)S(1)} %gather_fusion, pred[8]{0:T(512)(128)(4,1)S(1)} %get-tuple-element.227), kind=kOutput, calls=%fused_computation.11.clone.1 | convolution fusion | flops 1082392576 | bytes 19398664 | tf_op jit(solution)/shard_map/while/body/eval_jaxpr/ptxl,pjlsr->pjtxsr/dot_general | solution.py:30
  126.6 34.0 %bitcast_convert_fusion.4 = bf16[8,2,64,64,16]{3,4,2,1,0:T(8,128)(2,1)} fusion(bf16[8,2,8,64,16,64]{5,3,4,1,2,0:T(8,128)(2,1)} %convert_bitcast_fusion.6, bf16[3,8,16,16]{3,2,1,0:T(8,128)(2,1)S(1)} %get-tuple-element.255, s32[]{:T(128)} %get-tuple-element.243), kind=kOutput, calls=%fused_computation.12.clone.1 | convolution fusion | flops 269484032 | bytes 18907140 | tf_op jit(solution)/shard_map/while/body/eval_jaxpr/tys,pjtxsr->pjxyr/dot_general | solution.py:33
  160.7 5.1 constant_dynamic-update-slice_fusion.4
  168.5 16.3 %convert_bitcast_fusion.6 = bf16[8,2,8,64,16,64]{5,3,4,1,2,0:T(8,128)(2,1)} fusion(bf16[8,2,64,16,64]{4,2,3,1,0:T(8,128)(2,1)} %get-tuple-element.254, bf16[8,8,64,64]{3,2,1,0:T(8,128)(2,1)S(1)} %gather_fusion, pred[8]{0:T(512)(128)(4,1)S(1)} %get-tuple-element.227), kind=kOutput, calls=%fused_computation.11.clone.1 | convolution fusion | flops 1082392576 | bytes 19398664 | tf_op jit(solution)/shard_map/while/body/eval_jaxpr/ptxl,pjlsr->pjtxsr/dot_general | solution.py:30
  184.8 34.0 %bitcast_convert_fusion.4 = bf16[8,2,64,64,16]{3,4,2,1,0:T(8,128)(2,1)} fusion(bf16[8,2,8,64,16,64]{5,3,4,1,2,0:T(8,128)(2,1)} %convert_bitcast_fusion.6, bf16[3,8,16,16]{3,2,1,0:T(8,128)(2,1)S(1)} %get-tuple-element.255, s32[]{:T(128)} %get-tuple-element.243), kind=kOutput, calls=%fused_computation.12.clone.1 | convolution fusion | flops 269484032 | bytes 18907140 | tf_op jit(solution)/shard_map/while/body/eval_jaxpr/tys,pjtxsr->pjxyr/dot_general | solution.py:33
  218.8 5.1 constant_dynamic-update-slice_fusion.4
  236.7 11.1 gather_fusion.2
  247.8 12.8 %copy.128 = bf16[16,3,64,16,64]{4,2,1,3,0:T(8,128)(2,1)} copy(bf16[16,3,64,16,64]{4,3,2,1,0:T(8,128)(2,1)} %gather_fusion.2) | data formatting | bytes 12582912 | tf_op jit(solution)/shard_map/gather | solution.py:55
  260.7 13.8 %reshape.179 = bf16[8,2,196608]{2,1,0:T(2,128)(2,1)} reshape(bf16[16,16,3,64,64]{4,3,2,1,0:T(8,128)(2,1)} %bitcast.143) | data formatting | bytes 12582912
  274.5 6.0 all-to-all-start
  284.4 133.8 %all-to-all-done = bf16[8,2,196608]{2,1,0:T(2,128)(2,1)} async-done(((bf16[8,2,196608]{2,1,0:T(2,128)(2,1)}), bf16[8,2,196608]{2,1,0:T(2,128)(2,1)}, u32[]{:S(2)}, u32[]{:S(2)}) %all-to-all-start) | async-done | bytes 6291488 | tf_op jit(solution)/shard_map/all_to_all | solution.py:57
  418.1 13.3 %reshape.180 = bf16[16,16,3,64,64]{4,3,2,1,0:T(8,128)(2,1)} reshape(bf16[8,2,196608]{2,1,0:T(2,128)(2,1)} %all-to-all-done) | data formatting | bytes 12582912
  431.5 11.2 convolution_bitcast_fusion.1
  442.7 71.0 %reduce-scatter.3.cloned.1.call-done = f32[16,16,16,64]{3,1,2,0:T(8,128)} async-done(((f32[16,64,16,64]{3,1,2,0:T(8,128)}), f32[16,16,16,64]{3,1,2,0:T(8,128)}) %reduce-scatter.3.cloned.1.call-update) | async-done | bytes 1048592 | tf_op jit(solution)/shard_map/reduce_scatter | solution.py:50
  516.9 5.5 all-to-all-start.2
  523.7 13.1 %all-to-all-done.2 = bf16[8,2,16384]{2,1,0:T(2,128)(2,1)S(1)} async-done(((bf16[8,2,16384]{2,1,0:T(2,128)(2,1)}), bf16[8,2,16384]{2,1,0:T(2,128)(2,1)S(1)}, u32[]{:S(2)}, u32[]{:S(2)}) %all-to-all-start.2) | async-done | bytes 524320 | tf_op jit(solution)/shard_map/all_to_all | solution.py:62
  541.4 38.7 %all-reduce = (f32[]{:T(128)}, f32[]{:T(128)}) all-reduce(f32[]{:T(128)} %get-tuple-element.123, f32[]{:T(128)} %get-tuple-element.122), channel_id=1, replica_groups=mesh['sec'=8,'term'=4] {'sec','term'}, use_global_device_ids=true, to_apply=%region_8.10 | all-reduce | flops 2 | bytes 16 | tf_op jit(solution)/shard_map/psum | solution.py:70
  583.4 41.1 %psum.23 = f32[]{:T(128)} all-reduce(f32[]{:T(128)} %multiply_reduce_fusion), channel_id=1, replica_groups=mesh['sec'=8,'term'=4] {'sec','term'}, use_global_device_ids=true, to_apply=%region_10.12 | all-reduce | flops 1 | bytes 8 | tf_op jit(solution)/shard_map/psum | solution.py:75
  628.0 22.0 %all-gather.2.cloned.1.call-done = bf16[8,2,64,1024]{3,2,1,0:T(8,128)(2,1)} async-done(((bf16[8,2,16,1024]{3,2,1,0:T(8,128)(2,1)}), bf16[8,2,64,1024]{3,2,1,0:T(8,128)(2,1)}) %all-gather.2.cloned.1.call-update) | async-done | bytes 2097168 | tf_op jit(solution)/shard_map/all_gather | solution.py:77
  649.9 6.4 reshape.74
  656.3 5.2 copy.80
  661.5 7.4 broadcast.72.clone
  669.0 175.0 %while.21 = (s32[]{:T(128)}, bf16[3,16,64,16,64]{4,3,2,0,1:T(8,128)(2,1)}, s32[3,8]{1,0:T(4,128)S(1)}, bf16[8,26,64,64]{3,2,1,0:T(8,128)(2,1)}, bf16[8,2,64,16,6...) while((s32[]{:T(128)}, bf16[3,16,64,16,64]{4,3,2,0,1:T(8,128)(2,1)}, ...), condition=%wide.region_12.14_spmd, body=%wide.region_11.13_spmd.sunk | while | flops 1351877632 | bytes 47747812 | solution.py:40
  672.1 16.3 %convert_bitcast_fusion.7 = bf16[8,2,8,64,16,64]{5,3,4,1,2,0:T(8,128)(2,1)} fusion(bf16[8,2,64,16,64]{4,2,3,1,0:T(8,128)(2,1)} %get-tuple-element.275, bf16[8,8,64,64]{3,2,1,0:T(8,128)(2,1)S(1)} %gather_fusion.1, pred[8]{0:T(512)(128)(4,1)S(1)} %get-tuple-element.235), kind=kOutput, calls=%fused_computation.27.clone.1 | convolution fusion | flops 1082392576 | bytes 19398664 | tf_op jit(solution)/shard_map/while/body/eval_jaxpr/ptxl,pjlsr->pjtxsr/dot_general | solution.py:30
  688.4 34.0 %bitcast_convert_fusion.5 = bf16[8,2,64,64,16]{3,4,2,1,0:T(8,128)(2,1)} fusion(bf16[8,2,8,64,16,64]{5,3,4,1,2,0:T(8,128)(2,1)} %convert_bitcast_fusion.7, bf16[3,8,16,16]{3,2,1,0:T(8,128)(2,1)S(1)} %get-tuple-element.276, s32[]{:T(128)} %get-tuple-element.264), kind=kOutput, calls=%fused_computation.28.clone.1 | convolution fusion | flops 269484032 | bytes 18907140 | tf_op jit(solution)/shard_map/while/body/eval_jaxpr/tys,pjtxsr->pjxyr/dot_general | solution.py:33
  722.4 5.0 constant_dynamic-update-slice_fusion.5
  730.2 16.3 %convert_bitcast_fusion.7 = bf16[8,2,8,64,16,64]{5,3,4,1,2,0:T(8,128)(2,1)} fusion(bf16[8,2,64,16,64]{4,2,3,1,0:T(8,128)(2,1)} %get-tuple-element.275, bf16[8,8,64,64]{3,2,1,0:T(8,128)(2,1)S(1)} %gather_fusion.1, pred[8]{0:T(512)(128)(4,1)S(1)} %get-tuple-element.235), kind=kOutput, calls=%fused_computation.27.clone.1 | convolution fusion | flops 1082392576 | bytes 19398664 | tf_op jit(solution)/shard_map/while/body/eval_jaxpr/ptxl,pjlsr->pjtxsr/dot_general | solution.py:30
  746.5 34.0 %bitcast_convert_fusion.5 = bf16[8,2,64,64,16]{3,4,2,1,0:T(8,128)(2,1)} fusion(bf16[8,2,8,64,16,64]{5,3,4,1,2,0:T(8,128)(2,1)} %convert_bitcast_fusion.7, bf16[3,8,16,16]{3,2,1,0:T(8,128)(2,1)S(1)} %get-tuple-element.276, s32[]{:T(128)} %get-tuple-element.264), kind=kOutput, calls=%fused_computation.28.clone.1 | convolution fusion | flops 269484032 | bytes 18907140 | tf_op jit(solution)/shard_map/while/body/eval_jaxpr/tys,pjtxsr->pjxyr/dot_general | solution.py:33
  780.6 5.1 constant_dynamic-update-slice_fusion.5
  788.4 16.3 %convert_bitcast_fusion.7 = bf16[8,2,8,64,16,64]{5,3,4,1,2,0:T(8,128)(2,1)} fusion(bf16[8,2,64,16,64]{4,2,3,1,0:T(8,128)(2,1)} %get-tuple-element.275, bf16[8,8,64,64]{3,2,1,0:T(8,128)(2,1)S(1)} %gather_fusion.1, pred[8]{0:T(512)(128)(4,1)S(1)} %get-tuple-element.235), kind=kOutput, calls=%fused_computation.27.clone.1 | convolution fusion | flops 1082392576 | bytes 19398664 | tf_op jit(solution)/shard_map/while/body/eval_jaxpr/ptxl,pjlsr->pjtxsr/dot_general | solution.py:30
  804.7 34.0 %bitcast_convert_fusion.5 = bf16[8,2,64,64,16]{3,4,2,1,0:T(8,128)(2,1)} fusion(bf16[8,2,8,64,16,64]{5,3,4,1,2,0:T(8,128)(2,1)} %convert_bitcast_fusion.7, bf16[3,8,16,16]{3,2,1,0:T(8,128)(2,1)S(1)} %get-tuple-element.276, s32[]{:T(128)} %get-tuple-element.264), kind=kOutput, calls=%fused_computation.28.clone.1 | convolution fusion | flops 269484032 | bytes 18907140 | tf_op jit(solution)/shard_map/while/body/eval_jaxpr/tys,pjtxsr->pjxyr/dot_general | solution.py:33
  838.7 5.1 constant_dynamic-update-slice_fusion.5
  844.0 11.2 gather_fusion.7
  855.2 12.8 %copy.127 = bf16[16,3,64,16,64]{4,2,1,3,0:T(8,128)(2,1)} copy(bf16[16,3,64,16,64]{4,3,2,1,0:T(8,128)(2,1)} %gather_fusion.7) | data formatting | bytes 12582912 | tf_op jit(solution)/shard_map/gather | solution.py:55
  868.0 13.8 %reshape.183 = bf16[8,2,196608]{2,1,0:T(2,128)(2,1)} reshape(bf16[16,16,3,64,64]{4,3,2,1,0:T(8,128)(2,1)} %bitcast.144) | data formatting | bytes 12582912
  881.8 144.1 %all_to_all.30 = bf16[8,2,196608]{2,1,0:T(2,128)(2,1)} all-to-all(bf16[8,2,196608]{2,1,0:T(2,128)(2,1)} %reshape.183), channel_id=1, replica_groups=mesh['sec'=8,'term'=4] {'sec'}, dimensions={0} | all-to-all | bytes 12582912 | tf_op jit(solution)/shard_map/all_to_all | solution.py:57
  1026.0 13.4 %reshape.184 = bf16[16,16,3,64,64]{4,3,2,1,0:T(8,128)(2,1)} reshape(bf16[8,2,196608]{2,1,0:T(2,128)(2,1)} %all_to_all.30) | data formatting | bytes 12582912
  1039.4 11.3 convolution_bitcast_fusion
  1050.7 70.0 %reduce-scatter.5.cloned.1.call-done = f32[16,16,16,64]{3,1,2,0:T(8,128)} async-done(((f32[16,64,16,64]{3,1,2,0:T(8,128)}), f32[16,16,16,64]{3,1,2,0:T(8,128)}) %reduce-scatter.5.cloned.1.call-update) | async-done | bytes 1048592 | tf_op jit(solution)/shard_map/reduce_scatter | solution.py:50
  1123.1 20.0 %all_to_all.31 = bf16[8,2,16384]{2,1,0:T(2,128)(2,1)} all-to-all(bf16[8,2,16384]{2,1,0:T(2,128)(2,1)S(1)} %reshape.185), channel_id=1, replica_groups=mesh['sec'=8,'term'=4] {'sec'}, dimensions={0} | all-to-all | bytes 1048576 | tf_op jit(solution)/shard_map/all_to_all | solution.py:62
  (94 shorter events, 57.6 us)
Async XLA Ops:
  7.2 273.4 %copy-start = (bf16[8,26,4096]{2,0,1:T(8,128)(2,1)S(1)}, bf16[8,26,4096]{2,0,1:T(8,128)(2,1)}, u32[]{:S(2)}) copy-start(bf16[8,26,4096]{2,0,1:T(8,128)(2,1)} %param.16) | copy-start | bytes 5111812
  10.2 0.5 copy-start.10
  10.7 226.0 %copy-start.6 = (s32[1024]{0:T(1024)}, s32[1024]{0:T(1024)S(1)}, u32[]{:S(2)}) copy-start(s32[1024]{0:T(1024)S(1)} %pad_clamp_fusion.5) | copy-start | bytes 12292
  12.1 262.4 %all-to-all-start.1 = ((s32[8,2,1]{1,2,0:T(1,128)}), s32[8,2,1]{1,2,0:T(1,128)}, u32[]{:S(2)}, u32[]{:S(2)}) async-start(s32[8,2,1]{1,2,0:T(1,128)} %bitcast.28), calls=%async_computation.1 | async-start | bytes 8192 | tf_op jit(solution)/shard_map/all_to_all | solution.py:58
  30.0 19.1 %copy-start.5 = (s32[3,8]{1,0:T(4,128)S(1)}, s32[3,8]{1,0:T(4,128)}, u32[]{:S(2)}) copy-start(s32[3,8]{1,0:T(4,128)} %param.18) | copy-start | bytes 292
  30.0 19.1 %copy-start.8 = (bf16[3,8,16,16]{3,2,1,0:T(8,128)(2,1)S(1)}, bf16[3,8,16,16]{3,2,1,0:T(8,128)(2,1)}, u32[]{:S(2)}) copy-start(bf16[3,8,16,16]{3,2,1,0:T(8,128)(2,1)} %param.17) | copy-start | bytes 36868
  260.7 19.9 %copy-start.9 = (s32[3]{0:T(128)S(1)}, s32[3]{0:T(128)}, u32[]{:S(2)}) copy-start(s32[3]{0:T(128)} %param.19) | copy-start | bytes 40
  274.5 143.7 %all-to-all-start = ((bf16[8,2,196608]{2,1,0:T(2,128)(2,1)}), bf16[8,2,196608]{2,1,0:T(2,128)(2,1)}, u32[]{:S(2)}, u32[]{:S(2)}) async-start(bf16[8,2,196608]{2,1,0:T(2,128)(2,1)} %reshape.179), calls=%async_computation | async-start | bytes 12582912 | tf_op jit(solution)/shard_map/all_to_all | solution.py:57
  280.5 233.1 %reduce-scatter.3.cloned.1.call-start = ((), (), s32[]{:S(2)}) async-start(), calls=%async_computation.7 | async-start | bytes 10485760 | tf_op jit(solution)/shard_map/reduce_scatter | solution.py:50
  284.4 158.3 %copy-start.3 = (bf16[16,3,64,64]{3,2,0,1:T(8,128)(2,1)}, bf16[16,3,64,64]{3,2,0,1:T(8,128)(2,1)S(1)}, u32[]{:S(2)}) copy-start(bf16[16,3,64,64]{3,2,0,1:T(8,128)(2,1)S(1)} %reshape.72) | copy-start | bytes 1179652
  431.5 91.0 %copy-start.11 = (s32[16]{0:T(128)S(1)}, s32[16]{0:T(128)}, u32[]{:S(2)}) copy-start(s32[16]{0:T(128)} %copy-done.10) | copy-start | bytes 196
  516.9 20.0 %all-to-all-start.2 = ((bf16[8,2,16384]{2,1,0:T(2,128)(2,1)}), bf16[8,2,16384]{2,1,0:T(2,128)(2,1)S(1)}, u32[]{:S(2)}, u32[]{:S(2)}) async-start(bf16[8,2,16384]{2,1,0:T(2,128)(2,1)} %reshape.181), calls=%async_computation.3 | async-start | bytes 1048576 | tf_op jit(solution)/shard_map/all_to_all | solution.py:62
  522.4 127.5 %all-gather.2.cloned.1.call-start = ((), (), s32[]{:S(2)}) async-start(), calls=%async_computation.8 | async-start | bytes 2621440 | tf_op jit(solution)/shard_map/all_gather | solution.py:77
  523.7 137.8 %copy-start.7 = (s32[1024]{0:T(1024)}, s32[1024]{0:T(1024)S(1)}, u32[]{:S(2)}) copy-start(s32[1024]{0:T(1024)S(1)} %pad_clamp_fusion.2) | copy-start | bytes 12292
  539.3 129.7 %copy-start.2 = (bf16[8,2,16,1024]{3,2,1,0:T(8,128)(2,1)}, bf16[8,2,16,1024]{3,2,1,0:T(8,128)(2,1)S(1)}, u32[]{:S(2)}) copy-start(bf16[8,2,16,1024]{3,2,1,0:T(8,128)(2,1)S(1)} %reshape.73) | copy-start | bytes 1572868
  627.9 492.7 %reduce-scatter.5.cloned.1.call-start = ((), (), s32[]{:S(2)}) async-start(), calls=%async_computation.9 | async-start | bytes 10485760 | tf_op jit(solution)/shard_map/reduce_scatter | solution.py:50
  1026.0 13.4 %copy-start.4 = (bf16[16,3,64,64]{3,2,0,1:T(8,128)(2,1)S(1)}, bf16[16,3,64,64]{3,2,0,1:T(8,128)(2,1)}, u32[]{:S(2)}) copy-start(bf16[16,3,64,64]{3,2,0,1:T(8,128)(2,1)} %copy-done.3) | copy-start | bytes 1179652
  1039.3 110.8 %copy-start.1 = (bf16[8,26,4096]{2,0,1:T(8,128)(2,1)S(1)}, bf16[8,26,4096]{2,0,1:T(8,128)(2,1)}, u32[]{:S(2)}) copy-start(bf16[8,26,4096]{2,0,1:T(8,128)(2,1)} %param.16) | copy-start | bytes 5111812
Sparse Core Ops, SparseCore 0:
  442.8 70.7 reduce-scatter.2
  628.0 21.8 all-gather.1
  1050.8 69.8 reduce-scatter.4
where the time goes:
time: 1160 us
  matrix products  325 us (28%)
  waiting for transfers between devices  310 us (27%)
  blocking collectives  244 us (21%)
  local copies, waits for them, and re-layouts  215 us (19%)
  starting transfers between devices  18.9 us (2%)
  between operations  16.9 us (1%)
  other arithmetic  13.9 us (1%)
  loops' own time  13.8 us (1%)
    dot_general x6, matrix products, one_group(): jnp.einsum('tys,pjtxsr->pjxyr', operator, contracted, preferred_element_t...  204 us
    all_to_all x1, blocking collectives, apply_operator(): lax.all_to_all(mixed_terms, 'sec', split_axis=0, concat_axis=0, tiled=True)  144 us
    reduce_scatter x2, waiting for transfers between devices, finish_rows(): lax.psum_scatter(partial_value, 'term', scatter_dimension=1, tiled=True)  141 us
    all_to_all x1, waiting for transfers between devices, apply_operator(): lax.all_to_all(mixed_terms, 'sec', split_axis=0, concat_axis=0, tiled=True)  134 us
    dot_general x6, matrix products, one_group(): jnp.einsum('ptxl,pjlsr->pjtxsr', stacked, block_view, preferred_element_t...  97.8 us
    unnamed x33, local copies, waits for them, and re-layouts  60.8 us
    gather x4, local copies, waits for them, and re-layouts, apply_operator(): mixed_terms = left_section(source)[ordering]  48 us
    psum x1, blocking collectives, body(): lax.psum(jnp.sum(residual_rows * residual_rows), ('sec', 'term'))  41.1 us
  transfers between devices with their start and end apart: 6, of which 5 were waited for; matrix products, arithmetic and copies ran while one was open for 21% of the time, Pallas kernels for 0%

commit v1 on v0

v1 whole, which is shorter than its diff:
```python
import functools

import jax
import jax.numpy as jnp
from jax import lax
from jax.experimental import pallas as pl
from jax.experimental.pallas import tpu as pltpu
from jax.sharding import PartitionSpec as P

BF = jnp.bfloat16
F32 = jnp.float32
VMEM_LIMIT = 48 * 1024 * 1024


def low_half(shape):
    return lax.broadcasted_iota(jnp.int32, shape, len(shape) - 1) < shape[-1] // 2


def swap(tile):
    return pltpu.roll(tile, tile.shape[-1] // 2, 1)


def two_in_lanes(first, second):
    low = low_half(first.shape)
    return jnp.where(low, first, swap(second)), jnp.where(low, swap(first), second)


def fill_left(lhs, left_refs, wide):
    env_width = left_refs[0].shape[1]
    lane = 2 * wide
    depth = -(-env_width // 16) * 16
    lhs[...] = jnp.zeros_like(lhs)
    low = low_half((env_width, lane))
    for pair in range(wide // 2):
        for b, ref in enumerate(left_refs):
            tile = ref[0, :, pair * lane : (pair + 1) * lane].astype(F32)
            base = 2 * pair * depth
            cols = slice(b * lane, (b + 1) * lane)
            lhs[base : base + env_width, cols] = jnp.where(low, tile, 0.0).astype(BF)
            lhs[base + depth : base + depth + env_width, cols] = jnp.where(low, 0.0, tile).astype(BF)


def put_source(rhs, s, tile):
    rows, lane = tile.shape
    low = low_half(tile.shape)
    kept = (jnp.where(low, tile, 0.0).astype(BF), jnp.where(low, 0.0, tile).astype(BF))
    for b in range(2):
        for copy in range(2):
            base = (2 * b + copy) * rows
            rhs[base : base + rows, s * lane : (s + 1) * lane] = kept[b]


def contract_left(lhs, rhs, con, chunk=512):
    step = 256
    for n in range(rhs.shape[1] // step):
        cols = slice(n * step, (n + 1) * step)

        def one(i, carry):
            rows = pl.ds(pl.multiple_of(i * chunk, chunk), chunk)
            con[rows, cols] = jnp.dot(
                lhs[rows, :], rhs[:, cols], preferred_element_type=F32
            ).astype(BF)
            return carry

        lax.fori_loop(0, lhs.shape[0] // chunk, one, 0, unroll=True)


def mix(amat, con, mixed, phys, lane):
    depth = amat.shape[1] // phys
    groups = amat.shape[0] // phys
    pairs = con.shape[0] // depth // 2

    def one(pair, carry):
        halves = []
        for parity in range(2):
            rows = pl.ds(pl.multiple_of((2 * pair + parity) * depth, depth), depth)
            halves.append(
                jnp.concatenate(
                    [con[rows, s * lane : (s + 1) * lane] for s in range(phys)], axis=0
                )
            )
        out = jnp.dot(
            amat[...], jnp.concatenate(halves, axis=1), preferred_element_type=F32
        ).astype(BF)
        for parity in range(2):
            rows = pl.ds(pl.multiple_of((2 * pair + parity) * phys, phys), phys)
            for g in range(groups):
                mixed[rows, g * lane : (g + 1) * lane] = out[
                    g * phys : (g + 1) * phys, parity * lane : (parity + 1) * lane
                ]
        return carry

    lax.fori_loop(0, pairs, one, 0, unroll=2)


def fill_right(rmat, right_tiles, lane):
    for b, get in enumerate(right_tiles):
        wide = lane // 2
        rows = slice(b * wide, (b + 1) * wide)
        low = low_half((wide, lane))
        for pair in range(rmat.shape[1] // (2 * lane)):
            tile = get(pair).astype(F32)
            turned = swap(tile)
            if b == 0:
                first, second = jnp.where(low, tile, 0.0), jnp.where(low, turned, 0.0)
            else:
                first, second = jnp.where(low, 0.0, turned), jnp.where(low, 0.0, tile)
            rmat[rows, 2 * pair * lane : (2 * pair + 1) * lane] = first.astype(BF)
            rmat[rows, (2 * pair + 1) * lane : (2 * pair + 2) * lane] = second.astype(BF)


def contract_right(mixed, rmat, acc, chunk=256):
    for i in range(mixed.shape[0] // chunk):
        rows = slice(i * chunk, (i + 1) * chunk)
        acc[rows, :] = lax.dot_general(
            mixed[rows, :], rmat[...], (((1,), (1,)), ((), ())), preferred_element_type=F32
        )


def copy_operator(amat, parts):
    rows = amat.shape[0] // len(parts)
    for k, part in enumerate(parts):
        amat[k * rows : (k + 1) * rows, :] = part[:rows, :]


def left_kernel(parts_count, wide, phys, _, left_a, left_b, vec_a, vec_b, *refs):
    parts = refs[:parts_count]
    mixed, both, lhs, rhs, amat, con = refs[parts_count:]
    lane = 2 * wide
    copy_operator(amat, parts)
    fill_left(lhs, (left_a, left_b), wide)
    for pair in range(phys // 2):
        cols = slice(pair * lane, (pair + 1) * lane)
        tiles = two_in_lanes(vec_a[0, :, cols].astype(F32), vec_b[0, :, cols].astype(F32))
        for half, tile in enumerate(tiles):
            s = 2 * pair + half
            both[:, s * lane : (s + 1) * lane] = tile.astype(BF)
            put_source(rhs, s, tile)
    contract_left(lhs, rhs, con)
    mix(amat, con, mixed, phys, lane)


def split_rows(place, image, outs):
    terms = len(outs)
    rows = outs[0].shape[0]
    for k, out in enumerate(outs):
        quarter = lax.rem(place[0] + k, terms)
        out[...] = image[pl.ds(pl.multiple_of(quarter * rows, rows), rows), :]


def right_kernel(terms, kinds, wide, phys, place, mixed, both, *refs):
    rights = refs[: len(kinds)]
    image, stats = refs[len(kinds)], refs[len(kinds) + 1]
    outs = refs[len(kinds) + 2 : len(kinds) + 2 + terms]
    rmat, acc = refs[len(kinds) + 2 + terms :]
    lane = 2 * wide
    fill_right(
        rmat,
        [
            lambda pair, ref=ref, at=at: ref[at, :, pair * lane : (pair + 1) * lane]
            for ref, at in zip(rights, kinds)
        ],
        lane,
    )
    contract_right(mixed, rmat, acc)
    norm = jnp.zeros((wide, lane), F32)
    corr = jnp.zeros((wide, lane), F32)
    for y in range(phys):
        cols = slice(y * lane, (y + 1) * lane)
        tile = acc[pl.ds(y, wide, stride=phys), :].astype(BF)
        image[:, cols] = tile
        value = tile.astype(F32)
        vec = both[:, cols].astype(F32)
        norm += vec * vec
        corr += vec * value
    norm = jnp.sum(norm, keepdims=True)
    corr = jnp.sum(corr, keepdims=True)
    ratio = jnp.where(norm > 0, corr / jnp.where(norm > 0, norm, 1.0), 0.0)
    square = jnp.zeros((wide, lane), F32)
    cross = jnp.zeros((wide, lane), F32)
    for y in range(phys):
        cols = slice(y * lane, (y + 1) * lane)
        vec = both[:, cols].astype(F32)
        rest = image[:, cols].astype(F32) - ratio * vec
        square += rest * rest
        cross += rest * vec
    square = jnp.sum(square, keepdims=True)
    cross = jnp.sum(cross, keepdims=True)
    at = lax.broadcasted_iota(jnp.int32, stats.shape, 1)
    row = jnp.zeros(stats.shape, F32)
    for i, value in enumerate((norm, corr, ratio, square, cross)):
        row = jnp.where(at == i, value, row)
    stats[...] = row
    split_rows(place, image, outs)


def second_kernel(terms, kinds, wide, phys, place, scal, left_a, left_b, both, image, *refs):
    parts, refs = refs[:terms], refs[terms:]
    rights, refs = refs[: len(kinds)], refs[len(kinds) :]
    outs, refs = refs[:terms], refs[terms:]
    lhs, rhs, amat, con, mixed, rmat, acc, result = refs
    lane = 2 * wide
    copy_operator(amat, parts)
    fill_left(lhs, (left_a, left_b), wide)
    ratio, scale = scal[0], scal[1]
    for s in range(phys):
        cols = slice(s * lane, (s + 1) * lane)
        rest = image[:, cols].astype(F32) - ratio * both[:, cols].astype(F32)
        put_source(rhs, s, (rest * scale).astype(BF).astype(F32))
    contract_left(lhs, rhs, con)
    mix(amat, con, mixed, phys, lane)
    fill_right(
        rmat,
        [
            lambda pair, ref=ref, at=at: ref[at, :, pair * lane : (pair + 1) * lane]
            for ref, at in zip(rights, kinds)
        ],
        lane,
    )
    contract_right(mixed, rmat, acc)
    for y in range(phys):
        result[:, y * lane : (y + 1) * lane] = acc[pl.ds(y, wide, stride=phys), :].astype(BF)
    split_rows(place, result, outs)


def select_kernel(terms, wide, names, blocks, *refs):
    envs, outs = refs[: len(blocks)], refs[len(blocks) : -2]
    spread, rows_out = refs[-2:]
    env_width = envs[0].shape[1]
    lane = 2 * wide
    half = wide // 2
    groups = outs[0].shape[2] // wide
    local = groups // terms
    turn = names[groups]
    for env, (out, at) in zip(envs, blocks):
        for z in range(half):
            spread[pl.ds(z, env_width, stride=half), :] = env[
                0, :, z * lane : (z + 1) * lane
            ].astype(F32)

        def rows_of(g):
            k = lax.rem(turn + g // local, terms)
            name = names[k * local + g % local]
            return spread[pl.ds(pl.multiple_of(name * half, half), half), :]

        for pair in range(groups // 2):
            even, odd = two_in_lanes(rows_of(2 * pair), rows_of(2 * pair + 1))
            rows_out[pl.ds(0, half, stride=2), :] = even
            rows_out[pl.ds(1, half, stride=2), :] = odd
            outs[out][at, :, pair * lane : (pair + 1) * lane] = rows_out[...].astype(BF)


def place_kernel(terms, pairs, wide, phys, follows, table, *refs):
    if follows:
        scal, rows, refs = refs[0], refs[1], refs[2:]
    pieces, refs = refs[: terms * pairs], refs[terms * pairs :]
    out = refs[0]
    lane = 2 * wide
    slots = out.shape[0] // terms
    me = table[out.shape[0]]
    for k in range(terms):
        source = lax.rem(me + terms - k, terms)
        for pi in range(pairs):
            piece = pieces[k * pairs + pi]
            first = table[source * slots + 2 * pi]
            second = table[source * slots + 2 * pi + 1]
            for pair in range(phys // 2):
                cols = slice(pair * lane, (pair + 1) * lane)
                a, b = two_in_lanes(
                    piece[:, 2 * pair * lane : (2 * pair + 1) * lane].astype(F32),
                    piece[:, (2 * pair + 1) * lane : (2 * pair + 2) * lane].astype(F32),
                )
                out[first, :, cols] = a.astype(BF)
                out[second, :, cols] = b.astype(BF)
                if follows:
                    ratio, scale = scal[0], scal[1]
                    for where, value in ((first, a), (second, b)):
                        rest = value - ratio * rows[where, :, cols].astype(F32)
                        refs[1][where, :, cols] = (rest * scale).astype(BF)


def whole(shape):
    return pl.BlockSpec(shape, lambda *_: (0,) * len(shape))


def call(kernel, prefetch, in_specs, out_shapes, scratch, flops, moved):
    return pl.pallas_call(
        kernel,
        out_shape=out_shapes,
        grid_spec=pltpu.PrefetchScalarGridSpec(
            num_scalar_prefetch=prefetch,
            grid=(1,),
            in_specs=in_specs,
            out_specs=[whole(s.shape) for s in out_shapes],
            scratch_shapes=scratch,
        ),
        compiler_params=pltpu.CompilerParams(vmem_limit_bytes=VMEM_LIMIT),
        cost_estimate=pl.CostEstimate(flops=flops, bytes_accessed=moved, transcendentals=0),
    )


def body(vector, right_sector, left_env, right_env, term_ops, term_left, group_right):
    terms = lax.axis_size("term")
    secs = lax.axis_size("sec")
    per_device, per_left, wide, row_width = vector.shape
    phys = row_width // wide
    lane = 2 * wide
    blocks = per_device * per_left
    slots = blocks // terms
    pairs = slots // 2
    span = secs // terms
    each = blocks // secs
    env_width = left_env.shape[1]
    depth = -(-env_width // 16) * 16
    local = group_right.shape[0]
    groups = local * terms
    slab = wide // terms
    d = lax.axis_index("sec")
    me = lax.axis_index("term")
    both_axes = ("sec", "term")
    vec = vector.reshape(blocks, wide, row_width)

    flat = right_sector.reshape(blocks)
    dest = flat // per_device
    before = jnp.arange(blocks)[None, :] < jnp.arange(blocks)[:, None]
    rank = jnp.sum((dest[None, :] == dest[:, None]) & before, axis=1)
    turn = lax.rem(dest - d + secs, span)
    place = (dest // span) * slots + turn * each + rank
    hit = place[None, :] == jnp.arange(blocks)[:, None]
    order = jnp.sum(jnp.where(hit, jnp.arange(blocks)[None, :], 0), axis=1)
    by_place = jnp.sum(jnp.where(hit, (flat % per_device)[None, :], 0), axis=1)
    own = lax.dynamic_slice(order, (me * slots,), (slots,)).astype(jnp.int32)
    wanted = lax.dynamic_slice(by_place, (me * slots,), (slots,)).astype(jnp.int32)
    table = jnp.concatenate([order.astype(jnp.int32), me.reshape(1)])

    def partner(a, device, term):
        return (term * span + (a + device) % span) * terms + device // span

    asks = [
        [(dd * terms + t, partner(a, dd, t)) for dd in range(secs) for t in range(terms)]
        for a in range(span)
    ]
    asked = [
        lax.ppermute(wanted[a * each : (a + 1) * each], both_axes, asks[a]) for a in range(span)
    ]

    onehot = (term_left[:, :, None] == jnp.arange(depth)).astype(BF)
    operator = jnp.einsum(
        "gtys,gtw->gysw", term_ops, onehot, preferred_element_type=F32
    ).reshape(local * phys, phys * depth)
    names = jnp.pad(
        group_right.astype(F32)[None, :], ((0, 15), (0, phys * depth - local))
    )
    packed = jnp.concatenate([operator, names], axis=0).astype(BF)

    def shift(value, k):
        return lax.ppermute(value, "term", [(t, (t + k) % terms) for t in range(terms)])

    parts = [packed] + [shift(packed, k) for k in range(1, terms)]
    known = jnp.concatenate([p[local * phys, :local] for p in parts]).astype(jnp.int32)
    receiver = d // span
    names = jnp.concatenate([known, lax.rem(me - receiver + terms, terms).reshape(1)])
    asked = jnp.concatenate(asked)

    env_block = (1, env_width, wide * wide)
    right_shape = jax.ShapeDtypeStruct((each, wide, groups * wide), BF)
    chosen = call(
        functools.partial(
            lambda fn, names, asked, *refs: fn(names, *refs),
            lambda names, *refs: select_kernel(
                terms, wide, names, [(i // each, i % each) for i in range(slots)], *refs
            ),
        ),
        2,
        [
            pl.BlockSpec(env_block, lambda _, n, q, i=i: (q[i], 0, 0)) for i in range(slots)
        ],
        [right_shape] * span,
        [
            pltpu.VMEM((env_width * (wide // 2), lane), F32),
            pltpu.VMEM((wide, lane), F32),
        ],
        0,
        slots * env_width * wide * wide * 2,
    )(names, asked, *([right_env] * slots))
    rights = [
        lax.ppermute(chosen[a], both_axes, [(t, s) for s, t in asks[a]]) for a in range(span)
    ]

    rows = wide * depth
    left_flops = 2 * rows * 4 * wide * phys * lane
    mix_flops = 2 * groups * phys * phys * depth * wide * lane
    right_flops = 2 * wide * phys * groups * lane * lane
    part_shape = packed.shape
    mixed_shape = jax.ShapeDtypeStruct((wide * phys, groups * lane), BF)
    full_shape = jax.ShapeDtypeStruct((wide, phys * lane), BF)
    piece_shape = jax.ShapeDtypeStruct((slab, phys * lane), BF)
    con_scratch = [
        pltpu.VMEM((rows, 4 * wide), BF),
        pltpu.VMEM((4 * wide, phys * lane), BF),
        pltpu.VMEM((groups * phys, phys * depth), BF),
        pltpu.VMEM((rows, phys * lane), BF),
    ]
    right_scratch = [
        pltpu.VMEM((lane, groups * lane), BF),
        pltpu.VMEM((wide * phys, lane), F32),
    ]

    def left_specs(pi):
        return [
            pl.BlockSpec(
                env_block, lambda _, o, *s, i=i: (lax.div(o[i], per_left), 0, 0)
            )
            for i in (2 * pi, 2 * pi + 1)
        ]

    mixes = []
    for pi in range(pairs):
        mixes.append(
            call(
                functools.partial(left_kernel, terms, wide, phys),
                1,
                left_specs(pi)
                + [
                    pl.BlockSpec((1, wide, row_width), lambda _, o, i=i: (o[i], 0, 0))
                    for i in (2 * pi, 2 * pi + 1)
                ]
                + [whole(part_shape)] * terms,
                [mixed_shape, full_shape],
                con_scratch,
                left_flops + mix_flops,
                wide * phys * groups * lane * 2,
            )(own, left_env, left_env, vec, vec, *parts)
        )

    where = me.reshape(1).astype(jnp.int32)
    images, stats, pieces = [], [], []
    for pi in range(pairs):
        kinds = [(2 * pi) % each, (2 * pi + 1) % each]
        using = [rights[(2 * pi) // each], rights[(2 * pi + 1) // each]]
        image, stat, *outs = call(
            functools.partial(right_kernel, terms, kinds, wide, phys),
            1,
            [whole(mixed_shape.shape), whole(full_shape.shape)] + [whole(right_shape.shape)] * 2,
            [full_shape, jax.ShapeDtypeStruct((1, lane), F32)] + [piece_shape] * terms,
            right_scratch,
            right_flops,
            wide * phys * groups * lane * 2,
        )(where, *mixes[pi], *using)
        images.append(image)
        stats.append(stat)
        pieces.append(outs)

    def spread(pieces):
        return [
            pieces[pi][k] if k == 0 else shift(pieces[pi][k], k)
            for k in range(terms)
            for pi in range(pairs)
        ]

    first_pieces = spread(pieces)

    line = jnp.concatenate(stats, axis=0).reshape(1, pairs * lane)
    everyone = lax.all_to_all(
        jnp.broadcast_to(line, (secs * terms, pairs * lane)), both_axes, 0, 0, tiled=True
    ).reshape(secs * terms * pairs, lane)
    sums = [everyone[:, i] for i in range(5)]
    norm_sq = jnp.sum(sums[0])
    ratio = jnp.sum(sums[1]) / norm_sq
    off = sums[2] - ratio
    residual_sq = jnp.sum(sums[3] + 2 * off * sums[4] + off * off * sums[0])
    scal = jnp.stack([ratio, jnp.sqrt(norm_sq / (residual_sq + 1e-06))])

    smem = pl.BlockSpec(memory_space=pltpu.SMEM)
    pieces = []
    for pi in range(pairs):
        kinds = [(2 * pi) % each, (2 * pi + 1) % each]
        using = [rights[(2 * pi) // each], rights[(2 * pi + 1) // each]]
        pieces.append(
            call(
                functools.partial(
                    lambda fn, own, place, *refs: fn(place, *refs),
                    functools.partial(second_kernel, terms, kinds, wide, phys),
                ),
                2,
                [smem]
                + left_specs(pi)
                + [whole(full_shape.shape)] * 2
                + [whole(part_shape)] * terms
                + [whole(right_shape.shape)] * 2,
                [piece_shape] * terms,
                con_scratch
                + [pltpu.VMEM(mixed_shape.shape, BF)]
                + right_scratch
                + [pltpu.VMEM(full_shape.shape, BF)],
                left_flops + mix_flops + right_flops,
                4 * wide * phys * lane * 2,
            )(own, where, scal, left_env, left_env, mixes[pi][1], images[pi], *parts, *using)
        )
    second_pieces = spread(pieces)

    out_shape = jax.ShapeDtypeStruct((blocks, slab, row_width), BF)
    first_image, next_rows = call(
        functools.partial(place_kernel, terms, pairs, wide, phys, True),
        1,
        [smem, pl.BlockSpec((blocks, slab, row_width), lambda _, t: (0, t[blocks], 0))]
        + [whole(piece_shape.shape)] * (terms * pairs),
        [out_shape] * 2,
        [],
        0,
        blocks * slab * row_width * 8,
    )(table, scal, vec, *first_pieces)
    (second_image,) = call(
        functools.partial(place_kernel, terms, pairs, wide, phys, False),
        1,
        [whole(piece_shape.shape)] * (terms * pairs),
        [out_shape],
        [],
        0,
        blocks * slab * row_width * 4,
    )(table, *second_pieces)
    shape = (per_device, per_left, slab, row_width)
    return (first_image.reshape(shape), next_rows.reshape(shape), second_image.reshape(shape))


def solution(mesh):
    in_specs = (
        P("sec", None, None, None),
        P("sec", None),
        P("sec", None, None),
        P("sec", None, None),
        P("term", None, None, None),
        P("term", None),
        P("term"),
    )
    out_specs = (
        P("sec", None, "term", None),
        P("sec", None, "term", None),
        P("sec", None, "term", None),
    )
    return jax.shard_map(body, mesh=mesh, in_specs=in_specs, out_specs=out_specs, check_vma=False)
```

time: 1160 us -> 109 us (0.09)
  matrix products: 325 us -> 0.98 us
  waiting for transfers between devices: 310 us -> 3.82 us
  blocking collectives: 244 us -> 0 us
  local copies, waits for them, and re-layouts: 215 us -> 18.6 us
  Pallas kernels: 0 us -> 47 us
  loops' own time: 13.8 us -> 0 us
  between operations: 16.9 us -> 3.54 us
  starting transfers between devices: 18.9 us -> 31 us
    dot_general x14 -> x1, matrix products: 325 us -> 0.98 us  [body(): jnp.einsum('gtys,gtw->gysw', term_ops, onehot, preferred_element_type=F32)]
    all_to_all x2 -> x0, blocking collectives: 164 us -> none  [the longest x1 144 us: apply_operator(): lax.all_to_all(mixed_terms, 'sec', split_axis=0, concat_axis=0, tiled=True)]
    all_to_all x3 -> x1, waiting for transfers between devices: 147 us -> 3.55 us  [body(): lax.all_to_all(jnp.broadcast_to(line, (secs * terms, pairs * lane)), both...]
    reduce_scatter x2 -> x0, waiting for transfers between devices: 141 us -> none  [finish_rows(): lax.psum_scatter(partial_value, 'term', scatter_dimension=1, tiled=True)]
    psum x2 -> x0, blocking collectives: 79.8 us -> none  [the longest x1 41.1 us: body(): lax.psum(jnp.sum(residual_rows * residual_rows), ('sec', 'term'))]
    gather x18 -> x0, local copies, waits for them, and re-layouts: 71.1 us -> none  [the longest x4 48 us: apply_operator(): mixed_terms = left_section(source)[ordering]]
    pallas_call x0 -> x9, Pallas kernels: none -> 47 us  [the longest x2 18.6 us: body(): call(functools.partial(lambda fn, own, place, *refs: fn(place, *refs), fu...]
    unnamed x33 -> x59, local copies, waits for them, and re-layouts: 60.8 us -> 17.5 us
  transfers between devices with their start and end apart: 6 -> 20, of which waited for: 5 -> 2; matrix products, arithmetic and copies ran while one was open for 21% -> 10% of each run, Pallas kernels for 0% -> 38%
where the time goes in v1:
time: 109 us; the launch traced here: 108 us
  Pallas kernels  47 us (43%)
  starting transfers between devices  31 us (28%)
  local copies, waits for them, and re-layouts  18.6 us (17%)
  waiting for transfers between devices  3.82 us (4%)
  between operations  3.54 us (3%)
  other arithmetic  3.41 us (3%)
    pallas_call x2, Pallas kernels, body(): call(functools.partial(lambda fn, own, place, *refs: fn(place, *refs), fu...  18.6 us
    pallas_call x2, Pallas kernels, body(): call(functools.partial(left_kernel, terms, wide, phys), 1, left_specs(pi)...  18.6 us
    unnamed x59, local copies, waits for them, and re-layouts  17.5 us
    all_to_all x1, starting transfers between devices, body(): lax.all_to_all(jnp.broadcast_to(line, (secs * terms, pairs * lane)), both...  15.1 us
    ppermute x15, starting transfers between devices, shift(): lax.ppermute(value, 'term', [(t, (t + k) % terms) for t in range(terms)])  12.2 us
    all_to_all x1, waiting for transfers between devices, body(): lax.all_to_all(jnp.broadcast_to(line, (secs * terms, pairs * lane)), both...  3.55 us
    pallas_call x2, Pallas kernels, body(): call(functools.partial(right_kernel, terms, kinds, wide, phys), 1, [whole...  3.21 us
    pallas_call x1, Pallas kernels, body(): call(functools.partial(place_kernel, terms, pairs, wide, phys, True), 1,...  2.71 us
  transfers between devices with their start and end apart: 20, of which 2 were waited for; matrix products, arithmetic and copies ran while one was open for 10% of the time, Pallas kernels for 38%

profile of v1, /device:TPU:0, one launch (start us, length us, event | category | flops | bytes accessed | tf_op | source)
XLA Modules:
  0.0 108.4 jit_solution(9155476456398647921)
XLA Ops:
  0.6 0.7 convert_convert_fusion
  1.5 1.0 fusion
  2.8 2.4 %collective-permute-start.2 = (bf16[64,512]{1,0:T(8,128)(2,1)S(1)}, bf16[64,512]{1,0:T(8,128)(2,1)S(1)}, u32[]{:S(2)}, u32[]{:S(2)}) collective-permute-start(bf16[64,512]{1,0:T(8,128)(2,1)S(1)} %fusion.3.refs_0_.refs_5_), channel_id=1, source_target_pairs={{0,3},{1,0},{2,1},{3,2},{4,7},{5,4},{6,5},{7,6},{8,11},{9,8},{10,9... | collective-permute-start | bytes 196616 | tf_op jit(solution)/shard_map/ppermute | solution.py:357
  5.2 0.6 collective-permute-start.1
  6.0 0.8 copy.86
  7.3 0.7 collective-permute-start.3
  8.0 1.6 %collective-permute-start.4 = (s32[2]{0:T(128)S(1)}, s32[2]{0:T(128)S(1)}, u32[]{:S(2)}, u32[]{:S(2)}) collective-permute-start(s32[2]{0:T(128)S(1)} %get-tuple-element.70), channel_id=1, source_target_pairs={{0,4},{1,12},{2,20},{3,28},{4,0},{5,8},{6,16},{7,24},{8,5},{9,13},... | collective-permute-start | bytes 32 | tf_op jit(solution)/shard_map/ppermute | solution.py:344
  9.6 2.4 %copy.88.left_a.left_b.refs_1_.refs_2_ = bf16[8,26,4096]{2,1,0:T(8,128)(2,1)S(1)} copy(bf16[8,26,4096]{2,0,1:T(8,128)(2,1)} %param.9) | data formatting | bytes 3407872 | tf_op args[2]
  12.1 1.0 copy.90.refs_0_.refs_1_.refs_2_.refs_3_
  13.4 2.4 %shard_map.95 = (bf16[2,64,768]{2,1,0:T(8,128)(2,1)S(1)}, bf16[2,64,768]{2,1,0:T(8,128)(2,1)S(1)}) custom-call(s32[13]{0:T(128)S(1)} %pad_add_fusion.1.names, s32[4]{0:T(128)S(1)} %pad_add_fusion.2.asked, bf16[8,26,4096]{2,1,0:T(8,128)(2,1)S(1)} %copy.90.refs_0_.refs_1_.refs_2_.refs_3_, bf16[8,26,4096]{2,1,0:T(8,128)(2,1)S(1)} %copy.90.refs_0_.refs_1_.refs_2_.refs_3_, ...), custom_call_target="tpu_custom_call" | custom-call | bytes 851968 | tf_op jit(solution)/shard_map/pallas_call | solution.py:367
  15.7 0.9 collective-permute-start.5
  16.6 0.6 collective-permute-start.6
  17.2 9.3 %shard_map.97 = (bf16[1024,1536]{1,0:T(8,128)(2,1)}, bf16[64,2048]{1,0:T(8,128)(2,1)S(1)}) custom-call(s32[4]{0:T(128)S(1)} %dynamic_slice.6._.own, bf16[8,26,4096]{2,1,0:T(8,128)(2,1)S(1)} %copy.88.left_a.left_b.refs_1_.refs_2_, bf16[8,26,4096]{2,1,0:T(8,128)(2,1)S(1)} %copy.88.left_a.left_b.refs_1_.refs_2_, bf16[16,64,1024]{2,1,0:T(8,128)(2,1)S(1)} %bitcast.28, ...), custom_call_target="tpu_custom_call" | custom-call | flops 3758096384 | bytes 3145728 | tf_op jit(solution)/shard_map/pallas_call | solution.py:420
  26.5 9.3 %shard_map.94 = (bf16[1024,1536]{1,0:T(8,128)(2,1)}, bf16[64,2048]{1,0:T(8,128)(2,1)S(1)}) custom-call(s32[4]{0:T(128)S(1)} %dynamic_slice.6._.own, bf16[8,26,4096]{2,1,0:T(8,128)(2,1)S(1)} %copy.88.left_a.left_b.refs_1_.refs_2_, bf16[8,26,4096]{2,1,0:T(8,128)(2,1)S(1)} %copy.88.left_a.left_b.refs_1_.refs_2_, bf16[16,64,1024]{2,1,0:T(8,128)(2,1)S(1)} %bitcast.30, ...), custom_call_target="tpu_custom_call" | custom-call | flops 3758096384 | bytes 3145728 | tf_op jit(solution)/shard_map/pallas_call | solution.py:420
  35.8 1.6 %shard_map.98 = (bf16[64,2048]{1,0:T(8,128)(2,1)S(1)}, f32[1,128]{1,0:T(1,128)S(1)}, bf16[16,2048]{1,0:T(8,128)(2,1)S(1)}, bf16[16,2048]{1,0:T(8,128)(2,1)S(1)},...) custom-call(s32[1]{0:T(128)} %bitcast.place, bf16[1024,1536]{1,0:T(8,128)(2,1)S(1)} %copy-done.2, ...), custom_call_target="tpu_custom_call" | custom-call | flops 402653184 | bytes 3145728 | tf_op jit(solution)/shard_map/pallas_call | solution.py:441
  37.4 0.6 copy-done.21
  38.1 0.6 copy-done.23
  38.7 0.6 copy-done.24
  39.3 1.6 %shard_map.96 = (bf16[64,2048]{1,0:T(8,128)(2,1)S(1)}, f32[1,128]{1,0:T(1,128)S(1)}, bf16[16,2048]{1,0:T(8,128)(2,1)S(1)}, bf16[16,2048]{1,0:T(8,128)(2,1)S(1)},...) custom-call(s32[1]{0:T(128)} %bitcast.place, bf16[1024,1536]{1,0:T(8,128)(2,1)S(1)} %copy-done.1, ...), custom_call_target="tpu_custom_call" | custom-call | flops 402653184 | bytes 3145728 | tf_op jit(solution)/shard_map/pallas_call | solution.py:441
  40.9 0.7 copy-done.8
  41.6 0.6 copy-done.18
  42.3 0.6 copy-done.22
  42.9 0.6 broadcast_in_dim.41
  43.5 15.1 %all-to-all-start = ((f32[32,1,256]{2,1,0:T(1,128)}), f32[32,1,256]{2,1,0:T(1,128)S(1)}, u32[]{:S(2)}, u32[]{:S(2)}) async-start(f32[32,1,256]{2,1,0:T(1,128)} %broadcast_in_dim.41), calls=%async_computation | async-start | bytes 65536 | tf_op jit(solution)/shard_map/all_to_all | solution.py:464
  59.0 1.7 %collective-permute-start.10 = (bf16[16,2048]{1,0:T(8,128)(2,1)}, bf16[16,2048]{1,0:T(8,128)(2,1)S(1)}, u32[]{:S(2)}, u32[]{:S(2)}) collective-permute-start(bf16[16,2048]{1,0:T(8,128)(2,1)} %copy-done.23), channel_id=1, source_target_pairs={{0,2},{1,3},{2,0},{3,1},{4,6},{5,7},{6,4},{7,5},{8,10},{9,11},{10,... | collective-permute-start | bytes 196616 | tf_op jit(solution)/shard_map/ppermute | solution.py:357
  60.7 1.3 %collective-permute-start.12 = (bf16[16,2048]{1,0:T(8,128)(2,1)}, bf16[16,2048]{1,0:T(8,128)(2,1)S(1)}, u32[]{:S(2)}, u32[]{:S(2)}) collective-permute-start(bf16[16,2048]{1,0:T(8,128)(2,1)} %copy-done.21), channel_id=1, source_target_pairs={{0,3},{1,0},{2,1},{3,2},{4,7},{5,4},{6,5},{7,6},{8,11},{9,8},{10,9... | collective-permute-start | bytes 196616 | tf_op jit(solution)/shard_map/ppermute | solution.py:357
  62.0 0.4 collective-permute-start.9
  62.4 3.5 %all-to-all-done = f32[32,1,256]{2,1,0:T(1,128)S(1)} async-done(((f32[32,1,256]{2,1,0:T(1,128)}), f32[32,1,256]{2,1,0:T(1,128)S(1)}, u32[]{:S(2)}, u32[]{:S(2)}) %all-to-all-start) | async-done | bytes 32800 | tf_op jit(solution)/shard_map/all_to_all | solution.py:464
  65.9 1.4 %fusion.13 = (f32[64,1]{1,0:T(8,128)}, f32[64,1]{1,0:T(8,128)}, f32[64,1]{1,0:T(8,128)}, f32[64,1]{1,0:T(8,128)}, f32[]{:T(128)}, /*index=5*/f32[]{:T(128)}) fusion(f32[64,128]{1,0:T(8,128)S(1)} %bitcast.33), kind=kLoop, calls=%fused_computation.44 | loop fusion | flops 126 | bytes 2312 | tf_op jit(solution)/shard_map/slice | solution.py:467
  67.3 0.8 copy.109
  68.2 0.8 copy.108
  69.0 0.8 copy.107
  69.8 0.8 copy.110
  72.0 0.6 add_reduce_fusion
  73.9 1.6 %copy-done.5 = bf16[8,26,4096]{2,1,0:T(8,128)(2,1)S(1)} copy-done((bf16[8,26,4096]{2,1,0:T(8,128)(2,1)S(1)}, bf16[8,26,4096]{2,1,0:T(8,128)(2,1)}, u32[]{:S(2)}) %copy-start.5) | copy-done | bytes 1703960
  75.5 0.8 copy-done.7
  76.4 0.9 copy-done.11
  77.3 0.8 copy-done.13
  78.2 0.8 copy-done.15
  79.0 0.8 copy-done.17
  79.8 9.3 %shard_map.101 = (bf16[16,2048]{1,0:T(8,128)(2,1)S(1)}, bf16[16,2048]{1,0:T(8,128)(2,1)S(1)}, bf16[16,2048]{1,0:T(8,128)(2,1)S(1)}, bf16[16,2048]{1,0:T(8,128)(2,1)S(1)}) custom-call(s32[4]{0:T(128)S(1)} %dynamic_slice.6._.own, s32[1]{0:T(128)} %bitcast.place, f32[2]{0:T(128)S(1)} %pad_maximum_fusion.refs_0_, bf16[8,26,4096]{2,1,0:T(8,128)(2,1)S(1)} %copy-done.5, ...), custom_call_target="tpu_custom_call" | custom-call | flops 4160749568 | bytes 1048576 | tf_op jit(solution)/shard_map/pallas_call | solution.py:480
  89.7 9.3 %shard_map.100 = (bf16[16,2048]{1,0:T(8,128)(2,1)S(1)}, bf16[16,2048]{1,0:T(8,128)(2,1)S(1)}, bf16[16,2048]{1,0:T(8,128)(2,1)S(1)}, bf16[16,2048]{1,0:T(8,128)(2,1)S(1)}) custom-call(s32[4]{0:T(128)S(1)} %dynamic_slice.6._.own, s32[1]{0:T(128)} %bitcast.place, f32[2]{0:T(128)S(1)} %pad_maximum_fusion.refs_0_, bf16[8,26,4096]{2,1,0:T(8,128)(2,1)S(1)} %copy-done.5, ...), custom_call_target="tpu_custom_call" | custom-call | flops 4160749568 | bytes 1048576 | tf_op jit(solution)/shard_map/pallas_call | solution.py:480
  99.0 1.3 %collective-permute-start.16 = (bf16[16,2048]{1,0:T(8,128)(2,1)S(1)}, bf16[16,2048]{1,0:T(8,128)(2,1)S(1)}, u32[]{:S(2)}, u32[]{:S(2)}) collective-permute-start(bf16[16,2048]{1,0:T(8,128)(2,1)S(1)} %get-tuple-element.56), channel_id=1, source_target_pairs={{0,2},{1,3},{2,0},{3,1},{4,6},{5,7},{6,4},{7,5},{8,10},{9,11},{10,... | collective-permute-start | bytes 196616 | tf_op jit(solution)/shard_map/ppermute | solution.py:357
  100.4 1.5 %collective-permute-start.18 = (bf16[16,2048]{1,0:T(8,128)(2,1)S(1)}, bf16[16,2048]{1,0:T(8,128)(2,1)S(1)}, u32[]{:S(2)}, u32[]{:S(2)}) collective-permute-start(bf16[16,2048]{1,0:T(8,128)(2,1)S(1)} %get-tuple-element.58), channel_id=1, source_target_pairs={{0,3},{1,0},{2,1},{3,2},{4,7},{5,4},{6,5},{7,6},{8,11},{9,8},{10,9... | collective-permute-start | bytes 196616 | tf_op jit(solution)/shard_map/ppermute | solution.py:357
  101.8 0.6 collective-permute-start.15
  102.4 1.4 %collective-permute-start.17 = (bf16[16,2048]{1,0:T(8,128)(2,1)S(1)}, bf16[16,2048]{1,0:T(8,128)(2,1)S(1)}, u32[]{:S(2)}, u32[]{:S(2)}) collective-permute-start(bf16[16,2048]{1,0:T(8,128)(2,1)S(1)} %get-tuple-element.57), channel_id=1, source_target_pairs={{0,3},{1,0},{2,1},{3,2},{4,7},{5,4},{6,5},{7,6},{8,11},{9,8},{10,9... | collective-permute-start | bytes 196616 | tf_op jit(solution)/shard_map/ppermute | solution.py:357
  103.9 2.7 %shard_map.99 = (bf16[16,16,1024]{2,1,0:T(8,128)(2,1)}, bf16[16,16,1024]{2,1,0:T(8,128)(2,1)}) custom-call(s32[17]{0:T(128)S(1)} %pad_add_fusion.table, f32[2]{0:T(128)S(1)} %pad_maximum_fusion.refs_0_, bf16[16,64,1024]{2,1,0:T(8,128)(2,1)S(1)} %bitcast.32, bf16[16,2048]{1,0:T(8,128)(2,1)S(1)} %get-tuple-element.39.refs_2_, ...), custom_call_target="tpu_custom_call" | custom-call | bytes 2097152 | tf_op jit(solution)/shard_map/pallas_call | solution.py:503
  106.8 1.6 %shard_map.102 = bf16[16,16,1024]{2,1,0:T(8,128)(2,1)} custom-call(s32[17]{0:T(128)S(1)} %pad_add_fusion.table, bf16[16,2048]{1,0:T(8,128)(2,1)S(1)} %get-tuple-element.50.refs_0_, bf16[16,2048]{1,0:T(8,128)(2,1)S(1)} %get-tuple-element.52.refs_1_, bf16[16,2048]{1,0:T(8,128)(2,1)S(1)} %collective-permute-done.13.refs_2_, ...), custom_call_target="tpu_custom_call" | custom-call | bytes 1048576 | tf_op jit(solution)/shard_map/pallas_call | solution.py:513
  (84 shorter events, 2.8 us)
Async XLA Ops:
  0.6 0.9 copy-start
  2.5 9.5 %copy-start.25 = (bf16[8,26,4096]{2,0,1:T(8,128)(2,1)S(1)}, bf16[8,26,4096]{2,0,1:T(8,128)(2,1)}, u32[]{:S(2)}) copy-start(bf16[8,26,4096]{2,0,1:T(8,128)(2,1)} %param.10) | copy-start | bytes 5111812
  2.7 23.7 %copy-start.6 = (bf16[64,512]{1,0:T(8,128)(2,1)}, bf16[64,512]{1,0:T(8,128)(2,1)S(1)}, u32[]{:S(2)}) copy-start(bf16[64,512]{1,0:T(8,128)(2,1)S(1)} %fusion.3.refs_0_.refs_5_) | copy-start | bytes 196612
  2.8 10.4 %collective-permute-start.2 = (bf16[64,512]{1,0:T(8,128)(2,1)S(1)}, bf16[64,512]{1,0:T(8,128)(2,1)S(1)}, u32[]{:S(2)}, u32[]{:S(2)}) collective-permute-start(bf16[64,512]{1,0:T(8,128)(2,1)S(1)} %fusion.3.refs_0_.refs_5_), channel_id=1, source_target_pairs={{0,3},{1,0},{2,1},{3,2},{4,7},{5,4},{6,5},{7,6},{8,11},{9,8},{10,9... | collective-permute-start | bytes 196616 | tf_op jit(solution)/shard_map/ppermute | solution.py:357
  5.2 8.0 %collective-permute-start.1 = (bf16[64,512]{1,0:T(8,128)(2,1)S(1)}, bf16[64,512]{1,0:T(8,128)(2,1)S(1)}, u32[]{:S(2)}, u32[]{:S(2)}) collective-permute-start(bf16[64,512]{1,0:T(8,128)(2,1)S(1)} %fusion.3.refs_0_.refs_5_), channel_id=1, source_target_pairs={{0,2},{1,3},{2,0},{3,1},{4,6},{5,7},{6,4},{7,5},{8,10},{9,11},{10,... | collective-permute-start | bytes 196616 | tf_op jit(solution)/shard_map/ppermute | solution.py:357
  5.8 7.4 %collective-permute-start = (bf16[64,512]{1,0:T(8,128)(2,1)S(1)}, bf16[64,512]{1,0:T(8,128)(2,1)S(1)}, u32[]{:S(2)}, u32[]{:S(2)}) collective-permute-start(bf16[64,512]{1,0:T(8,128)(2,1)S(1)} %fusion.3.refs_0_.refs_5_), channel_id=1, source_target_pairs={{0,1},{1,2},{2,3},{3,0},{4,5},{5,6},{6,7},{7,4},{8,9},{9,10},{10,1... | collective-permute-start | bytes 196616 | tf_op jit(solution)/shard_map/ppermute | solution.py:357
  7.3 5.7 %collective-permute-start.3 = (s32[2]{0:T(128)S(1)}, s32[2]{0:T(128)S(1)}, u32[]{:S(2)}, u32[]{:S(2)}) collective-permute-start(s32[2]{0:T(128)S(1)} %get-tuple-element.69), channel_id=1, source_target_pairs={{0,0},{1,8},{2,16},{3,24},{4,4},{5,12},{6,20},{7,28},{8,1},{9,9},{... | collective-permute-start | bytes 32 | tf_op jit(solution)/shard_map/ppermute | solution.py:344
  8.0 5.1 %collective-permute-start.4 = (s32[2]{0:T(128)S(1)}, s32[2]{0:T(128)S(1)}, u32[]{:S(2)}, u32[]{:S(2)}) collective-permute-start(s32[2]{0:T(128)S(1)} %get-tuple-element.70), channel_id=1, source_target_pairs={{0,4},{1,12},{2,20},{3,28},{4,0},{5,8},{6,16},{7,24},{8,5},{9,13},... | collective-permute-start | bytes 32 | tf_op jit(solution)/shard_map/ppermute | solution.py:344
  12.1 14.4 %copy-start.4 = (bf16[8,26,4096]{2,1,0:T(8,128)(2,1)}, bf16[8,26,4096]{2,1,0:T(8,128)(2,1)S(1)}, u32[]{:S(2)}) copy-start(bf16[8,26,4096]{2,1,0:T(8,128)(2,1)S(1)} %copy.88.left_a.left_b.refs_1_.refs_2_) | copy-start | bytes 5111812
  13.2 13.3 %copy-start.12 = (bf16[64,512]{1,0:T(8,128)(2,1)}, bf16[64,512]{1,0:T(8,128)(2,1)S(1)}, u32[]{:S(2)}) copy-start(bf16[64,512]{1,0:T(8,128)(2,1)S(1)} %collective-permute-done.2.refs_3_.refs_8_) | copy-start | bytes 196612
  13.2 13.3 %copy-start.14 = (bf16[64,512]{1,0:T(8,128)(2,1)}, bf16[64,512]{1,0:T(8,128)(2,1)S(1)}, u32[]{:S(2)}) copy-start(bf16[64,512]{1,0:T(8,128)(2,1)S(1)} %collective-permute-done.1.refs_2_.refs_7_) | copy-start | bytes 196612
  13.2 13.3 %copy-start.16 = (bf16[64,512]{1,0:T(8,128)(2,1)}, bf16[64,512]{1,0:T(8,128)(2,1)S(1)}, u32[]{:S(2)}) copy-start(bf16[64,512]{1,0:T(8,128)(2,1)S(1)} %collective-permute-done.refs_1_.refs_6_) | copy-start | bytes 196612
  13.4 3.8 %copy-start.3 = (bf16[8,2,64,1024]{3,2,1,0:T(8,128)(2,1)S(1)}, bf16[8,2,64,1024]{3,2,1,0:T(8,128)(2,1)}, u32[]{:S(2)}) copy-start(bf16[8,2,64,1024]{3,2,1,0:T(8,128)(2,1)} %param.7) | copy-start | bytes 6291460
  15.7 23.6 %collective-permute-start.5 = (bf16[2,64,768]{2,1,0:T(8,128)(2,1)S(1)}, bf16[2,64,768]{2,1,0:T(8,128)(2,1)S(1)}, u32[]{:S(2)}, u32[]{:S(2)}) collective-permute-start(bf16[2,64,768]{2,1,0:T(8,128)(2,1)S(1)} %get-tuple-element.33), channel_id=1, source_target_pairs={{0,0},{8,1},{16,2},{24,3},{4,4},{12,5},{20,6},{28,7},{1,8},{9,9},{... | collective-permute-start | bytes 589832 | tf_op jit(solution)/shard_map/ppermute | solution.py:387
  16.6 19.2 %collective-permute-start.6 = (bf16[2,64,768]{2,1,0:T(8,128)(2,1)S(1)}, bf16[2,64,768]{2,1,0:T(8,128)(2,1)S(1)}, u32[]{:S(2)}, u32[]{:S(2)}) collective-permute-start(bf16[2,64,768]{2,1,0:T(8,128)(2,1)S(1)} %get-tuple-element.37), channel_id=1, source_target_pairs={{4,0},{12,1},{20,2},{28,3},{0,4},{8,5},{16,6},{24,7},{5,8},{13,9},... | collective-permute-start | bytes 589832 | tf_op jit(solution)/shard_map/ppermute | solution.py:387
  26.5 9.3 %copy-start.2 = (bf16[1024,1536]{1,0:T(8,128)(2,1)S(1)}, bf16[1024,1536]{1,0:T(8,128)(2,1)}, u32[]{:S(2)}) copy-start(bf16[1024,1536]{1,0:T(8,128)(2,1)} %get-tuple-element.35.mixed) | copy-start | bytes 9437188
  35.8 3.5 %copy-start.1 = (bf16[1024,1536]{1,0:T(8,128)(2,1)S(1)}, bf16[1024,1536]{1,0:T(8,128)(2,1)}, u32[]{:S(2)}) copy-start(bf16[1024,1536]{1,0:T(8,128)(2,1)} %get-tuple-element.31.mixed) | copy-start | bytes 9437188
  37.4 0.6 copy-start.21
  38.0 0.6 copy-start.23
  38.7 0.6 copy-start.24
  39.3 3.6 %copy-start.10 = (bf16[64,2048]{1,0:T(8,128)(2,1)}, bf16[64,2048]{1,0:T(8,128)(2,1)S(1)}, u32[]{:S(2)}) copy-start(bf16[64,2048]{1,0:T(8,128)(2,1)S(1)} %get-tuple-element.51.refs_4_) | copy-start | bytes 786436
  40.9 0.7 copy-start.8
  41.6 0.6 copy-start.18
  42.2 0.6 copy-start.22
  42.9 16.1 %copy-start.20 = (bf16[16,2048]{1,0:T(8,128)(2,1)}, bf16[16,2048]{1,0:T(8,128)(2,1)S(1)}, u32[]{:S(2)}) copy-start(bf16[16,2048]{1,0:T(8,128)(2,1)S(1)} %get-tuple-element.43) | copy-start | bytes 196612
  43.5 22.4 %all-to-all-start = ((f32[32,1,256]{2,1,0:T(1,128)}), f32[32,1,256]{2,1,0:T(1,128)S(1)}, u32[]{:S(2)}, u32[]{:S(2)}) async-start(f32[32,1,256]{2,1,0:T(1,128)} %broadcast_in_dim.41), calls=%async_computation | async-start | bytes 65536 | tf_op jit(solution)/shard_map/all_to_all | solution.py:464
  58.7 30.5 %collective-permute-start.8 = (bf16[16,2048]{1,0:T(8,128)(2,1)}, bf16[16,2048]{1,0:T(8,128)(2,1)S(1)}, u32[]{:S(2)}, u32[]{:S(2)}) collective-permute-start(bf16[16,2048]{1,0:T(8,128)(2,1)} %copy-done.24), channel_id=1, source_target_pairs={{0,1},{1,2},{2,3},{3,0},{4,5},{5,6},{6,7},{7,4},{8,9},{9,10},{10,1... | collective-permute-start | bytes 196616 | tf_op jit(solution)/shard_map/ppermute | solution.py:357
  59.0 30.4 %collective-permute-start.10 = (bf16[16,2048]{1,0:T(8,128)(2,1)}, bf16[16,2048]{1,0:T(8,128)(2,1)S(1)}, u32[]{:S(2)}, u32[]{:S(2)}) collective-permute-start(bf16[16,2048]{1,0:T(8,128)(2,1)} %copy-done.23), channel_id=1, source_target_pairs={{0,2},{1,3},{2,0},{3,1},{4,6},{5,7},{6,4},{7,5},{8,10},{9,11},{10,... | collective-permute-start | bytes 196616 | tf_op jit(solution)/shard_map/ppermute | solution.py:357
  60.7 38.4 %collective-permute-start.12 = (bf16[16,2048]{1,0:T(8,128)(2,1)}, bf16[16,2048]{1,0:T(8,128)(2,1)S(1)}, u32[]{:S(2)}, u32[]{:S(2)}) collective-permute-start(bf16[16,2048]{1,0:T(8,128)(2,1)} %copy-done.21), channel_id=1, source_target_pairs={{0,3},{1,0},{2,1},{3,2},{4,7},{5,4},{6,5},{7,6},{8,11},{9,8},{10,9... | collective-permute-start | bytes 196616 | tf_op jit(solution)/shard_map/ppermute | solution.py:357
  62.0 38.4 %collective-permute-start.7 = (bf16[16,2048]{1,0:T(8,128)(2,1)}, bf16[16,2048]{1,0:T(8,128)(2,1)S(1)}, u32[]{:S(2)}, u32[]{:S(2)}) collective-permute-start(bf16[16,2048]{1,0:T(8,128)(2,1)} %copy-done.22), channel_id=1, source_target_pairs={{0,1},{1,2},{2,3},{3,0},{4,5},{5,6},{6,7},{7,4},{8,9},{9,10},{10,1... | collective-permute-start | bytes 196616 | tf_op jit(solution)/shard_map/ppermute | solution.py:357
  62.0 39.8 %collective-permute-start.9 = (bf16[16,2048]{1,0:T(8,128)(2,1)}, bf16[16,2048]{1,0:T(8,128)(2,1)}, u32[]{:S(2)}, u32[]{:S(2)}) collective-permute-start(bf16[16,2048]{1,0:T(8,128)(2,1)} %copy-done.20), channel_id=1, source_target_pairs={{0,2},{1,3},{2,0},{3,1},{4,6},{5,7},{6,4},{7,5},{8,10},{9,11},{10,... | collective-permute-start | bytes 196616 | tf_op jit(solution)/shard_map/ppermute | solution.py:357
  73.9 1.6 %copy-start.5 = (bf16[8,26,4096]{2,1,0:T(8,128)(2,1)S(1)}, bf16[8,26,4096]{2,1,0:T(8,128)(2,1)}, u32[]{:S(2)}) copy-start(bf16[8,26,4096]{2,1,0:T(8,128)(2,1)} %copy-done.4) | copy-start | bytes 5111812
  75.5 0.8 copy-start.7
  76.4 0.9 copy-start.11
  77.3 0.8 copy-start.13
  78.2 0.8 copy-start.15
  79.0 0.8 copy-start.17
  79.8 9.3 %copy-start.19 = (bf16[16,2048]{1,0:T(8,128)(2,1)S(1)}, bf16[16,2048]{1,0:T(8,128)(2,1)}, u32[]{:S(2)}) copy-start(bf16[16,2048]{1,0:T(8,128)(2,1)} %copy-done.18) | copy-start | bytes 196612
  79.8 9.9 %copy-start.9 = (bf16[64,2048]{1,0:T(8,128)(2,1)S(1)}, bf16[64,2048]{1,0:T(8,128)(2,1)}, u32[]{:S(2)}) copy-start(bf16[64,2048]{1,0:T(8,128)(2,1)} %copy-done.8) | copy-start | bytes 786436
  89.2 12.7 %collective-permute-start.11 = (bf16[16,2048]{1,0:T(8,128)(2,1)S(1)}, bf16[16,2048]{1,0:T(8,128)(2,1)S(1)}, u32[]{:S(2)}, u32[]{:S(2)}) collective-permute-start(bf16[16,2048]{1,0:T(8,128)(2,1)S(1)} %copy-done.19), channel_id=1, source_target_pairs={{0,3},{1,0},{2,1},{3,2},{4,7},{5,4},{6,5},{7,6},{8,11},{9,8},{10,9... | collective-permute-start | bytes 196616 | tf_op jit(solution)/shard_map/ppermute | solution.py:357
  89.4 13.0 %collective-permute-start.14 = (bf16[16,2048]{1,0:T(8,128)(2,1)S(1)}, bf16[16,2048]{1,0:T(8,128)(2,1)S(1)}, u32[]{:S(2)}, u32[]{:S(2)}) collective-permute-start(bf16[16,2048]{1,0:T(8,128)(2,1)S(1)} %get-tuple-element.54), channel_id=1, source_target_pairs={{0,1},{1,2},{2,3},{3,0},{4,5},{5,6},{6,7},{7,4},{8,9},{9,10},{10,1... | collective-permute-start | bytes 196616 | tf_op jit(solution)/shard_map/ppermute | solution.py:357
  99.0 7.5 %collective-permute-start.16 = (bf16[16,2048]{1,0:T(8,128)(2,1)S(1)}, bf16[16,2048]{1,0:T(8,128)(2,1)S(1)}, u32[]{:S(2)}, u32[]{:S(2)}) collective-permute-start(bf16[16,2048]{1,0:T(8,128)(2,1)S(1)} %get-tuple-element.56), channel_id=1, source_target_pairs={{0,2},{1,3},{2,0},{3,1},{4,6},{5,7},{6,4},{7,5},{8,10},{9,11},{10,... | collective-permute-start | bytes 196616 | tf_op jit(solution)/shard_map/ppermute | solution.py:357
  100.4 6.2 %collective-permute-start.18 = (bf16[16,2048]{1,0:T(8,128)(2,1)S(1)}, bf16[16,2048]{1,0:T(8,128)(2,1)S(1)}, u32[]{:S(2)}, u32[]{:S(2)}) collective-permute-start(bf16[16,2048]{1,0:T(8,128)(2,1)S(1)} %get-tuple-element.58), channel_id=1, source_target_pairs={{0,3},{1,0},{2,1},{3,2},{4,7},{5,4},{6,5},{7,6},{8,11},{9,8},{10,9... | collective-permute-start | bytes 196616 | tf_op jit(solution)/shard_map/ppermute | solution.py:357
  101.8 4.8 %collective-permute-start.13 = (bf16[16,2048]{1,0:T(8,128)(2,1)S(1)}, bf16[16,2048]{1,0:T(8,128)(2,1)S(1)}, u32[]{:S(2)}, u32[]{:S(2)}) collective-permute-start(bf16[16,2048]{1,0:T(8,128)(2,1)S(1)} %get-tuple-element.53), channel_id=1, source_target_pairs={{0,1},{1,2},{2,3},{3,0},{4,5},{5,6},{6,7},{7,4},{8,9},{9,10},{10,1... | collective-permute-start | bytes 196616 | tf_op jit(solution)/shard_map/ppermute | solution.py:357
  101.8 5.0 %collective-permute-start.15 = (bf16[16,2048]{1,0:T(8,128)(2,1)S(1)}, bf16[16,2048]{1,0:T(8,128)(2,1)S(1)}, u32[]{:S(2)}, u32[]{:S(2)}) collective-permute-start(bf16[16,2048]{1,0:T(8,128)(2,1)S(1)} %get-tuple-element.55), channel_id=1, source_target_pairs={{0,2},{1,3},{2,0},{3,1},{4,6},{5,7},{6,4},{7,5},{8,10},{9,11},{10,... | collective-permute-start | bytes 196616 | tf_op jit(solution)/shard_map/ppermute | solution.py:357
  102.4 4.4 %collective-permute-start.17 = (bf16[16,2048]{1,0:T(8,128)(2,1)S(1)}, bf16[16,2048]{1,0:T(8,128)(2,1)S(1)}, u32[]{:S(2)}, u32[]{:S(2)}) collective-permute-start(bf16[16,2048]{1,0:T(8,128)(2,1)S(1)} %get-tuple-element.57), channel_id=1, source_target_pairs={{0,3},{1,0},{2,1},{3,2},{4,7},{5,4},{6,5},{7,6},{8,11},{9,8},{10,9... | collective-permute-start | bytes 196616 | tf_op jit(solution)/shard_map/ppermute | solution.py:357

commit v2 on v1

--- a/solution.py
+++ b/solution.py
@@ -9,7 +9,7 @@
 
 BF = jnp.bfloat16
 F32 = jnp.float32
-VMEM_LIMIT = 48 * 1024 * 1024
+VMEM_LIMIT = 26 * 1024 * 1024
 
 
 def low_half(shape):
@@ -90,7 +90,7 @@
                 ]
         return carry
 
-    lax.fori_loop(0, pairs, one, 0, unroll=2)
+    lax.fori_loop(0, pairs, one, 0, unroll=8)
 
 
 def fill_right(rmat, right_tiles, lane):
@@ -126,6 +126,7 @@
 def left_kernel(parts_count, wide, phys, _, left_a, left_b, vec_a, vec_b, *refs):
     parts = refs[:parts_count]
     mixed, both, lhs, rhs, amat, con = refs[parts_count:]
+    mixed, both = mixed.at[0], both.at[0]
     lane = 2 * wide
     copy_operator(amat, parts)
     fill_left(lhs, (left_a, left_b), wide)
@@ -148,100 +149,107 @@
         out[...] = image[pl.ds(pl.multiple_of(quarter * rows, rows), rows), :]
 
 
-def right_kernel(terms, kinds, wide, phys, place, mixed, both, *refs):
-    rights = refs[: len(kinds)]
-    image, stats = refs[len(kinds)], refs[len(kinds) + 1]
-    outs = refs[len(kinds) + 2 : len(kinds) + 2 + terms]
-    rmat, acc = refs[len(kinds) + 2 + terms :]
-    lane = 2 * wide
-    fill_right(
-        rmat,
-        [
-            lambda pair, ref=ref, at=at: ref[at, :, pair * lane : (pair + 1) * lane]
-            for ref, at in zip(rights, kinds)
-        ],
-        lane,
-    )
-    contract_right(mixed, rmat, acc)
-    norm = jnp.zeros((wide, lane), F32)
-    corr = jnp.zeros((wide, lane), F32)
-    for y in range(phys):
-        cols = slice(y * lane, (y + 1) * lane)
-        tile = acc[pl.ds(y, wide, stride=phys), :].astype(BF)
-        image[:, cols] = tile
-        value = tile.astype(F32)
-        vec = both[:, cols].astype(F32)
-        norm += vec * vec
-        corr += vec * value
-    norm = jnp.sum(norm, keepdims=True)
-    corr = jnp.sum(corr, keepdims=True)
-    ratio = jnp.where(norm > 0, corr / jnp.where(norm > 0, norm, 1.0), 0.0)
-    square = jnp.zeros((wide, lane), F32)
-    cross = jnp.zeros((wide, lane), F32)
-    for y in range(phys):
-        cols = slice(y * lane, (y + 1) * lane)
-        vec = both[:, cols].astype(F32)
-        rest = image[:, cols].astype(F32) - ratio * vec
-        square += rest * rest
-        cross += rest * vec
-    square = jnp.sum(square, keepdims=True)
-    cross = jnp.sum(cross, keepdims=True)
-    at = lax.broadcasted_iota(jnp.int32, stats.shape, 1)
-    row = jnp.zeros(stats.shape, F32)
-    for i, value in enumerate((norm, corr, ratio, square, cross)):
-        row = jnp.where(at == i, value, row)
-    stats[...] = row
-    split_rows(place, image, outs)
+def right_kernel(terms, kinds, wide, phys, place, mixes, boths, *refs):
+    pairs = len(kinds)
+    count = len({at for pair in kinds for at, _ in pair})
+    rights, refs = refs[:count], refs[count:]
+    images, line = refs[:2]
+    outs, (rmat, acc) = refs[2 : 2 + terms], refs[2 + terms :]
+    lane = 2 * wide
+    for pi in range(pairs):
+        mixed, both, image = mixes.at[pi], boths.at[pi], images.at[pi]
+        fill_right(rmat, tiles_of(rights, kinds[pi], lane), lane)
+        contract_right(mixed, rmat, acc)
+        norm = jnp.zeros((wide, lane), F32)
+        corr = jnp.zeros((wide, lane), F32)
+        for y in range(phys):
+            cols = slice(y * lane, (y + 1) * lane)
+            tile = acc[pl.ds(y, wide, stride=phys), :].astype(BF)
+            image[:, cols] = tile
+            value = tile.astype(F32)
+            vec = both[:, cols].astype(F32)
+            norm += vec * vec
+            corr += vec * value
+        norm = jnp.sum(norm, keepdims=True)
+        corr = jnp.sum(corr, keepdims=True)
+        ratio = jnp.where(norm > 0, corr / jnp.where(norm > 0, norm, 1.0), 0.0)
+        square = jnp.zeros((wide, lane), F32)
+        cross = jnp.zeros((wide, lane), F32)
+        for y in range(phys):
+            cols = slice(y * lane, (y + 1) * lane)
+            vec = both[:, cols].astype(F32)
+            rest = image[:, cols].astype(F32) - ratio * vec
+            square += rest * rest
+            cross += rest * vec
+        square = jnp.sum(square, keepdims=True)
+        cross = jnp.sum(cross, keepdims=True)
+        at = lax.broadcasted_iota(jnp.int32, (1, lane), 1)
+        row = jnp.zeros((1, lane), F32)
+        for i, value in enumerate((norm, corr, ratio, square, cross)):
+            row = jnp.where(at == i, value, row)
+        line[:, :, pi * lane : (pi + 1) * lane] = jnp.broadcast_to(
+            row[None], (line.shape[0], 1, lane)
+        )
+        split_rows(place, image, [out.at[pi] for out in outs])
+
+
+def tiles_of(rights, kind, lane):
+    return [
+        lambda pair, ref=rights[array], at=at: ref[at, :, pair * lane : (pair + 1) * lane]
+        for array, at in kind
+    ]
+
+
+def scalars(everyone):
+    norm, corr, own, square, cross = (everyone[:, i : i + 1] for i in range(5))
+    norm_sq = jnp.sum(norm, keepdims=True)
+    ratio = jnp.sum(corr, keepdims=True) / norm_sq
+    off = own - ratio
+    residual_sq = jnp.sum(square + 2 * off * cross + off * off * norm, keepdims=True)
+    return ratio, jnp.sqrt(norm_sq / (residual_sq + 1e-06))
 
 
 def second_kernel(terms, kinds, wide, phys, place, scal, left_a, left_b, both, image, *refs):
+    both, image = both.at[0], image.at[0]
     parts, refs = refs[:terms], refs[terms:]
-    rights, refs = refs[: len(kinds)], refs[len(kinds) :]
+    rights, refs = refs[:2], refs[2:]
     outs, refs = refs[:terms], refs[terms:]
     lhs, rhs, amat, con, mixed, rmat, acc, result = refs
     lane = 2 * wide
     copy_operator(amat, parts)
     fill_left(lhs, (left_a, left_b), wide)
-    ratio, scale = scal[0], scal[1]
+    ratio, scale = scalars(scal)
     for s in range(phys):
         cols = slice(s * lane, (s + 1) * lane)
         rest = image[:, cols].astype(F32) - ratio * both[:, cols].astype(F32)
         put_source(rhs, s, (rest * scale).astype(BF).astype(F32))
     contract_left(lhs, rhs, con)
     mix(amat, con, mixed, phys, lane)
-    fill_right(
-        rmat,
-        [
-            lambda pair, ref=ref, at=at: ref[at, :, pair * lane : (pair + 1) * lane]
-            for ref, at in zip(rights, kinds)
-        ],
-        lane,
-    )
+    fill_right(rmat, tiles_of(rights, kinds, lane), lane)
     contract_right(mixed, rmat, acc)
     for y in range(phys):
         result[:, y * lane : (y + 1) * lane] = acc[pl.ds(y, wide, stride=phys), :].astype(BF)
     split_rows(place, result, outs)
 
 
-def select_kernel(terms, wide, names, blocks, *refs):
+def select_kernel(wide, names, blocks, *refs):
     envs, outs = refs[: len(blocks)], refs[len(blocks) : -2]
     spread, rows_out = refs[-2:]
     env_width = envs[0].shape[1]
     lane = 2 * wide
     half = wide // 2
     groups = outs[0].shape[2] // wide
-    local = groups // terms
-    turn = names[groups]
     for env, (out, at) in zip(envs, blocks):
         for z in range(half):
-            spread[pl.ds(z, env_width, stride=half), :] = env[
-                0, :, z * lane : (z + 1) * lane
-            ].astype(F32)
+            tile = env[0, :, z * lane : (z + 1) * lane].astype(F32)
+            for top in range(0, env_width, 8):
+                part = tile[top : top + 8]
+                base = top * half + z * 8
+                spread[base : base + part.shape[0], :] = part
 
         def rows_of(g):
-            k = lax.rem(turn + g // local, terms)
-            name = names[k * local + g % local]
-            return spread[pl.ds(pl.multiple_of(name * half, half), half), :]
+            name = names[g]
+            return spread[pl.ds((name // 8) * (8 * half) + name % 8, half, stride=8), :]
 
         for pair in range(groups // 2):
             even, odd = two_in_lanes(rows_of(2 * pair), rows_of(2 * pair + 1))
@@ -253,7 +261,9 @@
 def place_kernel(terms, pairs, wide, phys, follows, table, *refs):
     if follows:
         scal, rows, refs = refs[0], refs[1], refs[2:]
-    pieces, refs = refs[: terms * pairs], refs[terms * pairs :]
+        ratio, scale = scalars(scal)
+    count = terms if follows else terms * pairs
+    pieces, refs = refs[:count], refs[count:]
     out = refs[0]
     lane = 2 * wide
     slots = out.shape[0] // terms
@@ -261,7 +271,7 @@
     for k in range(terms):
         source = lax.rem(me + terms - k, terms)
         for pi in range(pairs):
-            piece = pieces[k * pairs + pi]
+            piece = pieces[k].at[pi] if follows else pieces[k * pairs + pi]
             first = table[source * slots + 2 * pi]
             second = table[source * slots + 2 * pi + 1]
             for pair in range(phys // 2):
@@ -273,7 +283,6 @@
                 out[first, :, cols] = a.astype(BF)
                 out[second, :, cols] = b.astype(BF)
                 if follows:
-                    ratio, scale = scal[0], scal[1]
                     for where, value in ((first, a), (second, b)):
                         rest = value - ratio * rows[where, :, cols].astype(F32)
                         refs[1][where, :, cols] = (rest * scale).astype(BF)
@@ -283,15 +292,15 @@
     return pl.BlockSpec(shape, lambda *_: (0,) * len(shape))
 
 
-def call(kernel, prefetch, in_specs, out_shapes, scratch, flops, moved):
+def call(kernel, prefetch, in_specs, out_shapes, scratch, flops, moved, grid=1, out_specs=None):
     return pl.pallas_call(
         kernel,
         out_shape=out_shapes,
         grid_spec=pltpu.PrefetchScalarGridSpec(
             num_scalar_prefetch=prefetch,
-            grid=(1,),
+            grid=(grid,),
             in_specs=in_specs,
-            out_specs=[whole(s.shape) for s in out_shapes],
+            out_specs=out_specs or [whole(s.shape) for s in out_shapes],
             scratch_shapes=scratch,
         ),
         compiler_params=pltpu.CompilerParams(vmem_limit_bytes=VMEM_LIMIT),
@@ -320,12 +329,18 @@
     both_axes = ("sec", "term")
     vec = vector.reshape(blocks, wide, row_width)
 
+    lines = terms // 2
+
+    def flip(t, a):
+        return (t % 2 * span + a) * lines + t // 2
+
     flat = right_sector.reshape(blocks)
     dest = flat // per_device
     before = jnp.arange(blocks)[None, :] < jnp.arange(blocks)[:, None]
     rank = jnp.sum((dest[None, :] == dest[:, None]) & before, axis=1)
-    turn = lax.rem(dest - d + secs, span)
-    place = (dest // span) * slots + turn * each + rank
+    flips = dest ^ d
+    column = flips // lines
+    place = (flips % lines * 2 + column // span) * slots + column % span * each + rank
     hit = place[None, :] == jnp.arange(blocks)[:, None]
     order = jnp.sum(jnp.where(hit, jnp.arange(blocks)[None, :], 0), axis=1)
     by_place = jnp.sum(jnp.where(hit, (flat % per_device)[None, :], 0), axis=1)
@@ -333,15 +348,12 @@
     wanted = lax.dynamic_slice(by_place, (me * slots,), (slots,)).astype(jnp.int32)
     table = jnp.concatenate([order.astype(jnp.int32), me.reshape(1)])
 
-    def partner(a, device, term):
-        return (term * span + (a + device) % span) * terms + device // span
-
-    asks = [
-        [(dd * terms + t, partner(a, dd, t)) for dd in range(secs) for t in range(terms)]
+    swaps = [
+        [(e * terms + t, (e ^ flip(t, a)) * terms + t) for e in range(secs) for t in range(terms)]
         for a in range(span)
     ]
     asked = [
-        lax.ppermute(wanted[a * each : (a + 1) * each], both_axes, asks[a]) for a in range(span)
+        lax.ppermute(wanted[a * each : (a + 1) * each], both_axes, swaps[a]) for a in range(span)
     ]
 
     onehot = (term_left[:, :, None] == jnp.arange(depth)).astype(BF)
@@ -358,8 +370,6 @@
 
     parts = [packed] + [shift(packed, k) for k in range(1, terms)]
     known = jnp.concatenate([p[local * phys, :local] for p in parts]).astype(jnp.int32)
-    receiver = d // span
-    names = jnp.concatenate([known, lax.rem(me - receiver + terms, terms).reshape(1)])
     asked = jnp.concatenate(asked)
 
     env_block = (1, env_width, wide * wide)
@@ -368,7 +378,7 @@
         functools.partial(
             lambda fn, names, asked, *refs: fn(names, *refs),
             lambda names, *refs: select_kernel(
-                terms, wide, names, [(i // each, i % each) for i in range(slots)], *refs
+                wide, names, [(i // each, i % each) for i in range(slots)], *refs
             ),
         ),
         2,
@@ -377,15 +387,13 @@
         ],
         [right_shape] * span,
         [
-            pltpu.VMEM((env_width * (wide // 2), lane), F32),
+            pltpu.VMEM((-(-env_width // 8) * 8 * (wide // 2), lane), F32),
             pltpu.VMEM((wide, lane), F32),
         ],
         0,
         slots * env_width * wide * wide * 2,
-    )(names, asked, *([right_env] * slots))
-    rights = [
-        lax.ppermute(chosen[a], both_axes, [(t, s) for s, t in asks[a]]) for a in range(span)
-    ]
+    )(known, asked, *([right_env] * slots))
+    rights = [lax.ppermute(chosen[a], both_axes, swaps[a]) for a in range(span)]
 
     rows = wide * depth
     left_flops = 2 * rows * 4 * wide * phys * lane
@@ -414,102 +422,95 @@
             for i in (2 * pi, 2 * pi + 1)
         ]
 
-    mixes = []
+    def of_pair(shape):
+        return pl.BlockSpec((1, *shape), lambda i, *_: (i, *(0,) * len(shape)))
+
+    def stacked(shape):
+        return jax.ShapeDtypeStruct((pairs, *shape.shape), shape.dtype)
+
+    mixes, boths = call(
+        functools.partial(left_kernel, terms, wide, phys),
+        1,
+        [
+            pl.BlockSpec(env_block, lambda i, o, b=b: (lax.div(o[2 * i + b], per_left), 0, 0))
+            for b in range(2)
+        ]
+        + [
+            pl.BlockSpec((1, wide, row_width), lambda i, o, b=b: (o[2 * i + b], 0, 0))
+            for b in range(2)
+        ]
+        + [whole(part_shape)] * terms,
+        [stacked(mixed_shape), stacked(full_shape)],
+        con_scratch,
+        pairs * (left_flops + mix_flops),
+        pairs * wide * phys * groups * lane * 2,
+        pairs,
+        [of_pair(mixed_shape.shape), of_pair(full_shape.shape)],
+    )(own, left_env, left_env, vec, vec, *parts)
+
+    where = me.reshape(1).astype(jnp.int32)
+    kinds = [[((2 * pi + b) // each, (2 * pi + b) % each) for b in range(2)] for pi in range(pairs)]
+    images, line, *pieces = call(
+        functools.partial(right_kernel, terms, kinds, wide, phys),
+        1,
+        [whole((pairs, *mixed_shape.shape)), whole((pairs, *full_shape.shape))]
+        + [whole(right_shape.shape)] * span,
+        [stacked(full_shape), jax.ShapeDtypeStruct((secs * terms, 1, pairs * lane), F32)]
+        + [stacked(piece_shape)] * terms,
+        right_scratch,
+        pairs * right_flops,
+        pairs * wide * phys * groups * lane * 2,
+    )(where, mixes, boths, *rights)
+
+    everyone = lax.all_to_all(line, both_axes, 0, 0, tiled=True).reshape(-1, lane)
+    pieces, everyone = lax.optimization_barrier((pieces, everyone))
+    first_pieces = [pieces[0]] + [shift(pieces[k], k) for k in range(1, terms)]
+
+    sums_spec = whole(everyone.shape)
+    second_pieces = [None] * (terms * pairs)
+    sums = everyone
     for pi in range(pairs):
-        mixes.append(
-            call(
-                functools.partial(left_kernel, terms, wide, phys),
-                1,
-                left_specs(pi)
-                + [
-                    pl.BlockSpec((1, wide, row_width), lambda _, o, i=i: (o[i], 0, 0))
-                    for i in (2 * pi, 2 * pi + 1)
-                ]
-                + [whole(part_shape)] * terms,
-                [mixed_shape, full_shape],
-                con_scratch,
-                left_flops + mix_flops,
-                wide * phys * groups * lane * 2,
-            )(own, left_env, left_env, vec, vec, *parts)
+        if pi == pairs - 1:
+            first_pieces, sums = lax.optimization_barrier((first_pieces, sums))
+        one_pair = pl.BlockSpec((1, *full_shape.shape), lambda *_, pi=pi: (pi, 0, 0))
+        outs = call(
+            functools.partial(
+                lambda fn, own, place, *refs: fn(place, *refs),
+                functools.partial(
+                    second_kernel, terms, [(b, at) for b, (_, at) in enumerate(kinds[pi])], wide, phys
+                ),
+            ),
+            2,
+            [sums_spec]
+            + left_specs(pi)
+            + [one_pair] * 2
+            + [whole(part_shape)] * terms
+            + [whole(right_shape.shape)] * 2,
+            [piece_shape] * terms,
+            con_scratch
+            + [pltpu.VMEM(mixed_shape.shape, BF)]
+            + right_scratch
+            + [pltpu.VMEM(full_shape.shape, BF)],
+            left_flops + mix_flops + right_flops,
+            4 * wide * phys * lane * 2,
+        )(
+            own, where, sums, left_env, left_env, boths, images, *parts,
+            *(rights[array] for array, _ in kinds[pi]),
         )
-
-    where = me.reshape(1).astype(jnp.int32)
-    images, stats, pieces = [], [], []
-    for pi in range(pairs):
-        kinds = [(2 * pi) % each, (2 * pi + 1) % each]
-        using = [rights[(2 * pi) // each], rights[(2 * pi + 1) // each]]
-        image, stat, *outs = call(
-            functools.partial(right_kernel, terms, kinds, wide, phys),
-            1,
-            [whole(mixed_shape.shape), whole(full_shape.shape)] + [whole(right_shape.shape)] * 2,
-            [full_shape, jax.ShapeDtypeStruct((1, lane), F32)] + [piece_shape] * terms,
-            right_scratch,
-            right_flops,
-            wide * phys * groups * lane * 2,
-        )(where, *mixes[pi], *using)
-        images.append(image)
-        stats.append(stat)
-        pieces.append(outs)
-
-    def spread(pieces):
-        return [
-            pieces[pi][k] if k == 0 else shift(pieces[pi][k], k)
-            for k in range(terms)
-            for pi in range(pairs)
-        ]
-
-    first_pieces = spread(pieces)
-
-    line = jnp.concatenate(stats, axis=0).reshape(1, pairs * lane)
-    everyone = lax.all_to_all(
-        jnp.broadcast_to(line, (secs * terms, pairs * lane)), both_axes, 0, 0, tiled=True
-    ).reshape(secs * terms * pairs, lane)
-    sums = [everyone[:, i] for i in range(5)]
-    norm_sq = jnp.sum(sums[0])
-    ratio = jnp.sum(sums[1]) / norm_sq
-    off = sums[2] - ratio
-    residual_sq = jnp.sum(sums[3] + 2 * off * sums[4] + off * off * sums[0])
-    scal = jnp.stack([ratio, jnp.sqrt(norm_sq / (residual_sq + 1e-06))])
-
-    smem = pl.BlockSpec(memory_space=pltpu.SMEM)
-    pieces = []
-    for pi in range(pairs):
-        kinds = [(2 * pi) % each, (2 * pi + 1) % each]
-        using = [rights[(2 * pi) // each], rights[(2 * pi + 1) // each]]
-        pieces.append(
-            call(
-                functools.partial(
-                    lambda fn, own, place, *refs: fn(place, *refs),
-                    functools.partial(second_kernel, terms, kinds, wide, phys),
-                ),
-                2,
-                [smem]
-                + left_specs(pi)
-                + [whole(full_shape.shape)] * 2
-                + [whole(part_shape)] * terms
-                + [whole(right_shape.shape)] * 2,
-                [piece_shape] * terms,
-                con_scratch
-                + [pltpu.VMEM(mixed_shape.shape, BF)]
-                + right_scratch
-                + [pltpu.VMEM(full_shape.shape, BF)],
-                left_flops + mix_flops + right_flops,
-                4 * wide * phys * lane * 2,
-            )(own, where, scal, left_env, left_env, mixes[pi][1], images[pi], *parts, *using)
-        )
-    second_pieces = spread(pieces)
+        for k, out in enumerate(outs):
+            second_pieces[k * pairs + pi] = out if k == 0 else shift(out, k)
 
     out_shape = jax.ShapeDtypeStruct((blocks, slab, row_width), BF)
     first_image, next_rows = call(
         functools.partial(place_kernel, terms, pairs, wide, phys, True),
         1,
-        [smem, pl.BlockSpec((blocks, slab, row_width), lambda _, t: (0, t[blocks], 0))]
-        + [whole(piece_shape.shape)] * (terms * pairs),
+        [sums_spec, pl.BlockSpec((blocks, slab, row_width), lambda _, t: (0, t[blocks], 0))]
+        + [whole((pairs, *piece_shape.shape))] * terms,
         [out_shape] * 2,
         [],
         0,
         blocks * slab * row_width * 8,
-    )(table, scal, vec, *first_pieces)
+    )(table, everyone, vec, *first_pieces)
     (second_image,) = call(
         functools.partial(place_kernel, terms, pairs, wide, phys, False),
         1,

time: 109 us -> 75.4 us (0.69)
  blocking collectives: 0 us -> 20 us
  starting transfers between devices: 31 us -> 13.7 us
  Pallas kernels: 47 us -> 32.6 us
  local copies, waits for them, and re-layouts: 18.6 us -> 4.89 us
  waiting for transfers between devices: 3.82 us -> 0.69 us
  between operations: 3.54 us -> 0.84 us
  other arithmetic: 3.41 us -> 1.27 us
    all_to_all x0 -> x1, blocking collectives: none -> 20 us  [body(): lax.all_to_all(line, both_axes, 0, 0, tiled=True).reshape(-1, lane)]
    all_to_all x1 -> x0, starting transfers between devices: 15.1 us -> none  [body(): lax.all_to_all(jnp.broadcast_to(line, (secs * terms, pairs * lane)), both...]
    unnamed x59 -> x9, local copies, waits for them, and re-layouts: 17.5 us -> 4.39 us
    pallas_call x2 -> x1, Pallas kernels: 18.6 us -> 10.5 us  [body(): call(functools.partial(left_kernel, terms, wide, phys), 1, [pl.BlockSpec(...]
    pallas_call x2, Pallas kernels: 18.6 us -> 14.3 us  [body(): call(functools.partial(lambda fn, own, place, *refs: fn(place, *refs), fu...]
    all_to_all x1 -> x0, waiting for transfers between devices: 3.55 us -> none  [body(): lax.all_to_all(jnp.broadcast_to(line, (secs * terms, pairs * lane)), both...]
    ppermute x15 -> x12, starting transfers between devices: 12.2 us -> 10.2 us  [shift(): lax.ppermute(value, 'term', [(t, (t + k) % terms) for t in range(terms)])]
    slice x1 -> x0, other arithmetic: 1.39 us -> none  [body(): sums = [everyone[:, i] for i in range(5)]]
  transfers between devices with their start and end apart: 20 -> 16, of which waited for: 2 -> 1; matrix products, arithmetic and copies ran while one was open for 10% -> 7% of each run, Pallas kernels for 38% -> 36%
where the time goes in v2:
time: 75.4 us; the launch traced here: 75 us
  Pallas kernels  32.6 us (43%)
  blocking collectives  20 us (27%)
  starting transfers between devices  13.7 us (18%)
  local copies, waits for them, and re-layouts  4.89 us (6%)
  other arithmetic  1.27 us (2%)
  matrix products  0.98 us (1%)
  between operations  0.84 us (1%)
    all_to_all x1, blocking collectives, body(): lax.all_to_all(line, both_axes, 0, 0, tiled=True).reshape(-1, lane)  20 us
    pallas_call x2, Pallas kernels, body(): call(functools.partial(lambda fn, own, place, *refs: fn(place, *refs), fu...  14.3 us
    pallas_call x1, Pallas kernels, body(): call(functools.partial(left_kernel, terms, wide, phys), 1, [pl.BlockSpec(...  10.5 us
    ppermute x12, starting transfers between devices, shift(): lax.ppermute(value, 'term', [(t, (t + k) % terms) for t in range(terms)])  10.2 us
    unnamed x9, local copies, waits for them, and re-layouts  4.39 us
    pallas_call x1, Pallas kernels, body(): call(functools.partial(right_kernel, terms, kinds, wide, phys), 1, [whole...  2.76 us
    ppermute x2, starting transfers between devices, body(): lax.ppermute(wanted[a * each:(a + 1) * each], both_axes, swaps[a])  2.3 us
    pallas_call x1, Pallas kernels, body(): call(functools.partial(place_kernel, terms, pairs, wide, phys, True), 1,...  2.29 us
  transfers between devices with their start and end apart: 16, of which 1 were waited for; matrix products, arithmetic and copies ran while one was open for 7% of the time, Pallas kernels for 36%

profile of v2, /device:TPU:0, one launch (start us, length us, event | category | flops | bytes accessed | tf_op | source)
XLA Modules:
  0.0 75.0 jit_solution(10326315352688486156)
XLA Ops:
  0.6 0.0 copy-start
  0.6 0.7 convert_convert_fusion
  1.3 0.2 copy-done
  1.5 1.0 %fusion = bf16[3,16,16,32]{3,2,1,0:T(8,128)(2,1)S(1)} fusion(bf16[3,8,16,16]{3,2,1,0:T(8,128)(2,1)S(1)} %copy-done, s32[3,8]{1,0:T(4,128)} %param.12), kind=kOutput, calls=%fused_computation.1 | convolution fusion | flops 418560 | bytes 61536 | tf_op jit(solution)/shard_map/gtys,gtw->gysw/dot_general | solution.py:360
  2.5 0.0 copy-start.2
  2.5 0.2 reshape.184
  2.7 2.4 %collective-permute-start.2 = (bf16[64,512]{1,0:T(8,128)(2,1)S(1)}, bf16[64,512]{1,0:T(8,128)(2,1)S(1)}, u32[]{:S(2)}, u32[]{:S(2)}) collective-permute-start(bf16[64,512]{1,0:T(8,128)(2,1)S(1)} %fusion.3.refs_0_.refs_5_), channel_id=1, source_target_pairs={{0,3},{1,0},{2,1},{3,2},{4,7},{5,4},{6,5},{7,6},{8,11},{9,8},{10,9... | collective-permute-start | bytes 196616 | tf_op jit(solution)/shard_map/ppermute | solution.py:369
  5.2 0.6 collective-permute-start.1
  5.8 0.2 collective-permute-start
  6.0 0.8 %copy.34 = s32[8,2]{1,0:T(8,128)S(1)} copy(s32[8,2]{0,1:T(2,128)} %param.8) | data formatting | bytes 128 | tf_op args[1]
  6.7 0.1 reshape.181
  6.8 0.2 convert_reduce_fusion
  7.0 0.1 select_reduce_fusion
  7.2 0.1 dynamic_slice.7
  7.2 0.1 fusion.14
  7.3 0.7 collective-permute-start.3
  8.0 1.6 %collective-permute-start.4 = (s32[2]{0:T(128)S(1)}, s32[2]{0:T(128)S(1)}, u32[]{:S(2)}, u32[]{:S(2)}) collective-permute-start(s32[2]{0:T(128)S(1)} %get-tuple-element.66), channel_id=1, source_target_pairs={{0,8},{1,25},{2,14},{3,31},{4,12},{5,29},{6,10},{7,27},{8,0},{9,17... | collective-permute-start | bytes 32 | tf_op jit(solution)/shard_map/ppermute | solution.py:356
  9.6 0.1 dynamic_slice.6._.own
  9.7 2.4 %copy.36.left_a.left_b.refs_1_.refs_2_ = bf16[8,26,4096]{2,1,0:T(8,128)(2,1)S(1)} copy(bf16[8,26,4096]{2,0,1:T(8,128)(2,1)} %param.9) | data formatting | bytes 3407872 | tf_op args[2]
  12.2 1.0 %copy.38.refs_0_.refs_1_.refs_2_.refs_3_ = bf16[8,26,4096]{2,1,0:T(8,128)(2,1)S(1)} copy(bf16[8,26,4096]{2,0,1:T(8,128)(2,1)S(1)} %copy-done.2) | data formatting | bytes 3407872 | tf_op args[3]
  13.1 0.0 collective-permute-done.3
  13.1 0.0 collective-permute-done.4
  13.2 0.1 pad_add_fusion.1.asked
  13.2 0.0 collective-permute-done.2.refs_3_.refs_8_
  13.2 0.0 collective-permute-done.refs_1_.refs_6_
  13.3 0.1 maximum_convert_fusion.names
  13.4 1.1 %shard_map.95 = (bf16[2,64,768]{2,1,0:T(8,128)(2,1)S(1)}, bf16[2,64,768]{2,1,0:T(8,128)(2,1)S(1)}) custom-call(s32[12]{0:T(128)S(1)} %maximum_convert_fusion.names, s32[4]{0:T(128)S(1)} %pad_add_fusion.1.asked, bf16[8,26,4096]{2,1,0:T(8,128)(2,1)S(1)} %copy.38.refs_0_.refs_1_.refs_2_.refs_3_, bf16[8,26,4096]{2,1,0:T(8,128)(2,1)S(1)} %copy.38.refs_0_.refs_1_.refs_2_.refs_3_, ...), custom_call_target="tpu_custom_call" | custom-call | bytes 851968 | tf_op jit(solution)/shard_map/pallas_call | solution.py:377
  14.5 0.7 collective-permute-start.5
  15.2 0.5 collective-permute-start.6
  15.7 10.5 %shard_map.94 = (bf16[2,1024,1536]{2,1,0:T(8,128)(2,1)S(1)}, bf16[2,64,2048]{2,1,0:T(8,128)(2,1)S(1)}) custom-call(s32[4]{0:T(128)S(1)} %dynamic_slice.6._.own, bf16[8,26,4096]{2,1,0:T(8,128)(2,1)S(1)} %copy.36.left_a.left_b.refs_1_.refs_2_, bf16[8,26,4096]{2,1,0:T(8,128)(2,1)S(1)} %copy.36.left_a.left_b.refs_1_.refs_2_, bf16[16,64,1024]{2,1,0:T(8,128)(2,1)S(1)} %bitcast.23, ...), custom_call_target="tpu_custom_call" | custom-call | flops 7516192768 | bytes 6291456 | tf_op jit(solution)/shard_map/pallas_call | solution.py:431
  26.2 0.0 collective-permute-done.5.refs_0_.refs_9_.refs_10_
  26.2 2.8 %shard_map.96 = (bf16[2,64,2048]{2,1,0:T(8,128)(2,1)S(1)}, f32[32,1,256]{2,1,0:T(1,128)S(1)}, bf16[2,16,2048]{2,1,0:T(8,128)(2,1)S(1)}, bf16[2,16,2048]{2,1,0:T(...) custom-call(s32[1]{0:T(128)} %bitcast.place, ...), custom_call_target="tpu_custom_call" | custom-call | flops 805306368 | bytes 6291456 | tf_op jit(solution)/shard_map/pallas_call | solution.py:453
  29.0 20.0 %all_to_all.5 = f32[32,1,256]{2,1,0:T(1,128)S(1)} all-to-all(f32[32,1,256]{2,1,0:T(1,128)S(1)} %get-tuple-element.41), channel_id=1, replica_groups=mesh['sec'=8,'term'=4] {'sec','term'}, dimensions={0} | all-to-all | bytes 65536 | tf_op jit(solution)/shard_map/all_to_all | solution.py:465
  49.0 0.1 collective-permute-start.7
  49.1 0.5 collective-permute-start.8
  49.6 1.4 %collective-permute-start.9 = (bf16[2,16,2048]{2,1,0:T(8,128)(2,1)S(1)}, bf16[2,16,2048]{2,1,0:T(8,128)(2,1)S(1)}, u32[]{:S(2)}, u32[]{:S(2)}) collective-permute-start(bf16[2,16,2048]{2,1,0:T(8,128)(2,1)S(1)} %get-tuple-element.46), channel_id=1, source_target_pairs={{0,3},{1,0},{2,1},{3,2},{4,7},{5,4},{6,5},{7,6},{8,11},{9,8},{10,9... | collective-permute-start | bytes 393224 | tf_op jit(solution)/shard_map/ppermute | solution.py:369
  50.9 7.2 %shard_map.98 = (bf16[16,2048]{1,0:T(8,128)(2,1)S(1)}, bf16[16,2048]{1,0:T(8,128)(2,1)S(1)}, bf16[16,2048]{1,0:T(8,128)(2,1)S(1)}, bf16[16,2048]{1,0:T(8,128)(2,1)S(1)}) custom-call(s32[4]{0:T(128)S(1)} %dynamic_slice.6._.own, s32[1]{0:T(128)} %bitcast.place, f32[64,128]{1,0:T(8,128)S(1)} %bitcast.26, ...), custom_call_target="tpu_custom_call" | custom-call | flops 4160749568 | bytes 1048576 | tf_op jit(solution)/shard_map/pallas_call | solution.py:476
  58.1 0.1 collective-permute-start.10
  58.2 1.6 %collective-permute-start.12 = (bf16[16,2048]{1,0:T(8,128)(2,1)S(1)}, bf16[16,2048]{1,0:T(8,128)(2,1)S(1)}, u32[]{:S(2)}, u32[]{:S(2)}) collective-permute-start(bf16[16,2048]{1,0:T(8,128)(2,1)S(1)} %get-tuple-element.59), channel_id=1, source_target_pairs={{0,2},{1,3},{2,0},{3,1},{4,6},{5,7},{6,4},{7,5},{8,10},{9,11},{10,... | collective-permute-start | bytes 196616 | tf_op jit(solution)/shard_map/ppermute | solution.py:369
  59.8 1.4 %collective-permute-start.14 = (bf16[16,2048]{1,0:T(8,128)(2,1)S(1)}, bf16[16,2048]{1,0:T(8,128)(2,1)S(1)}, u32[]{:S(2)}, u32[]{:S(2)}) collective-permute-start(bf16[16,2048]{1,0:T(8,128)(2,1)S(1)} %get-tuple-element.61), channel_id=1, source_target_pairs={{0,3},{1,0},{2,1},{3,2},{4,7},{5,4},{6,5},{7,6},{8,11},{9,8},{10,9... | collective-permute-start | bytes 196616 | tf_op jit(solution)/shard_map/ppermute | solution.py:369
  61.2 7.2 %shard_map.99 = (bf16[16,2048]{1,0:T(8,128)(2,1)S(1)}, bf16[16,2048]{1,0:T(8,128)(2,1)S(1)}, bf16[16,2048]{1,0:T(8,128)(2,1)S(1)}, bf16[16,2048]{1,0:T(8,128)(2,1)S(1)}) custom-call(s32[4]{0:T(128)S(1)} %dynamic_slice.6._.own, s32[1]{0:T(128)} %bitcast.place, f32[64,128]{1,0:T(8,128)S(1)} %bitcast.27, ...), custom_call_target="tpu_custom_call" | custom-call | flops 4160749568 | bytes 1048576 | tf_op jit(solution)/shard_map/pallas_call | solution.py:476
  68.3 0.1 collective-permute-start.11
  68.4 0.6 collective-permute-start.13
  69.0 1.4 %collective-permute-start.15 = (bf16[16,2048]{1,0:T(8,128)(2,1)S(1)}, bf16[16,2048]{1,0:T(8,128)(2,1)S(1)}, u32[]{:S(2)}, u32[]{:S(2)}) collective-permute-start(bf16[16,2048]{1,0:T(8,128)(2,1)S(1)} %get-tuple-element.62), channel_id=1, source_target_pairs={{0,3},{1,0},{2,1},{3,2},{4,7},{5,4},{6,5},{7,6},{8,11},{9,8},{10,9... | collective-permute-start | bytes 196616 | tf_op jit(solution)/shard_map/ppermute | solution.py:369
  70.4 0.1 pad_add_fusion.table
  70.4 2.3 %shard_map.97 = (bf16[16,16,1024]{2,1,0:T(8,128)(2,1)}, bf16[16,16,1024]{2,1,0:T(8,128)(2,1)}) custom-call(s32[17]{0:T(128)S(1)} %pad_add_fusion.table, f32[64,128]{1,0:T(8,128)S(1)} %bitcast.28, bf16[16,64,1024]{2,1,0:T(8,128)(2,1)S(1)} %bitcast.25, bf16[2,16,2048]{2,1,0:T(8,128)(2,1)S(1)} %get-tuple-element.47.refs_2_, ...), custom_call_target="tpu_custom_call" | custom-call | bytes 2097152 | tf_op jit(solution)/shard_map/pallas_call | solution.py:504
  72.7 0.6 collective-permute-done.13.refs_5_
  73.4 1.6 %shard_map.100 = bf16[16,16,1024]{2,1,0:T(8,128)(2,1)} custom-call(s32[17]{0:T(128)S(1)} %pad_add_fusion.table, bf16[16,2048]{1,0:T(8,128)(2,1)S(1)} %get-tuple-element.54.refs_0_, bf16[16,2048]{1,0:T(8,128)(2,1)S(1)} %get-tuple-element.56.refs_1_, bf16[16,2048]{1,0:T(8,128)(2,1)S(1)} %collective-permute-done.10.refs_2_, ...), custom_call_target="tpu_custom_call" | custom-call | bytes 1048576 | tf_op jit(solution)/shard_map/pallas_call | solution.py:514
  (19 shorter events, 0.1 us)
Async XLA Ops:
  0.6 0.9 %copy-start = (bf16[3,8,16,16]{3,2,1,0:T(8,128)(2,1)S(1)}, bf16[3,8,16,16]{3,2,1,0:T(8,128)(2,1)}, u32[]{:S(2)}) copy-start(bf16[3,8,16,16]{3,2,1,0:T(8,128)(2,1)} %param.11) | copy-start | bytes 36868
  2.5 9.6 %copy-start.2 = (bf16[8,26,4096]{2,0,1:T(8,128)(2,1)S(1)}, bf16[8,26,4096]{2,0,1:T(8,128)(2,1)}, u32[]{:S(2)}) copy-start(bf16[8,26,4096]{2,0,1:T(8,128)(2,1)} %param.10) | copy-start | bytes 5111812
  2.7 10.5 %collective-permute-start.2 = (bf16[64,512]{1,0:T(8,128)(2,1)S(1)}, bf16[64,512]{1,0:T(8,128)(2,1)S(1)}, u32[]{:S(2)}, u32[]{:S(2)}) collective-permute-start(bf16[64,512]{1,0:T(8,128)(2,1)S(1)} %fusion.3.refs_0_.refs_5_), channel_id=1, source_target_pairs={{0,3},{1,0},{2,1},{3,2},{4,7},{5,4},{6,5},{7,6},{8,11},{9,8},{10,9... | collective-permute-start | bytes 196616 | tf_op jit(solution)/shard_map/ppermute | solution.py:369
  5.2 8.1 %collective-permute-start.1 = (bf16[64,512]{1,0:T(8,128)(2,1)S(1)}, bf16[64,512]{1,0:T(8,128)(2,1)S(1)}, u32[]{:S(2)}, u32[]{:S(2)}) collective-permute-start(bf16[64,512]{1,0:T(8,128)(2,1)S(1)} %fusion.3.refs_0_.refs_5_), channel_id=1, source_target_pairs={{0,2},{1,3},{2,0},{3,1},{4,6},{5,7},{6,4},{7,5},{8,10},{9,11},{10,... | collective-permute-start | bytes 196616 | tf_op jit(solution)/shard_map/ppermute | solution.py:369
  5.8 7.4 %collective-permute-start = (bf16[64,512]{1,0:T(8,128)(2,1)S(1)}, bf16[64,512]{1,0:T(8,128)(2,1)S(1)}, u32[]{:S(2)}, u32[]{:S(2)}) collective-permute-start(bf16[64,512]{1,0:T(8,128)(2,1)S(1)} %fusion.3.refs_0_.refs_5_), channel_id=1, source_target_pairs={{0,1},{1,2},{2,3},{3,0},{4,5},{5,6},{6,7},{7,4},{8,9},{9,10},{10,1... | collective-permute-start | bytes 196616 | tf_op jit(solution)/shard_map/ppermute | solution.py:369
  7.3 5.8 %collective-permute-start.3 = (s32[2]{0:T(128)S(1)}, s32[2]{0:T(128)S(1)}, u32[]{:S(2)}, u32[]{:S(2)}) collective-permute-start(s32[2]{0:T(128)S(1)} %get-tuple-element.65), channel_id=1, source_target_pairs={{0,0},{1,17},{2,6},{3,23},{4,4},{5,21},{6,2},{7,19},{8,8},{9,25},{... | collective-permute-start | bytes 32 | tf_op jit(solution)/shard_map/ppermute | solution.py:356
  8.0 5.2 %collective-permute-start.4 = (s32[2]{0:T(128)S(1)}, s32[2]{0:T(128)S(1)}, u32[]{:S(2)}, u32[]{:S(2)}) collective-permute-start(s32[2]{0:T(128)S(1)} %get-tuple-element.66), channel_id=1, source_target_pairs={{0,8},{1,25},{2,14},{3,31},{4,12},{5,29},{6,10},{7,27},{8,0},{9,17... | collective-permute-start | bytes 32 | tf_op jit(solution)/shard_map/ppermute | solution.py:356
  13.4 2.3 %copy-start.1 = (bf16[8,2,64,1024]{3,2,1,0:T(8,128)(2,1)S(1)}, bf16[8,2,64,1024]{3,2,1,0:T(8,128)(2,1)}, u32[]{:S(2)}) copy-start(bf16[8,2,64,1024]{3,2,1,0:T(8,128)(2,1)} %param.7) | copy-start | bytes 6291460
  14.5 11.7 %collective-permute-start.5 = (bf16[2,64,768]{2,1,0:T(8,128)(2,1)S(1)}, bf16[2,64,768]{2,1,0:T(8,128)(2,1)S(1)}, u32[]{:S(2)}, u32[]{:S(2)}) collective-permute-start(bf16[2,64,768]{2,1,0:T(8,128)(2,1)S(1)} %get-tuple-element.35), channel_id=1, source_target_pairs={{0,0},{1,17},{2,6},{3,23},{4,4},{5,21},{6,2},{7,19},{8,8},{9,25},{... | collective-permute-start | bytes 589832 | tf_op jit(solution)/shard_map/ppermute | solution.py:396
  15.2 11.1 %collective-permute-start.6 = (bf16[2,64,768]{2,1,0:T(8,128)(2,1)S(1)}, bf16[2,64,768]{2,1,0:T(8,128)(2,1)S(1)}, u32[]{:S(2)}, u32[]{:S(2)}) collective-permute-start(bf16[2,64,768]{2,1,0:T(8,128)(2,1)S(1)} %get-tuple-element.36), channel_id=1, source_target_pairs={{0,8},{1,25},{2,14},{3,31},{4,12},{5,29},{6,10},{7,27},{8,0},{9,17... | collective-permute-start | bytes 589832 | tf_op jit(solution)/shard_map/ppermute | solution.py:396
  49.0 10.8 %collective-permute-start.7 = (bf16[2,16,2048]{2,1,0:T(8,128)(2,1)S(1)}, bf16[2,16,2048]{2,1,0:T(8,128)(2,1)S(1)}, u32[]{:S(2)}, u32[]{:S(2)}) collective-permute-start(bf16[2,16,2048]{2,1,0:T(8,128)(2,1)S(1)} %get-tuple-element.44), channel_id=1, source_target_pairs={{0,1},{1,2},{2,3},{3,0},{4,5},{5,6},{6,7},{7,4},{8,9},{9,10},{10,1... | collective-permute-start | bytes 393224 | tf_op jit(solution)/shard_map/ppermute | solution.py:369
  49.1 12.1 %collective-permute-start.8 = (bf16[2,16,2048]{2,1,0:T(8,128)(2,1)S(1)}, bf16[2,16,2048]{2,1,0:T(8,128)(2,1)S(1)}, u32[]{:S(2)}, u32[]{:S(2)}) collective-permute-start(bf16[2,16,2048]{2,1,0:T(8,128)(2,1)S(1)} %get-tuple-element.45), channel_id=1, source_target_pairs={{0,2},{1,3},{2,0},{3,1},{4,6},{5,7},{6,4},{7,5},{8,10},{9,11},{10,... | collective-permute-start | bytes 393224 | tf_op jit(solution)/shard_map/ppermute | solution.py:369
  49.6 11.6 %collective-permute-start.9 = (bf16[2,16,2048]{2,1,0:T(8,128)(2,1)S(1)}, bf16[2,16,2048]{2,1,0:T(8,128)(2,1)S(1)}, u32[]{:S(2)}, u32[]{:S(2)}) collective-permute-start(bf16[2,16,2048]{2,1,0:T(8,128)(2,1)S(1)} %get-tuple-element.46), channel_id=1, source_target_pairs={{0,3},{1,0},{2,1},{3,2},{4,7},{5,4},{6,5},{7,6},{8,11},{9,8},{10,9... | collective-permute-start | bytes 393224 | tf_op jit(solution)/shard_map/ppermute | solution.py:369
  58.1 10.9 %collective-permute-start.10 = (bf16[16,2048]{1,0:T(8,128)(2,1)S(1)}, bf16[16,2048]{1,0:T(8,128)(2,1)S(1)}, u32[]{:S(2)}, u32[]{:S(2)}) collective-permute-start(bf16[16,2048]{1,0:T(8,128)(2,1)S(1)} %get-tuple-element.57), channel_id=1, source_target_pairs={{0,1},{1,2},{2,3},{3,0},{4,5},{5,6},{6,7},{7,4},{8,9},{9,10},{10,1... | collective-permute-start | bytes 196616 | tf_op jit(solution)/shard_map/ppermute | solution.py:369
  58.2 14.6 %collective-permute-start.12 = (bf16[16,2048]{1,0:T(8,128)(2,1)S(1)}, bf16[16,2048]{1,0:T(8,128)(2,1)S(1)}, u32[]{:S(2)}, u32[]{:S(2)}) collective-permute-start(bf16[16,2048]{1,0:T(8,128)(2,1)S(1)} %get-tuple-element.59), channel_id=1, source_target_pairs={{0,2},{1,3},{2,0},{3,1},{4,6},{5,7},{6,4},{7,5},{8,10},{9,11},{10,... | collective-permute-start | bytes 196616 | tf_op jit(solution)/shard_map/ppermute | solution.py:369
  59.8 13.0 %collective-permute-start.14 = (bf16[16,2048]{1,0:T(8,128)(2,1)S(1)}, bf16[16,2048]{1,0:T(8,128)(2,1)S(1)}, u32[]{:S(2)}, u32[]{:S(2)}) collective-permute-start(bf16[16,2048]{1,0:T(8,128)(2,1)S(1)} %get-tuple-element.61), channel_id=1, source_target_pairs={{0,3},{1,0},{2,1},{3,2},{4,7},{5,4},{6,5},{7,6},{8,11},{9,8},{10,9... | collective-permute-start | bytes 196616 | tf_op jit(solution)/shard_map/ppermute | solution.py:369
  68.3 4.4 %collective-permute-start.11 = (bf16[16,2048]{1,0:T(8,128)(2,1)S(1)}, bf16[16,2048]{1,0:T(8,128)(2,1)S(1)}, u32[]{:S(2)}, u32[]{:S(2)}) collective-permute-start(bf16[16,2048]{1,0:T(8,128)(2,1)S(1)} %get-tuple-element.58), channel_id=1, source_target_pairs={{0,1},{1,2},{2,3},{3,0},{4,5},{5,6},{6,7},{7,4},{8,9},{9,10},{10,1... | collective-permute-start | bytes 196616 | tf_op jit(solution)/shard_map/ppermute | solution.py:369
  68.4 5.0 %collective-permute-start.13 = (bf16[16,2048]{1,0:T(8,128)(2,1)S(1)}, bf16[16,2048]{1,0:T(8,128)(2,1)S(1)}, u32[]{:S(2)}, u32[]{:S(2)}) collective-permute-start(bf16[16,2048]{1,0:T(8,128)(2,1)S(1)} %get-tuple-element.60), channel_id=1, source_target_pairs={{0,2},{1,3},{2,0},{3,1},{4,6},{5,7},{6,4},{7,5},{8,10},{9,11},{10,... | collective-permute-start | bytes 196616 | tf_op jit(solution)/shard_map/ppermute | solution.py:369
  69.0 4.4 %collective-permute-start.15 = (bf16[16,2048]{1,0:T(8,128)(2,1)S(1)}, bf16[16,2048]{1,0:T(8,128)(2,1)S(1)}, u32[]{:S(2)}, u32[]{:S(2)}) collective-permute-start(bf16[16,2048]{1,0:T(8,128)(2,1)S(1)} %get-tuple-element.62), channel_id=1, source_target_pairs={{0,3},{1,0},{2,1},{3,2},{4,7},{5,4},{6,5},{7,6},{8,11},{9,8},{10,9... | collective-permute-start | bytes 196616 | tf_op jit(solution)/shard_map/ppermute | solution.py:369

commit v3 on v2

v3 whole, which is shorter than its diff:
```python
import functools

import jax
import jax.numpy as jnp
from jax import lax
from jax.experimental import pallas as pl
from jax.experimental.pallas import tpu as pltpu
from jax.sharding import PartitionSpec as P

BF = jnp.bfloat16
F32 = jnp.float32
SUMS = 5
VMEM_LIMIT = 26 * 1024 * 1024


def low_half(shape):
    return lax.broadcasted_iota(jnp.int32, shape, len(shape) - 1) < shape[-1] // 2


def swap(tile):
    return pltpu.roll(tile, tile.shape[-1] // 2, 1)


def two_in_lanes(first, second):
    low = low_half(first.shape)
    return jnp.where(low, first, swap(second)), jnp.where(low, swap(first), second)


def fill_left(lhs, left_refs, wide):
    env_width = left_refs[0].shape[0]
    lane = 2 * wide
    depth = -(-env_width // 16) * 16
    lhs[...] = jnp.zeros_like(lhs)
    low = low_half((env_width, lane))
    for pair in range(wide // 2):
        for b, ref in enumerate(left_refs):
            tile = ref[:, pair * lane : (pair + 1) * lane].astype(F32)
            base = 2 * pair * depth
            cols = slice(b * lane, (b + 1) * lane)
            lhs[base : base + env_width, cols] = jnp.where(low, tile, 0.0).astype(BF)
            lhs[base + depth : base + depth + env_width, cols] = jnp.where(low, 0.0, tile).astype(BF)


def put_source(rhs, s, tile):
    rows, lane = tile.shape
    low = low_half(tile.shape)
    kept = (jnp.where(low, tile, 0.0).astype(BF), jnp.where(low, 0.0, tile).astype(BF))
    for b in range(2):
        for copy in range(2):
            base = (2 * b + copy) * rows
            rhs[base : base + rows, s * lane : (s + 1) * lane] = kept[b]


def contract_left(lhs, rhs, con, chunk=512):
    step = 256
    for n in range(rhs.shape[1] // step):
        cols = slice(n * step, (n + 1) * step)

        def one(i, carry):
            rows = pl.ds(pl.multiple_of(i * chunk, chunk), chunk)
            con[rows, cols] = jnp.dot(
                lhs[rows, :], rhs[:, cols], preferred_element_type=F32
            ).astype(BF)
            return carry

        lax.fori_loop(0, lhs.shape[0] // chunk, one, 0, unroll=True)


def mix(amat, con, mixed, phys, lane):
    depth = amat.shape[1] // phys
    groups = amat.shape[0] // phys
    pairs = con.shape[0] // depth // 2

    def one(pair, carry):
        halves = []
        for parity in range(2):
            rows = pl.ds(pl.multiple_of((2 * pair + parity) * depth, depth), depth)
            halves.append(
                jnp.concatenate(
                    [con[rows, s * lane : (s + 1) * lane] for s in range(phys)], axis=0
                )
            )
        out = jnp.dot(
            amat[...], jnp.concatenate(halves, axis=1), preferred_element_type=F32
        ).astype(BF)
        for parity in range(2):
            rows = pl.ds(pl.multiple_of((2 * pair + parity) * phys, phys), phys)
            for g in range(groups):
                mixed[rows, g * lane : (g + 1) * lane] = out[
                    g * phys : (g + 1) * phys, parity * lane : (parity + 1) * lane
                ]
        return carry

    lax.fori_loop(0, pairs, one, 0, unroll=True)


def fill_right(rmat, right_tiles, lane):
    for b, get in enumerate(right_tiles):
        wide = lane // 2
        rows = slice(b * wide, (b + 1) * wide)
        low = low_half((wide, lane))
        for pair in range(rmat.shape[1] // (2 * lane)):
            tile = get(pair).astype(F32)
            turned = swap(tile)
            if b == 0:
                first, second = jnp.where(low, tile, 0.0), jnp.where(low, turned, 0.0)
            else:
                first, second = jnp.where(low, 0.0, turned), jnp.where(low, 0.0, tile)
            rmat[rows, 2 * pair * lane : (2 * pair + 1) * lane] = first.astype(BF)
            rmat[rows, (2 * pair + 1) * lane : (2 * pair + 2) * lane] = second.astype(BF)


def contract_right(mixed, rmat, acc, chunk=256):
    for i in range(mixed.shape[0] // chunk):
        rows = slice(i * chunk, (i + 1) * chunk)
        acc[rows, :] = lax.dot_general(
            mixed[rows, :], rmat[...], (((1,), (1,)), ((), ())), preferred_element_type=F32
        )


def copy_operator(amat, parts):
    rows = amat.shape[0] // len(parts)
    for k, part in enumerate(parts):
        amat[k * rows : (k + 1) * rows, :] = part[:rows, :]


def left_kernel(per_left, wide, phys, own, left_env, vec, *refs):
    parts = refs[:-6]
    mixes, boths, lefts, amat, rhs, con = refs[-6:]
    lane = 2 * wide
    copy_operator(amat, parts)

    def one(pi, carry):
        first, second = own[2 * pi], own[2 * pi + 1]
        both, lhs = boths.at[pi], lefts.at[pi]
        fill_left(lhs, [left_env.at[lax.div(n, per_left)] for n in (first, second)], wide)
        for pair in range(phys // 2):
            cols = slice(pair * lane, (pair + 1) * lane)
            tiles = two_in_lanes(vec[first, :, cols].astype(F32), vec[second, :, cols].astype(F32))
            for half, tile in enumerate(tiles):
                s = 2 * pair + half
                both[:, s * lane : (s + 1) * lane] = tile.astype(BF)
                put_source(rhs, s, tile)
        contract_left(lhs, rhs, con)
        mix(amat, con, mixes.at[pi], phys, lane)
        return carry

    lax.fori_loop(0, boths.shape[0], one, 0)


def quarter_of(place, k, rows):
    return pl.multiple_of(lax.bitwise_xor(place[0], k) * rows, rows)


def right_kernel(terms, kinds, wide, phys, place, mixes, boths, *refs):
    pairs = len(kinds)
    count = len({at for pair in kinds for at, _ in pair})
    rights, refs = refs[:count], refs[count:]
    images, line, rmats = refs[:3]
    outs, accs = refs[3 : 3 + terms], refs[3 + terms]
    lane = 2 * wide
    slab = wide // terms
    at = lax.broadcasted_iota(jnp.int32, (1, lane), 1)
    row = jnp.zeros((1, lane), F32)
    for pi in range(pairs):
        both, image = boths.at[pi], images.at[pi]
        fill_right(rmats.at[pi], tiles_of(rights, kinds[pi], lane), lane)
        acc = accs.at[pi]
        contract_right(mixes.at[pi], rmats.at[pi], acc)
        norm = jnp.zeros((wide, lane), F32)
        corr = jnp.zeros((wide, lane), F32)
        for y in range(phys):
            cols = slice(y * lane, (y + 1) * lane)
            tile = acc[pl.ds(y, wide, stride=phys), :].astype(BF)
            image[:, cols] = tile
            value = tile.astype(F32)
            vec = both[:, cols].astype(F32)
            norm += vec * vec
            corr += vec * value
        norm = jnp.sum(norm, keepdims=True)
        corr = jnp.sum(corr, keepdims=True)
        ratio = jnp.where(norm > 0, corr / jnp.where(norm > 0, norm, 1.0), 0.0)
        square = jnp.zeros((wide, lane), F32)
        cross = jnp.zeros((wide, lane), F32)
        for y in range(phys):
            cols = slice(y * lane, (y + 1) * lane)
            vec = both[:, cols].astype(F32)
            rest = image[:, cols].astype(F32) - ratio * vec
            square += rest * rest
            cross += rest * vec
        square = jnp.sum(square, keepdims=True)
        cross = jnp.sum(cross, keepdims=True)
        for i, value in enumerate((norm, corr, ratio, square, cross)):
            row = jnp.where(at == SUMS * pi + i, value, row)
        for k, out in enumerate(outs):
            out[pi] = image[pl.ds(quarter_of(place, k, slab), slab), :]
    line[...] = jnp.broadcast_to(row[None], line.shape)


def tiles_of(rights, kind, lane):
    return [
        lambda pair, ref=rights[array], at=at: ref[at, :, pair * lane : (pair + 1) * lane]
        for array, at in kind
    ]


def scalars(everyone, pairs):
    def all_of(i):
        return [everyone[:, SUMS * pi + i : SUMS * pi + i + 1] for pi in range(pairs)]

    def total(columns):
        return jnp.sum(functools.reduce(jnp.add, columns), keepdims=True)

    norm_sq = total(all_of(0))
    ratio = total(all_of(1)) / norm_sq
    rests = []
    for norm, own, square, cross in zip(*(all_of(i) for i in (0, 2, 3, 4))):
        off = own - ratio
        rests.append(square + 2 * off * cross + off * off * norm)
    return ratio, jnp.sqrt(norm_sq / (total(rests) + 1e-06))


def second_kernel(terms, pi, wide, phys, place, everyone, boths, images, lefts, amat, rmats, *refs):
    carried = refs[:terms] if pi == 0 else ()
    outs = refs[len(carried) : len(carried) + terms]
    rhs, con, mixed, acc = refs[len(carried) + terms :]
    lane = 2 * wide
    slab = wide // terms
    ratio, scale = scalars(everyone, boths.shape[0])
    for s in range(phys):
        cols = slice(s * lane, (s + 1) * lane)
        rest = images[pi, :, cols].astype(F32) - ratio * boths[pi, :, cols].astype(F32)
        put_source(rhs, s, (rest * scale).astype(BF).astype(F32))
    contract_left(lefts.at[pi], rhs, con)
    mix(amat, con, mixed, phys, lane)
    contract_right(mixed, rmats.at[pi], acc)
    for k, out in enumerate(outs):
        last = out.shape[0] - 1
        if carried:
            out[:last] = carried[k][...]
        base = quarter_of(place, k, slab) * phys
        for y in range(phys):
            out[last, :, y * lane : (y + 1) * lane] = acc[
                pl.ds(base + y, slab, stride=phys), :
            ].astype(BF)


def select_kernel(wide, blocks, names, asked, right_env, *refs):
    outs = refs[:-2]
    spread, rows_out = refs[-2:]
    env_width = right_env.shape[1]
    lane = 2 * wide
    half = wide // 2
    groups = outs[0].shape[2] // wide
    for i, (out, at) in enumerate(blocks):
        env = right_env.at[asked[i]]
        for z in range(half):
            tile = env[:, z * lane : (z + 1) * lane].astype(F32)
            for top in range(0, env_width, 8):
                part = tile[top : top + 8]
                base = top * half + z * 8
                spread[base : base + part.shape[0], :] = part

        def rows_of(g):
            name = names[g]
            return spread[pl.ds((name // 8) * (8 * half) + name % 8, half, stride=8), :]

        for pair in range(groups // 2):
            even, odd = two_in_lanes(rows_of(2 * pair), rows_of(2 * pair + 1))
            rows_out[pl.ds(0, half, stride=2), :] = even
            rows_out[pl.ds(1, half, stride=2), :] = odd
            outs[out][at, :, pair * lane : (pair + 1) * lane] = rows_out[...].astype(BF)


def place_kernel(terms, wide, phys, count, follows, table, *refs):
    if follows:
        ratio, scale = scalars(refs[0], count)
        vec, refs = refs[1], refs[2:]
        out, following = refs[-2:]
    else:
        out = refs[-1]
    lane = 2 * wide
    blocks, slab, _ = out.shape
    slots = blocks // terms
    me = table[blocks]
    for k in range(terms):
        source = lax.bitwise_xor(me, k)
        for pi in range(count):
            if follows:
                piece = refs[k].at[pi]
            elif pi == 0:
                piece = refs[k].at[count]
            else:
                piece = refs[terms * pi + k].at[0]
            first = table[source * slots + 2 * pi]
            second = table[source * slots + 2 * pi + 1]
            for pair in range(phys // 2):
                cols = slice(pair * lane, (pair + 1) * lane)
                both = two_in_lanes(
                    piece[:, 2 * pair * lane : (2 * pair + 1) * lane].astype(F32),
                    piece[:, (2 * pair + 1) * lane : (2 * pair + 2) * lane].astype(F32),
                )
                for where, value in zip((first, second), both):
                    out[where, :, cols] = value.astype(BF)
                    if follows:
                        rows = pl.ds(pl.multiple_of(me * slab, slab), slab)
                        rest = value - ratio * vec[where, rows, cols].astype(F32)
                        following[where, :, cols] = (rest * scale).astype(BF)


def call(kernel, tables, operands, out_shapes, scratch, flops, moved):
    specs = [
        pl.BlockSpec(memory_space=pltpu.SMEM if i < tables else pltpu.VMEM)
        for i in range(len(operands))
    ]
    return pl.pallas_call(
        kernel,
        out_shape=out_shapes,
        in_specs=specs,
        out_specs=[pl.BlockSpec(memory_space=pltpu.VMEM)] * len(out_shapes),
        scratch_shapes=scratch,
        compiler_params=pltpu.CompilerParams(vmem_limit_bytes=VMEM_LIMIT),
        cost_estimate=pl.CostEstimate(flops=flops, bytes_accessed=moved, transcendentals=0),
    )(*operands)


def body(vector, right_sector, left_env, right_env, term_ops, term_left, group_right):
    terms = lax.axis_size("term")
    secs = lax.axis_size("sec")
    per_device, per_left, wide, row_width = vector.shape
    phys = row_width // wide
    lane = 2 * wide
    blocks = per_device * per_left
    slots = blocks // terms
    pairs = slots // 2
    span = secs // terms
    each = blocks // secs
    env_width = left_env.shape[1]
    depth = -(-env_width // 16) * 16
    local = group_right.shape[0]
    groups = local * terms
    slab = wide // terms
    d = lax.axis_index("sec")
    me = lax.axis_index("term")
    both_axes = ("sec", "term")
    vec = vector.reshape(blocks, wide, row_width)

    lines = terms // 2

    def flip(t, a):
        return (2 * a + (t + a) % 2) * lines + t // 2

    flat = right_sector.reshape(blocks)
    dest = flat // per_device
    before = jnp.arange(blocks)[None, :] < jnp.arange(blocks)[:, None]
    rank = jnp.sum((dest[None, :] == dest[:, None]) & before, axis=1)
    flips = dest ^ d
    a = flips // lines // 2
    t = flips % lines * 2 + (flips // lines + a) % 2
    place = t * slots + a * each + rank
    hit = place[None, :] == jnp.arange(blocks)[:, None]
    order = jnp.sum(jnp.where(hit, jnp.arange(blocks)[None, :], 0), axis=1)
    by_place = jnp.sum(jnp.where(hit, (flat % per_device)[None, :], 0), axis=1)
    own = lax.dynamic_slice(order, (me * slots,), (slots,)).astype(jnp.int32)
    wanted = lax.dynamic_slice(by_place, (me * slots,), (slots,)).astype(jnp.int32)
    table = jnp.concatenate([order.astype(jnp.int32), me.reshape(1)])

    swaps = [
        [(e * terms + t, (e ^ flip(t, a)) * terms + t) for e in range(secs) for t in range(terms)]
        for a in range(span)
    ]
    asked = [
        lax.ppermute(wanted[a * each : (a + 1) * each], both_axes, swaps[a]) for a in range(span)
    ]

    onehot = (term_left[:, :, None] == jnp.arange(depth)).astype(BF)
    operator = jnp.einsum(
        "gtys,gtw->gysw", term_ops, onehot, preferred_element_type=F32
    ).reshape(local * phys, phys * depth)
    names = jnp.pad(
        group_right.astype(F32)[None, :], ((0, 15), (0, phys * depth - local))
    )
    packed = jnp.concatenate([operator, names], axis=0).astype(BF)

    def shift(value, k):
        return lax.ppermute(value, "term", [(t, t ^ k) for t in range(terms)])

    parts = [packed] + [shift(packed, k) for k in range(1, terms)]
    known = jnp.concatenate([p[local * phys, :local] for p in parts]).astype(jnp.int32)
    asked = jnp.concatenate(asked)

    right_shape = jax.ShapeDtypeStruct((each, wide, groups * wide), BF)
    chosen = call(
        functools.partial(select_kernel, wide, [(i // each, i % each) for i in range(slots)]),
        2,
        (known, asked, right_env),
        [right_shape] * span,
        [
            pltpu.VMEM((-(-env_width // 8) * 8 * (wide // 2), lane), F32),
            pltpu.VMEM((wide, lane), F32),
        ],
        0,
        slots * env_width * wide * wide * 2,
    )
    rights = [lax.ppermute(chosen[a], both_axes, swaps[a]) for a in range(span)]
    left_env, _ = lax.optimization_barrier((left_env, chosen))

    rows = wide * depth
    left_flops = 2 * rows * 4 * wide * phys * lane
    mix_flops = 2 * groups * phys * phys * depth * wide * lane
    right_flops = 2 * wide * phys * groups * lane * lane

    def stacked(*shape):
        return jax.ShapeDtypeStruct(shape, BF)

    mixed_shape = (wide * phys, groups * lane)
    rhs_scratch = pltpu.VMEM((4 * wide, phys * lane), BF)
    con_scratch = pltpu.VMEM((rows, phys * lane), BF)
    acc_scratch = pltpu.VMEM((wide * phys, lane), F32)
    mixes, boths, lefts, amat = call(
        functools.partial(left_kernel, per_left, wide, phys),
        1,
        (own, left_env, vec, *parts),
        [
            stacked(pairs, *mixed_shape),
            stacked(pairs, wide, phys * lane),
            stacked(pairs, rows, 4 * wide),
            stacked(groups * phys, phys * depth),
        ],
        [rhs_scratch, con_scratch],
        pairs * (left_flops + mix_flops),
        pairs * wide * phys * groups * lane * 2,
    )

    where = me.reshape(1).astype(jnp.int32)
    kinds = [[((2 * pi + b) // each, (2 * pi + b) % each) for b in range(2)] for pi in range(pairs)]
    images, line, rmats, *pieces = call(
        functools.partial(right_kernel, terms, kinds, wide, phys),
        1,
        (where, mixes, boths, *rights),
        [
            stacked(pairs, wide, phys * lane),
            jax.ShapeDtypeStruct((secs * terms, 1, lane), F32),
            stacked(pairs, lane, groups * lane),
        ]
        + [stacked(pairs, slab, phys * lane)] * terms,
        [pltpu.VMEM((pairs, wide * phys, lane), F32)],
        pairs * right_flops,
        pairs * wide * phys * groups * lane * 2,
    )

    everyone = lax.all_to_all(line, both_axes, 0, 0, tiled=True).reshape(-1, lane)

    second_pieces = []
    for pi in range(pairs):
        carried = pieces if pi == 0 else []
        outs = call(
            functools.partial(second_kernel, terms, pi, wide, phys),
            1,
            (where, everyone, boths, images, lefts, amat, rmats, *carried),
            [stacked(pairs + 1 if carried else 1, slab, phys * lane)] * terms,
            [rhs_scratch, con_scratch, pltpu.VMEM(mixed_shape, BF), acc_scratch],
            left_flops + mix_flops + right_flops,
            4 * wide * phys * lane * 2,
        )
        second_pieces.append([outs[0]] + [shift(outs[k], k) for k in range(1, terms)])

    out_shape = jax.ShapeDtypeStruct((blocks, slab, row_width), BF)
    first_image, next_rows = call(
        functools.partial(place_kernel, terms, wide, phys, pairs, True),
        1,
        (table, everyone, vec, *second_pieces[0]),
        [out_shape] * 2,
        [],
        0,
        blocks * slab * row_width * 8,
    )
    (second_image,) = call(
        functools.partial(place_kernel, terms, wide, phys, pairs, False),
        1,
        (table, *(piece for one_pair in second_pieces for piece in one_pair)),
        [out_shape],
        [],
        0,
        blocks * slab * row_width * 4,
    )
    shape = (per_device, per_left, slab, row_width)
    return (first_image.reshape(shape), next_rows.reshape(shape), second_image.reshape(shape))


def solution(mesh):
    in_specs = (
        P("sec", None, None, None),
        P("sec", None),
        P("sec", None, None),
        P("sec", None, None),
        P("term", None, None, None),
        P("term", None),
        P("term"),
    )
    out_specs = (
        P("sec", None, "term", None),
        P("sec", None, "term", None),
        P("sec", None, "term", None),
    )
    return jax.shard_map(body, mesh=mesh, in_specs=in_specs, out_specs=out_specs, check_vma=False)
```

time: 75.4 us -> 69.3 us (0.919)
  Pallas kernels: 32.6 us -> 28.2 us
  blocking collectives: 20 us -> 15.8 us
  starting transfers between devices: 13.7 us -> 15.1 us
  waiting for transfers between devices: 0.69 us -> 1.9 us
    pallas_call x7, Pallas kernels: 32.6 us -> 28.2 us  [call(): pl.pallas_call(kernel, out_shape=out_shapes, in_specs=specs, out_specs=[p...]
    all_to_all x1, blocking collectives: 20 us -> 15.8 us  [body(): lax.all_to_all(line, both_axes, 0, 0, tiled=True).reshape(-1, lane)]
    ppermute x12 -> x9, starting transfers between devices: 10.2 us -> 6.98 us  [shift(): return lax.ppermute(value, 'term', [(t, t ^ k) for t in range(terms)])]
    ppermute x2, starting transfers between devices: 1.19 us -> 3.56 us  [body(): rights = [lax.ppermute(chosen[a], both_axes, swaps[a]) for a in range(span)]]
    ppermute x2, starting transfers between devices: 2.3 us -> 4.57 us  [body(): lax.ppermute(wanted[a * each:(a + 1) * each], both_axes, swaps[a])]
    ppermute x12 -> x9, waiting for transfers between devices: 0.67 us -> 1.89 us  [shift(): return lax.ppermute(value, 'term', [(t, t ^ k) for t in range(terms)])]
    optimization_barrier x0 -> x1, local copies, waits for them, and re-layouts: none -> 0.97 us  [body(): left_env, _ = lax.optimization_barrier((left_env, chosen))]
    unnamed x9 -> x8, local copies, waits for them, and re-layouts: 4.39 us -> 3.52 us
  transfers between devices with their start and end apart: 16 -> 13, of which waited for: 1 -> 2; matrix products, arithmetic and copies ran while one was open for 7% -> 7% of each run, Pallas kernels for 36% -> 25%
where the time goes in v3:
time: 69.3 us; the launch traced here: 69.1 us
  Pallas kernels  28.2 us (41%)
  blocking collectives  15.8 us (23%)
  starting transfers between devices  15.1 us (22%)
  local copies, waits for them, and re-layouts  5 us (7%)
  waiting for transfers between devices  1.9 us (3%)
  other arithmetic  1.27 us (2%)
  matrix products  0.98 us (1%)
  between operations  0.82 us (1%)
    pallas_call x7, Pallas kernels, call(): pl.pallas_call(kernel, out_shape=out_shapes, in_specs=specs, out_specs=[p...  28.2 us
    all_to_all x1, blocking collectives, body(): lax.all_to_all(line, both_axes, 0, 0, tiled=True).reshape(-1, lane)  15.8 us
    ppermute x9, starting transfers between devices, shift(): return lax.ppermute(value, 'term', [(t, t ^ k) for t in range(terms)])  6.98 us
    ppermute x2, starting transfers between devices, body(): lax.ppermute(wanted[a * each:(a + 1) * each], both_axes, swaps[a])  4.57 us
    ppermute x2, starting transfers between devices, body(): rights = [lax.ppermute(chosen[a], both_axes, swaps[a]) for a in range(span)]  3.56 us
    unnamed x8, local copies, waits for them, and re-layouts  3.52 us
    ppermute x9, waiting for transfers between devices, shift(): return lax.ppermute(value, 'term', [(t, t ^ k) for t in range(terms)])  1.89 us
  transfers between devices with their start and end apart: 13, of which 2 were waited for; matrix products, arithmetic and copies ran while one was open for 7% of the time, Pallas kernels for 25%

profile of v3, /device:TPU:0, one launch (start us, length us, event | category | flops | bytes accessed | tf_op | source)
XLA Modules:
  0.0 69.1 jit_solution(15063415347727576773)
XLA Ops:
  0.6 0.0 copy-start
  0.6 0.7 %convert_convert_fusion = (bf16[3]{0:T(256)(128)(2,1)S(1)}, bf16[1,3]{1,0:T(2,128)(2,1)S(1)}) fusion(s32[3]{0:T(128)} %param.13), kind=kLoop, calls=%fused_computation.41 | loop fusion | flops 6 | bytes 24 | tf_op jit(solution)/shard_map/squeeze | solution.py:389
  1.3 0.2 copy-done
  1.5 1.0 %fusion = bf16[3,16,16,32]{3,2,1,0:T(8,128)(2,1)S(1)} fusion(bf16[3,8,16,16]{3,2,1,0:T(8,128)(2,1)S(1)} %copy-done, s32[3,8]{1,0:T(4,128)} %param.12), kind=kOutput, calls=%fused_computation.1 | convolution fusion | flops 418560 | bytes 61536 | tf_op jit(solution)/shard_map/gtys,gtw->gysw/dot_general | solution.py:377
  2.5 0.2 reshape.184
  2.7 2.4 %collective-permute-start.2 = (bf16[64,512]{1,0:T(8,128)(2,1)S(1)}, bf16[64,512]{1,0:T(8,128)(2,1)S(1)}, u32[]{:S(2)}, u32[]{:S(2)}) collective-permute-start(bf16[64,512]{1,0:T(8,128)(2,1)S(1)} %fusion.3.refs_0_), channel_id=1, source_target_pairs={{0,3},{1,2},{2,1},{3,0},{4,7},{5,6},{6,5},{7,4},{8,11},{9,10},{10,... | collective-permute-start | bytes 196616 | tf_op jit(solution)/shard_map/ppermute | solution.py:386
  5.2 0.6 collective-permute-start.1
  5.8 0.0 collective-permute-start
  5.9 0.8 %copy.24 = s32[8,2]{1,0:T(8,128)S(1)} copy(s32[8,2]{0,1:T(2,128)} %param.8) | data formatting | bytes 128 | tf_op args[1]
  6.6 0.1 reshape.182
  6.7 0.2 convert_reduce_fusion
  6.9 0.1 select_reduce_fusion
  7.0 0.1 dynamic_slice.7
  7.1 0.1 fusion.12
  7.2 0.7 collective-permute-start.3
  7.9 3.9 %collective-permute-start.4 = (s32[2]{0:T(128)S(1)}, s32[2]{0:T(128)S(1)}, u32[]{:S(2)}, u32[]{:S(2)}) collective-permute-start(s32[2]{0:T(128)S(1)} %get-tuple-element.54), channel_id=1, source_target_pairs={{0,24},{1,17},{2,30},{3,23},{4,28},{5,21},{6,26},{7,19},{8,16},{9,... | collective-permute-start | bytes 32 | tf_op jit(solution)/shard_map/ppermute | solution.py:373
  11.8 0.1 dynamic_slice.6.own
  11.9 2.5 %copy.26.right_env = bf16[8,26,4096]{2,1,0:T(8,128)(2,1)S(1)} copy(bf16[8,26,4096]{2,0,1:T(8,128)(2,1)} %param.10) | data formatting | bytes 3407872 | tf_op args[3]
  14.4 0.0 collective-permute-done.3
  14.4 0.0 collective-permute-done.4
  14.4 0.1 pad_add_fusion.1.asked
  14.5 0.0 collective-permute-done.refs_1_
  14.5 0.1 maximum_convert_fusion.names
  14.6 1.1 %shard_map.94 = (bf16[2,64,768]{2,1,0:T(8,128)(2,1)S(1)}, bf16[2,64,768]{2,1,0:T(8,128)(2,1)S(1)}) custom-call(s32[12]{0:T(128)S(1)} %maximum_convert_fusion.names, s32[4]{0:T(128)S(1)} %pad_add_fusion.1.asked, bf16[8,26,4096]{2,1,0:T(8,128)(2,1)S(1)} %copy.26.right_env), custom_call_target="tpu_custom_call" | custom-call | bytes 851968 | tf_op jit(solution)/shard_map/pallas_call | solution.py:316
  15.8 0.0 copy-start.1
  15.8 0.8 %collective-permute-start.5 = (bf16[2,64,768]{2,1,0:T(8,128)(2,1)S(1)}, bf16[2,64,768]{2,1,0:T(8,128)(2,1)S(1)}, u32[]{:S(2)}, u32[]{:S(2)}) collective-permute-start(bf16[2,64,768]{2,1,0:T(8,128)(2,1)S(1)} %get-tuple-element.27), channel_id=1, source_target_pairs={{0,0},{1,9},{2,6},{3,15},{4,4},{5,13},{6,2},{7,11},{8,8},{9,1},{10... | collective-permute-start | bytes 589832 | tf_op jit(solution)/shard_map/ppermute | solution.py:405
  16.6 2.8 %collective-permute-start.6 = (bf16[2,64,768]{2,1,0:T(8,128)(2,1)S(1)}, bf16[2,64,768]{2,1,0:T(8,128)(2,1)S(1)}, u32[]{:S(2)}, u32[]{:S(2)}) collective-permute-start(bf16[2,64,768]{2,1,0:T(8,128)(2,1)S(1)} %get-tuple-element.28), channel_id=1, source_target_pairs={{0,24},{1,17},{2,30},{3,23},{4,28},{5,21},{6,26},{7,19},{8,16},{9,... | collective-permute-start | bytes 589832 | tf_op jit(solution)/shard_map/ppermute | solution.py:405
  19.3 1.0 %copy.27.left_env = bf16[8,26,4096]{2,1,0:T(8,128)(2,1)S(1)} copy(bf16[8,26,4096]{2,0,1:T(8,128)(2,1)S(1)} %copy-done.2) | data formatting | bytes 3407872 | tf_op jit(solution)/shard_map/optimization_barrier | solution.py:406
  20.3 8.9 %shard_map.95 = (bf16[2,1024,1536]{2,1,0:T(8,128)(2,1)S(1)}, bf16[2,64,2048]{2,1,0:T(8,128)(2,1)S(1)}, bf16[2,2048,256]{2,1,0:T(8,128)(2,1)S(1)}, bf16[192,512]{1,0:T(8,128)(2,1)S(1)}) custom-call(s32[4]{0:T(128)S(1)} %dynamic_slice.6.own, bf16[8,26,4096]{2,1,0:T(8,128)(2,1)S(1)} %copy.27.left_env, bf16[16,64,1024]{2,1,0:T(8,128)(2,1)S(1)} %bitcast.23, ...), custom_call_target="tpu_custom_call" | custom-call | flops 7516192768 | bytes 6291456 | tf_op jit(solution)/shard_map/pallas_call | solution.py:316
  29.3 0.0 collective-permute-done.6.refs_1_
  29.3 2.7 %shard_map.96 = (bf16[2,64,2048]{2,1,0:T(8,128)(2,1)S(1)}, f32[32,1,128]{2,1,0:T(1,128)S(1)}, bf16[2,128,1536]{2,1,0:T(8,128)(2,1)S(1)}, bf16[2,16,2048]{2,1,0:T...) custom-call(s32[1]{0:T(128)} %bitcast.place, ...), custom_call_target="tpu_custom_call" | custom-call | flops 805306368 | bytes 6291456 | tf_op jit(solution)/shard_map/pallas_call | solution.py:316
  32.0 15.8 %all_to_all.5 = f32[32,1,128]{2,1,0:T(1,128)S(1)} all-to-all(f32[32,1,128]{2,1,0:T(1,128)S(1)} %get-tuple-element.32), channel_id=1, replica_groups=mesh['sec'=8,'term'=4] {'sec','term'}, dimensions={0} | all-to-all | bytes 32768 | tf_op jit(solution)/shard_map/all_to_all | solution.py:452
  47.8 5.7 %shard_map.97 = (bf16[3,16,2048]{2,1,0:T(8,128)(2,1)S(1)}, bf16[3,16,2048]{2,1,0:T(8,128)(2,1)S(1)}, bf16[3,16,2048]{2,1,0:T(8,128)(2,1)S(1)}, bf16[3,16,2048]{2,1,0:T(8,128)(2,1)S(1)}) custom-call(s32[1]{0:T(128)} %bitcast.place, f32[32,128]{1,0:T(8,128)S(1)} %bitcast.25, bf16[2,64,2048]{2,1,0:T(8,128)(2,1)S(1)} %get-tuple-element.31.boths, ...), custom_call_target="tpu_custom_call" | custom-call | flops 4160749568 | bytes 1048576 | tf_op jit(solution)/shard_map/pallas_call | solution.py:316
  53.5 0.1 collective-permute-start.7
  53.6 0.6 collective-permute-start.8
  54.2 1.3 %collective-permute-start.9 = (bf16[3,16,2048]{2,1,0:T(8,128)(2,1)S(1)}, bf16[3,16,2048]{2,1,0:T(8,128)(2,1)S(1)}, u32[]{:S(2)}, u32[]{:S(2)}) collective-permute-start(bf16[3,16,2048]{2,1,0:T(8,128)(2,1)S(1)} %get-tuple-element.44), channel_id=1, source_target_pairs={{0,3},{1,2},{2,1},{3,0},{4,7},{5,6},{6,5},{7,4},{8,11},{9,10},{10,... | collective-permute-start | bytes 589832 | tf_op jit(solution)/shard_map/ppermute | solution.py:386
  55.5 5.7 %shard_map.99 = (bf16[1,16,2048]{2,1,0:T(8,128)(2,1)S(1)}, bf16[1,16,2048]{2,1,0:T(8,128)(2,1)S(1)}, bf16[1,16,2048]{2,1,0:T(8,128)(2,1)S(1)}, bf16[1,16,2048]{2,1,0:T(8,128)(2,1)S(1)}) custom-call(s32[1]{0:T(128)} %bitcast.place, f32[32,128]{1,0:T(8,128)S(1)} %bitcast.26, bf16[2,64,2048]{2,1,0:T(8,128)(2,1)S(1)} %get-tuple-element.31.boths, ...), custom_call_target="tpu_custom_call" | custom-call | flops 4160749568 | bytes 1048576 | tf_op jit(solution)/shard_map/pallas_call | solution.py:316
  61.2 0.4 collective-permute-start.10
  61.6 0.5 collective-permute-start.11
  62.1 0.0 collective-permute-done.7.refs_3_.refs_1_
  62.1 1.0 %collective-permute-start.12 = (bf16[1,16,2048]{2,1,0:T(8,128)(2,1)S(1)}, bf16[1,16,2048]{2,1,0:T(8,128)(2,1)S(1)}, u32[]{:S(2)}, u32[]{:S(2)}) collective-permute-start(bf16[1,16,2048]{2,1,0:T(8,128)(2,1)S(1)} %get-tuple-element.50), channel_id=1, source_target_pairs={{0,3},{1,2},{2,1},{3,0},{4,7},{5,6},{6,5},{7,4},{8,11},{9,10},{10,... | collective-permute-start | bytes 196616 | tf_op jit(solution)/shard_map/ppermute | solution.py:386
  63.1 0.1 pad_add_fusion.table
  63.2 1.5 %collective-permute-done.9.refs_5_.refs_3_ = bf16[3,16,2048]{2,1,0:T(8,128)(2,1)S(1)} collective-permute-done((bf16[3,16,2048]{2,1,0:T(8,128)(2,1)S(1)}, bf16[3,16,2048]{2,1,0:T(8,128)(2,1)S(1)}, u32[]{:S(2)}, u32[]{:S(2)}) %collective-permute-start.9) | collective-permute-done | bytes 196640 | tf_op jit(solution)/shard_map/ppermute | solution.py:386
  64.7 2.4 %shard_map.98 = (bf16[16,16,1024]{2,1,0:T(8,128)(2,1)}, bf16[16,16,1024]{2,1,0:T(8,128)(2,1)}) custom-call(s32[17]{0:T(128)S(1)} %pad_add_fusion.table, f32[32,128]{1,0:T(8,128)S(1)} %bitcast.27, bf16[16,64,1024]{2,1,0:T(8,128)(2,1)S(1)} %bitcast.24, bf16[3,16,2048]{2,1,0:T(8,128)(2,1)S(1)} %get-tuple-element.41.refs_2_.refs_0_, ...), custom_call_target="tpu_custom_call" | custom-call | bytes 2097152 | tf_op jit(solution)/shard_map/pallas_call | solution.py:316
  67.1 0.0 collective-permute-done.10.refs_5_
  67.1 0.0 collective-permute-done.11.refs_6_
  67.1 0.4 collective-permute-done.12.refs_7_
  67.5 1.6 %shard_map.100 = bf16[16,16,1024]{2,1,0:T(8,128)(2,1)} custom-call(s32[17]{0:T(128)S(1)} %pad_add_fusion.table, bf16[3,16,2048]{2,1,0:T(8,128)(2,1)S(1)} %get-tuple-element.41.refs_2_.refs_0_, bf16[3,16,2048]{2,1,0:T(8,128)(2,1)S(1)} %collective-permute-done.7.refs_3_.refs_1_, bf16[3,16,2048]{2,1,0:T(8,128)(2,1)S(1)} %collective-permute-done.8.refs_4_.refs_2_, ...), custom_call_target="tpu_custom_call" | custom-call | bytes 1048576 | tf_op jit(solution)/shard_map/pallas_call | solution.py:316
  (13 shorter events, 0.1 us)
Async XLA Ops:
  0.6 0.9 %copy-start = (bf16[3,8,16,16]{3,2,1,0:T(8,128)(2,1)S(1)}, bf16[3,8,16,16]{3,2,1,0:T(8,128)(2,1)}, u32[]{:S(2)}) copy-start(bf16[3,8,16,16]{3,2,1,0:T(8,128)(2,1)} %param.11) | copy-start | bytes 36868
  2.7 11.8 %collective-permute-start.2 = (bf16[64,512]{1,0:T(8,128)(2,1)S(1)}, bf16[64,512]{1,0:T(8,128)(2,1)S(1)}, u32[]{:S(2)}, u32[]{:S(2)}) collective-permute-start(bf16[64,512]{1,0:T(8,128)(2,1)S(1)} %fusion.3.refs_0_), channel_id=1, source_target_pairs={{0,3},{1,2},{2,1},{3,0},{4,7},{5,6},{6,5},{7,4},{8,11},{9,10},{10,... | collective-permute-start | bytes 196616 | tf_op jit(solution)/shard_map/ppermute | solution.py:386
  5.2 9.3 %collective-permute-start.1 = (bf16[64,512]{1,0:T(8,128)(2,1)S(1)}, bf16[64,512]{1,0:T(8,128)(2,1)S(1)}, u32[]{:S(2)}, u32[]{:S(2)}) collective-permute-start(bf16[64,512]{1,0:T(8,128)(2,1)S(1)} %fusion.3.refs_0_), channel_id=1, source_target_pairs={{0,2},{1,3},{2,0},{3,1},{4,6},{5,7},{6,4},{7,5},{8,10},{9,11},{10,... | collective-permute-start | bytes 196616 | tf_op jit(solution)/shard_map/ppermute | solution.py:386
  5.8 8.7 %collective-permute-start = (bf16[64,512]{1,0:T(8,128)(2,1)S(1)}, bf16[64,512]{1,0:T(8,128)(2,1)S(1)}, u32[]{:S(2)}, u32[]{:S(2)}) collective-permute-start(bf16[64,512]{1,0:T(8,128)(2,1)S(1)} %fusion.3.refs_0_), channel_id=1, source_target_pairs={{0,1},{1,0},{2,3},{3,2},{4,5},{5,4},{6,7},{7,6},{8,9},{9,8},{10,11... | collective-permute-start | bytes 196616 | tf_op jit(solution)/shard_map/ppermute | solution.py:386
  7.2 7.2 %collective-permute-start.3 = (s32[2]{0:T(128)S(1)}, s32[2]{0:T(128)S(1)}, u32[]{:S(2)}, u32[]{:S(2)}) collective-permute-start(s32[2]{0:T(128)S(1)} %get-tuple-element.53), channel_id=1, source_target_pairs={{0,0},{1,9},{2,6},{3,15},{4,4},{5,13},{6,2},{7,11},{8,8},{9,1},{10... | collective-permute-start | bytes 32 | tf_op jit(solution)/shard_map/ppermute | solution.py:373
  7.9 6.6 %collective-permute-start.4 = (s32[2]{0:T(128)S(1)}, s32[2]{0:T(128)S(1)}, u32[]{:S(2)}, u32[]{:S(2)}) collective-permute-start(s32[2]{0:T(128)S(1)} %get-tuple-element.54), channel_id=1, source_target_pairs={{0,24},{1,17},{2,30},{3,23},{4,28},{5,21},{6,26},{7,19},{8,16},{9,... | collective-permute-start | bytes 32 | tf_op jit(solution)/shard_map/ppermute | solution.py:373
  11.9 7.5 %copy-start.2 = (bf16[8,26,4096]{2,0,1:T(8,128)(2,1)S(1)}, bf16[8,26,4096]{2,0,1:T(8,128)(2,1)}, u32[]{:S(2)}) copy-start(bf16[8,26,4096]{2,0,1:T(8,128)(2,1)} %param.9) | copy-start | bytes 5111812
  15.8 4.6 %copy-start.1 = (bf16[8,2,64,1024]{3,2,1,0:T(8,128)(2,1)S(1)}, bf16[8,2,64,1024]{3,2,1,0:T(8,128)(2,1)}, u32[]{:S(2)}) copy-start(bf16[8,2,64,1024]{3,2,1,0:T(8,128)(2,1)} %param.7) | copy-start | bytes 6291460
  15.8 13.5 %collective-permute-start.5 = (bf16[2,64,768]{2,1,0:T(8,128)(2,1)S(1)}, bf16[2,64,768]{2,1,0:T(8,128)(2,1)S(1)}, u32[]{:S(2)}, u32[]{:S(2)}) collective-permute-start(bf16[2,64,768]{2,1,0:T(8,128)(2,1)S(1)} %get-tuple-element.27), channel_id=1, source_target_pairs={{0,0},{1,9},{2,6},{3,15},{4,4},{5,13},{6,2},{7,11},{8,8},{9,1},{10... | collective-permute-start | bytes 589832 | tf_op jit(solution)/shard_map/ppermute | solution.py:405
  16.6 12.7 %collective-permute-start.6 = (bf16[2,64,768]{2,1,0:T(8,128)(2,1)S(1)}, bf16[2,64,768]{2,1,0:T(8,128)(2,1)S(1)}, u32[]{:S(2)}, u32[]{:S(2)}) collective-permute-start(bf16[2,64,768]{2,1,0:T(8,128)(2,1)S(1)} %get-tuple-element.28), channel_id=1, source_target_pairs={{0,24},{1,17},{2,30},{3,23},{4,28},{5,21},{6,26},{7,19},{8,16},{9,... | collective-permute-start | bytes 589832 | tf_op jit(solution)/shard_map/ppermute | solution.py:405
  53.5 8.6 %collective-permute-start.7 = (bf16[3,16,2048]{2,1,0:T(8,128)(2,1)S(1)}, bf16[3,16,2048]{2,1,0:T(8,128)(2,1)S(1)}, u32[]{:S(2)}, u32[]{:S(2)}) collective-permute-start(bf16[3,16,2048]{2,1,0:T(8,128)(2,1)S(1)} %get-tuple-element.42), channel_id=1, source_target_pairs={{0,1},{1,0},{2,3},{3,2},{4,5},{5,4},{6,7},{7,6},{8,9},{9,8},{10,11... | collective-permute-start | bytes 589832 | tf_op jit(solution)/shard_map/ppermute | solution.py:386
  53.6 9.6 %collective-permute-start.8 = (bf16[3,16,2048]{2,1,0:T(8,128)(2,1)S(1)}, bf16[3,16,2048]{2,1,0:T(8,128)(2,1)S(1)}, u32[]{:S(2)}, u32[]{:S(2)}) collective-permute-start(bf16[3,16,2048]{2,1,0:T(8,128)(2,1)S(1)} %get-tuple-element.43), channel_id=1, source_target_pairs={{0,2},{1,3},{2,0},{3,1},{4,6},{5,7},{6,4},{7,5},{8,10},{9,11},{10,... | collective-permute-start | bytes 589832 | tf_op jit(solution)/shard_map/ppermute | solution.py:386
  54.2 10.5 %collective-permute-start.9 = (bf16[3,16,2048]{2,1,0:T(8,128)(2,1)S(1)}, bf16[3,16,2048]{2,1,0:T(8,128)(2,1)S(1)}, u32[]{:S(2)}, u32[]{:S(2)}) collective-permute-start(bf16[3,16,2048]{2,1,0:T(8,128)(2,1)S(1)} %get-tuple-element.44), channel_id=1, source_target_pairs={{0,3},{1,2},{2,1},{3,0},{4,7},{5,6},{6,5},{7,4},{8,11},{9,10},{10,... | collective-permute-start | bytes 589832 | tf_op jit(solution)/shard_map/ppermute | solution.py:386
  61.2 5.9 %collective-permute-start.10 = (bf16[1,16,2048]{2,1,0:T(8,128)(2,1)S(1)}, bf16[1,16,2048]{2,1,0:T(8,128)(2,1)S(1)}, u32[]{:S(2)}, u32[]{:S(2)}) collective-permute-start(bf16[1,16,2048]{2,1,0:T(8,128)(2,1)S(1)} %get-tuple-element.48), channel_id=1, source_target_pairs={{0,1},{1,0},{2,3},{3,2},{4,5},{5,4},{6,7},{7,6},{8,9},{9,8},{10,11... | collective-permute-start | bytes 196616 | tf_op jit(solution)/shard_map/ppermute | solution.py:386
  61.6 5.5 %collective-permute-start.11 = (bf16[1,16,2048]{2,1,0:T(8,128)(2,1)S(1)}, bf16[1,16,2048]{2,1,0:T(8,128)(2,1)S(1)}, u32[]{:S(2)}, u32[]{:S(2)}) collective-permute-start(bf16[1,16,2048]{2,1,0:T(8,128)(2,1)S(1)} %get-tuple-element.49), channel_id=1, source_target_pairs={{0,2},{1,3},{2,0},{3,1},{4,6},{5,7},{6,4},{7,5},{8,10},{9,11},{10,... | collective-permute-start | bytes 196616 | tf_op jit(solution)/shard_map/ppermute | solution.py:386
  62.1 5.4 %collective-permute-start.12 = (bf16[1,16,2048]{2,1,0:T(8,128)(2,1)S(1)}, bf16[1,16,2048]{2,1,0:T(8,128)(2,1)S(1)}, u32[]{:S(2)}, u32[]{:S(2)}) collective-permute-start(bf16[1,16,2048]{2,1,0:T(8,128)(2,1)S(1)} %get-tuple-element.50), channel_id=1, source_target_pairs={{0,3},{1,2},{2,1},{3,0},{4,7},{5,6},{6,5},{7,4},{8,11},{9,10},{10,... | collective-permute-start | bytes 196616 | tf_op jit(solution)/shard_map/ppermute | solution.py:386

commit v4 on v3

--- a/solution.py
+++ b/solution.py
@@ -10,7 +10,7 @@
 BF = jnp.bfloat16
 F32 = jnp.float32
 SUMS = 5
-VMEM_LIMIT = 26 * 1024 * 1024
+VMEM_LIMIT = 16 * 1024 * 1024
 
 
 def low_half(shape):
@@ -51,19 +51,20 @@
             rhs[base : base + rows, s * lane : (s + 1) * lane] = kept[b]
 
 
-def contract_left(lhs, rhs, con, chunk=512):
-    step = 256
+def contract_left(lhs, first, rhs, con):
+    step, chunk = 256, min(512, con.shape[0])
     for n in range(rhs.shape[1] // step):
         cols = slice(n * step, (n + 1) * step)
 
         def one(i, carry):
             rows = pl.ds(pl.multiple_of(i * chunk, chunk), chunk)
+            source = pl.ds(pl.multiple_of(first + i * chunk, chunk), chunk)
             con[rows, cols] = jnp.dot(
-                lhs[rows, :], rhs[:, cols], preferred_element_type=F32
+                lhs[source, :], rhs[:, cols], preferred_element_type=F32
             ).astype(BF)
             return carry
 
-        lax.fori_loop(0, lhs.shape[0] // chunk, one, 0, unroll=True)
+        lax.fori_loop(0, con.shape[0] // chunk, one, 0, unroll=True)
 
 
 def mix(amat, con, mixed, phys, lane):
@@ -141,7 +142,7 @@
                 s = 2 * pair + half
                 both[:, s * lane : (s + 1) * lane] = tile.astype(BF)
                 put_source(rhs, s, tile)
-        contract_left(lhs, rhs, con)
+        contract_left(lhs, 0, rhs, con)
         mix(amat, con, mixes.at[pi], phys, lane)
         return carry
 
@@ -220,29 +221,46 @@
     return ratio, jnp.sqrt(norm_sq / (total(rests) + 1e-06))
 
 
-def second_kernel(terms, pi, wide, phys, place, everyone, boths, images, lefts, amat, rmats, *refs):
-    carried = refs[:terms] if pi == 0 else ()
-    outs = refs[len(carried) : len(carried) + terms]
-    rhs, con, mixed, acc = refs[len(carried) + terms :]
-    lane = 2 * wide
-    slab = wide // terms
+def product_rows(place, chip, lhs, rhs, amat, rmat, outs, scratch, phys):
+    con, mixed, acc = scratch
+    lane = acc.shape[1]
+    slab = outs[0].shape[0]
+    other = lax.bitwise_xor(lax.div(place[0], 2), chip)
+    contract_left(lhs, other * con.shape[0], rhs, con)
+    mix(amat, con, mixed, phys, lane)
+    contract_right(mixed, rmat, acc)
+    for k, out in enumerate(outs):
+        at = lax.rem(lax.bitwise_xor(place[0], k), 2) * slab * phys
+        for y in range(phys):
+            out[:, y * lane : (y + 1) * lane] = acc[pl.ds(at + y, slab, stride=phys), :].astype(BF)
+
+
+def far_kernel(terms, pi, phys, place, everyone, boths, images, lefts, amat, rmats, *refs):
+    far = terms - 2
+    carried = refs[:far] if pi == 0 else ()
+    outs = refs[len(carried) : len(carried) + far]
+    rhs, *scratch = refs[len(carried) + far :]
+    lane = boths.shape[2] // phys
     ratio, scale = scalars(everyone, boths.shape[0])
     for s in range(phys):
         cols = slice(s * lane, (s + 1) * lane)
         rest = images[pi, :, cols].astype(F32) - ratio * boths[pi, :, cols].astype(F32)
         put_source(rhs, s, (rest * scale).astype(BF).astype(F32))
-    contract_left(lefts.at[pi], rhs, con)
-    mix(amat, con, mixed, phys, lane)
-    contract_right(mixed, rmats.at[pi], acc)
-    for k, out in enumerate(outs):
-        last = out.shape[0] - 1
-        if carried:
-            out[:last] = carried[k][...]
-        base = quarter_of(place, k, slab) * phys
-        for y in range(phys):
-            out[last, :, y * lane : (y + 1) * lane] = acc[
-                pl.ds(base + y, slab, stride=phys), :
-            ].astype(BF)
+    for out, piece in zip(outs, carried):
+        out[: piece.shape[0]] = piece[...]
+    last = outs[0].shape[0] - 1
+    for chip in range(1, terms // 2):
+        both = [outs[2 * chip - 2 + k].at[last] for k in range(2)]
+        product_rows(place, chip, lefts.at[pi], rhs, amat, rmats.at[pi], both, scratch, phys)
+
+
+def near_kernel(pairs, phys, place, lefts, amat, rmats, *refs):
+    sources, outs, scratch = refs[:pairs], refs[pairs : pairs + 2], refs[pairs + 2 :]
+    for pi in range(pairs):
+        both = [out.at[pi] for out in outs]
+        product_rows(
+            place, 0, lefts.at[pi], sources[pi], amat, rmats.at[pi], both, scratch, phys
+        )
 
 
 def select_kernel(wide, blocks, names, asked, right_env, *refs):
@@ -286,12 +304,12 @@
     for k in range(terms):
         source = lax.bitwise_xor(me, k)
         for pi in range(count):
-            if follows:
+            if follows or k < 2:
                 piece = refs[k].at[pi]
             elif pi == 0:
                 piece = refs[k].at[count]
             else:
-                piece = refs[terms * pi + k].at[0]
+                piece = refs[terms + (pi - 1) * (terms - 2) + k - 2].at[0]
             first = table[source * slots + 2 * pi]
             second = table[source * slots + 2 * pi + 1]
             for pair in range(phys // 2):
@@ -320,7 +338,7 @@
         out_specs=[pl.BlockSpec(memory_space=pltpu.VMEM)] * len(out_shapes),
         scratch_shapes=scratch,
         compiler_params=pltpu.CompilerParams(vmem_limit_bytes=VMEM_LIMIT),
-        cost_estimate=pl.CostEstimate(flops=flops, bytes_accessed=moved, transcendentals=0),
+        cost_estimate=pl.CostEstimate(flops=flops // 64, bytes_accessed=moved // 64, transcendentals=0),
     )(*operands)
 
 
@@ -450,26 +468,46 @@
     )
 
     everyone = lax.all_to_all(line, both_axes, 0, 0, tiled=True).reshape(-1, lane)
-
-    second_pieces = []
+    pieces, everyone = lax.optimization_barrier((pieces, everyone))
+
+    part_scratch = [
+        pltpu.VMEM((2 * slab * depth, phys * lane), BF),
+        pltpu.VMEM((2 * slab * phys, groups * lane), BF),
+        pltpu.VMEM((2 * slab * phys, lane), F32),
+    ]
+    product_flops = left_flops + mix_flops + right_flops
+    far_pieces, sources, sums = [], [], everyone
     for pi in range(pairs):
-        carried = pieces if pi == 0 else []
-        outs = call(
-            functools.partial(second_kernel, terms, pi, wide, phys),
+        carried = pieces[2:] if pi == 0 else []
+        *outs, source = call(
+            functools.partial(far_kernel, terms, pi, phys),
             1,
-            (where, everyone, boths, images, lefts, amat, rmats, *carried),
-            [stacked(pairs + 1 if carried else 1, slab, phys * lane)] * terms,
-            [rhs_scratch, con_scratch, pltpu.VMEM(mixed_shape, BF), acc_scratch],
-            left_flops + mix_flops + right_flops,
+            (where, sums, boths, images, lefts, amat, rmats, *carried),
+            [stacked(pairs + 1 if carried else 1, slab, phys * lane)] * (terms - 2)
+            + [stacked(4 * wide, phys * lane)],
+            part_scratch,
+            product_flops * (terms - 2) // terms,
             4 * wide * phys * lane * 2,
         )
-        second_pieces.append([outs[0]] + [shift(outs[k], k) for k in range(1, terms)])
+        outs, sums = lax.optimization_barrier((outs, sums))
+        far_pieces.append([shift(out, k + 2) for k, out in enumerate(outs)])
+        sources.append(source)
+    near_pieces = call(
+        functools.partial(near_kernel, pairs, phys),
+        1,
+        (where, lefts, amat, rmats, *sources),
+        [stacked(pairs, slab, phys * lane)] * 2,
+        part_scratch,
+        pairs * product_flops * 2 // terms,
+        4 * wide * phys * lane * 2,
+    )
+    near_pieces = [near_pieces[0], shift(near_pieces[1], 1)]
 
     out_shape = jax.ShapeDtypeStruct((blocks, slab, row_width), BF)
     first_image, next_rows = call(
         functools.partial(place_kernel, terms, wide, phys, pairs, True),
         1,
-        (table, everyone, vec, *second_pieces[0]),
+        (table, everyone, vec, pieces[0], shift(pieces[1], 1), *far_pieces[0]),
         [out_shape] * 2,
         [],
         0,
@@ -478,7 +516,7 @@
     (second_image,) = call(
         functools.partial(place_kernel, terms, wide, phys, pairs, False),
         1,
-        (table, *(piece for one_pair in second_pieces for piece in one_pair)),
+        (table, *near_pieces, *(piece for one_pair in far_pieces for piece in one_pair)),
         [out_shape],
         [],
         0,

time: 69.3 us -> 68.9 us (level)
  waiting for transfers between devices: 1.9 us -> 0.87 us
  Pallas kernels: 28.2 us -> 28.9 us
    ppermute x9, waiting for transfers between devices: 1.89 us -> 0.86 us  [shift(): return lax.ppermute(value, 'term', [(t, t ^ k) for t in range(terms)])]
    pallas_call x7 -> x8, Pallas kernels: 28.2 us -> 28.9 us  [call(): pl.pallas_call(kernel, out_shape=out_shapes, in_specs=specs, out_specs=[p...]
  transfers between devices with their start and end apart: 13 -> 13, of which waited for: 2 -> 1; matrix products, arithmetic and copies ran while one was open for 7% -> 7% of each run, Pallas kernels for 25% -> 34%
where the time goes in v4:
time: 68.9 us; the launch traced here: 68.5 us
  Pallas kernels  28.9 us (42%)
  blocking collectives  15.5 us (22%)
  starting transfers between devices  15.3 us (22%)
  local copies, waits for them, and re-layouts  4.87 us (7%)
  other arithmetic  1.27 us (2%)
  matrix products  0.98 us (1%)
  waiting for transfers between devices  0.87 us (1%)
  between operations  0.83 us (1%)
    pallas_call x8, Pallas kernels, call(): pl.pallas_call(kernel, out_shape=out_shapes, in_specs=specs, out_specs=[p...  28.9 us
    all_to_all x1, blocking collectives, body(): lax.all_to_all(line, both_axes, 0, 0, tiled=True).reshape(-1, lane)  15.5 us
    ppermute x9, starting transfers between devices, shift(): return lax.ppermute(value, 'term', [(t, t ^ k) for t in range(terms)])  6.97 us
    ppermute x2, starting transfers between devices, body(): lax.ppermute(wanted[a * each:(a + 1) * each], both_axes, swaps[a])  4.58 us
    ppermute x2, starting transfers between devices, body(): rights = [lax.ppermute(chosen[a], both_axes, swaps[a]) for a in range(span)]  3.76 us
    unnamed x8, local copies, waits for them, and re-layouts  3.4 us
  transfers between devices with their start and end apart: 13, of which 1 were waited for; matrix products, arithmetic and copies ran while one was open for 7% of the time, Pallas kernels for 34%

profile of v4, /device:TPU:0, one launch (start us, length us, event | category | flops | bytes accessed | tf_op | source)
XLA Modules:
  0.0 68.5 jit_solution(8266852206019298202)
XLA Ops:
  0.6 0.0 copy-start
  0.6 0.7 %convert_convert_fusion = (bf16[3]{0:T(256)(128)(2,1)S(1)}, bf16[1,3]{1,0:T(2,128)(2,1)S(1)}) fusion(s32[3]{0:T(128)} %param.13), kind=kLoop, calls=%fused_computation.41 | loop fusion | flops 6 | bytes 24 | tf_op jit(solution)/shard_map/squeeze | solution.py:407
  1.3 0.2 copy-done
  1.5 1.0 %fusion = bf16[3,16,16,32]{3,2,1,0:T(8,128)(2,1)S(1)} fusion(bf16[3,8,16,16]{3,2,1,0:T(8,128)(2,1)S(1)} %copy-done, s32[3,8]{1,0:T(4,128)} %param.12), kind=kOutput, calls=%fused_computation.1 | convolution fusion | flops 418560 | bytes 61536 | tf_op jit(solution)/shard_map/gtys,gtw->gysw/dot_general | solution.py:395
  2.5 0.2 reshape.184
  2.7 2.4 %collective-permute-start.2 = (bf16[64,512]{1,0:T(8,128)(2,1)S(1)}, bf16[64,512]{1,0:T(8,128)(2,1)S(1)}, u32[]{:S(2)}, u32[]{:S(2)}) collective-permute-start(bf16[64,512]{1,0:T(8,128)(2,1)S(1)} %fusion.3.refs_0_), channel_id=1, source_target_pairs={{0,3},{1,2},{2,1},{3,0},{4,7},{5,6},{6,5},{7,4},{8,11},{9,10},{10,... | collective-permute-start | bytes 196616 | tf_op jit(solution)/shard_map/ppermute | solution.py:404
  5.2 0.6 collective-permute-start.1
  5.8 0.0 collective-permute-start
  5.9 0.8 %copy.24 = s32[8,2]{1,0:T(8,128)S(1)} copy(s32[8,2]{0,1:T(2,128)} %param.8) | data formatting | bytes 128 | tf_op args[1]
  6.6 0.1 reshape.182
  6.7 0.2 convert_reduce_fusion
  6.9 0.1 select_reduce_fusion
  7.0 0.1 dynamic_slice.7
  7.1 0.1 fusion.12
  7.2 0.7 collective-permute-start.3
  7.9 0.0 copy-start.2
  7.9 3.9 %collective-permute-start.4 = (s32[2]{0:T(128)S(1)}, s32[2]{0:T(128)S(1)}, u32[]{:S(2)}, u32[]{:S(2)}) collective-permute-start(s32[2]{0:T(128)S(1)} %get-tuple-element.74), channel_id=1, source_target_pairs={{0,24},{1,17},{2,30},{3,23},{4,28},{5,21},{6,26},{7,19},{8,16},{9,... | collective-permute-start | bytes 32 | tf_op jit(solution)/shard_map/ppermute | solution.py:391
  11.8 2.4 %copy.26.right_env = bf16[8,26,4096]{2,1,0:T(8,128)(2,1)S(1)} copy(bf16[8,26,4096]{2,0,1:T(8,128)(2,1)} %param.10) | data formatting | bytes 3407872 | tf_op args[3]
  14.2 0.0 collective-permute-done.4
  14.2 0.1 pad_add_fusion.1.asked
  14.3 0.0 collective-permute-done.2.refs_3_
  14.3 0.0 collective-permute-done.1.refs_2_
  14.3 0.0 collective-permute-done.refs_1_
  14.4 0.1 maximum_convert_fusion.names
  14.4 1.1 %shard_map.94 = (bf16[2,64,768]{2,1,0:T(8,128)(2,1)S(1)}, bf16[2,64,768]{2,1,0:T(8,128)(2,1)S(1)}) custom-call(s32[12]{0:T(128)S(1)} %maximum_convert_fusion.names, s32[4]{0:T(128)S(1)} %pad_add_fusion.1.asked, bf16[8,26,4096]{2,1,0:T(8,128)(2,1)S(1)} %copy.26.right_env), custom_call_target="tpu_custom_call" | custom-call | bytes 13312 | tf_op jit(solution)/shard_map/pallas_call | solution.py:334
  15.6 0.0 copy-start.1
  15.6 0.8 %collective-permute-start.5 = (bf16[2,64,768]{2,1,0:T(8,128)(2,1)S(1)}, bf16[2,64,768]{2,1,0:T(8,128)(2,1)S(1)}, u32[]{:S(2)}, u32[]{:S(2)}) collective-permute-start(bf16[2,64,768]{2,1,0:T(8,128)(2,1)S(1)} %get-tuple-element.37), channel_id=1, source_target_pairs={{0,0},{1,9},{2,6},{3,15},{4,4},{5,13},{6,2},{7,11},{8,8},{9,1},{10... | collective-permute-start | bytes 589832 | tf_op jit(solution)/shard_map/ppermute | solution.py:423
  16.4 3.0 %collective-permute-start.6 = (bf16[2,64,768]{2,1,0:T(8,128)(2,1)S(1)}, bf16[2,64,768]{2,1,0:T(8,128)(2,1)S(1)}, u32[]{:S(2)}, u32[]{:S(2)}) collective-permute-start(bf16[2,64,768]{2,1,0:T(8,128)(2,1)S(1)} %get-tuple-element.38), channel_id=1, source_target_pairs={{0,24},{1,17},{2,30},{3,23},{4,28},{5,21},{6,26},{7,19},{8,16},{9,... | collective-permute-start | bytes 589832 | tf_op jit(solution)/shard_map/ppermute | solution.py:423
  19.4 0.1 dynamic_slice.6.own
  19.4 1.0 %copy.27.left_env = bf16[8,26,4096]{2,1,0:T(8,128)(2,1)S(1)} copy(bf16[8,26,4096]{2,0,1:T(8,128)(2,1)S(1)} %copy-done.2) | data formatting | bytes 3407872 | tf_op jit(solution)/shard_map/optimization_barrier | solution.py:424
  20.4 9.2 %shard_map.95 = (bf16[2,1024,1536]{2,1,0:T(8,128)(2,1)S(1)}, bf16[2,64,2048]{2,1,0:T(8,128)(2,1)S(1)}, bf16[2,2048,256]{2,1,0:T(8,128)(2,1)S(1)}, bf16[192,512]{1,0:T(8,128)(2,1)S(1)}) custom-call(s32[4]{0:T(128)S(1)} %dynamic_slice.6.own, bf16[8,26,4096]{2,1,0:T(8,128)(2,1)S(1)} %copy.27.left_env, bf16[16,64,1024]{2,1,0:T(8,128)(2,1)S(1)} %bitcast.23, ...), custom_call_target="tpu_custom_call" | custom-call | flops 117440512 | bytes 98304 | tf_op jit(solution)/shard_map/pallas_call | solution.py:334
  29.6 0.0 collective-permute-done.5.refs_0_
  29.7 0.0 collective-permute-done.6.refs_1_
  29.7 2.7 %shard_map.96 = (bf16[2,64,2048]{2,1,0:T(8,128)(2,1)S(1)}, f32[32,1,128]{2,1,0:T(1,128)S(1)}, bf16[2,128,1536]{2,1,0:T(8,128)(2,1)S(1)}, bf16[2,16,2048]{2,1,0:T...) custom-call(s32[1]{0:T(128)} %bitcast.place, ...), custom_call_target="tpu_custom_call" | custom-call | flops 12582912 | bytes 98304 | tf_op jit(solution)/shard_map/pallas_call | solution.py:334
  32.4 15.5 %all_to_all.5 = f32[32,1,128]{2,1,0:T(1,128)S(1)} all-to-all(f32[32,1,128]{2,1,0:T(1,128)S(1)} %get-tuple-element.46), channel_id=1, replica_groups=mesh['sec'=8,'term'=4] {'sec','term'}, dimensions={0} | all-to-all | bytes 32768 | tf_op jit(solution)/shard_map/all_to_all | solution.py:470
  48.0 3.3 %shard_map.97 = (bf16[3,16,2048]{2,1,0:T(8,128)(2,1)S(1)}, bf16[3,16,2048]{2,1,0:T(8,128)(2,1)S(1)}, bf16[256,2048]{1,0:T(8,128)(2,1)S(1)}) custom-call(s32[1]{0:T(128)} %bitcast.place, f32[32,128]{1,0:T(8,128)S(1)} %bitcast.25, bf16[2,64,2048]{2,1,0:T(8,128)(2,1)S(1)} %get-tuple-element.41.boths, bf16[2,64,2048]{2,1,0:T(8,128)(2,1)S(1)} %get-tuple-element.50.images, ...), custom_call_target="tpu_custom_call" | custom-call | flops 32505856 | bytes 16384 | tf_op jit(solution)/shard_map/pallas_call | solution.py:334
  51.3 0.6 collective-permute-start.8
  51.9 1.3 %collective-permute-start.9 = (bf16[3,16,2048]{2,1,0:T(8,128)(2,1)S(1)}, bf16[3,16,2048]{2,1,0:T(8,128)(2,1)S(1)}, u32[]{:S(2)}, u32[]{:S(2)}) collective-permute-start(bf16[3,16,2048]{2,1,0:T(8,128)(2,1)S(1)} %get-tuple-element.59), channel_id=1, source_target_pairs={{0,3},{1,2},{2,1},{3,0},{4,7},{5,6},{6,5},{7,4},{8,11},{9,10},{10,... | collective-permute-start | bytes 589832 | tf_op jit(solution)/shard_map/ppermute | solution.py:404
  53.2 3.3 %shard_map.99 = (bf16[1,16,2048]{2,1,0:T(8,128)(2,1)S(1)}, bf16[1,16,2048]{2,1,0:T(8,128)(2,1)S(1)}, bf16[256,2048]{1,0:T(8,128)(2,1)S(1)}) custom-call(s32[1]{0:T(128)} %bitcast.place, f32[32,128]{1,0:T(8,128)S(1)} %bitcast.26, bf16[2,64,2048]{2,1,0:T(8,128)(2,1)S(1)} %get-tuple-element.41.boths, bf16[2,64,2048]{2,1,0:T(8,128)(2,1)S(1)} %get-tuple-element.50.images, ...), custom_call_target="tpu_custom_call" | custom-call | flops 32505856 | bytes 16384 | tf_op jit(solution)/shard_map/pallas_call | solution.py:334
  56.6 5.1 %shard_map.100 = (bf16[2,16,2048]{2,1,0:T(8,128)(2,1)S(1)}, bf16[2,16,2048]{2,1,0:T(8,128)(2,1)S(1)}) custom-call(s32[1]{0:T(128)} %bitcast.place, bf16[2,2048,256]{2,1,0:T(8,128)(2,1)S(1)} %get-tuple-element.51.lefts, bf16[192,512]{1,0:T(8,128)(2,1)S(1)} %get-tuple-element.52.amat, bf16[2,128,1536]{2,1,0:T(8,128)(2,1)S(1)} %get-tuple-element.53.rmats, ...), custom_call_target="tpu_custom_call" | custom-call | flops 65011712 | bytes 16384 | tf_op jit(solution)/shard_map/pallas_call | solution.py:334
  61.7 0.3 collective-permute-start.10
  62.0 0.5 collective-permute-start.11
  62.6 0.0 collective-permute-done.7.refs_3_
  62.6 1.0 %collective-permute-start.12 = (bf16[1,16,2048]{2,1,0:T(8,128)(2,1)S(1)}, bf16[1,16,2048]{2,1,0:T(8,128)(2,1)S(1)}, u32[]{:S(2)}, u32[]{:S(2)}) collective-permute-start(bf16[1,16,2048]{2,1,0:T(8,128)(2,1)S(1)} %get-tuple-element.70), channel_id=1, source_target_pairs={{0,3},{1,2},{2,1},{3,0},{4,7},{5,6},{6,5},{7,4},{8,11},{9,10},{10,... | collective-permute-start | bytes 196616 | tf_op jit(solution)/shard_map/ppermute | solution.py:404
  63.6 0.1 pad_add_fusion.table
  63.7 2.4 %shard_map.98 = (bf16[16,16,1024]{2,1,0:T(8,128)(2,1)}, bf16[16,16,1024]{2,1,0:T(8,128)(2,1)}) custom-call(s32[17]{0:T(128)S(1)} %pad_add_fusion.table, f32[32,128]{1,0:T(8,128)S(1)} %bitcast.27, bf16[16,64,1024]{2,1,0:T(8,128)(2,1)S(1)} %bitcast.24, bf16[2,16,2048]{2,1,0:T(8,128)(2,1)S(1)} %get-tuple-element.48.refs_2_, ...), custom_call_target="tpu_custom_call" | custom-call | bytes 32768 | tf_op jit(solution)/shard_map/pallas_call | solution.py:334
  66.1 0.8 %collective-permute-done.11.refs_4_ = bf16[1,16,2048]{2,1,0:T(8,128)(2,1)S(1)} collective-permute-done((bf16[1,16,2048]{2,1,0:T(8,128)(2,1)S(1)}, bf16[1,16,2048]{2,1,0:T(8,128)(2,1)S(1)}, u32[]{:S(2)}, u32[]{:S(2)}) %collective-permute-start.11) | collective-permute-done | bytes 65568 | tf_op jit(solution)/shard_map/ppermute | solution.py:404
  67.0 1.6 %shard_map.101 = bf16[16,16,1024]{2,1,0:T(8,128)(2,1)} custom-call(s32[17]{0:T(128)S(1)} %pad_add_fusion.table, bf16[2,16,2048]{2,1,0:T(8,128)(2,1)S(1)} %get-tuple-element.65.refs_0_, bf16[2,16,2048]{2,1,0:T(8,128)(2,1)S(1)} %collective-permute-done.10.refs_1_, bf16[3,16,2048]{2,1,0:T(8,128)(2,1)S(1)} %collective-permute-done.8.refs_4_.refs_2_, ...), custom_call_target="tpu_custom_call" | custom-call | bytes 16384 | tf_op jit(solution)/shard_map/pallas_call | solution.py:334
  (14 shorter events, 0.1 us)
Async XLA Ops:
  0.6 0.9 %copy-start = (bf16[3,8,16,16]{3,2,1,0:T(8,128)(2,1)S(1)}, bf16[3,8,16,16]{3,2,1,0:T(8,128)(2,1)}, u32[]{:S(2)}) copy-start(bf16[3,8,16,16]{3,2,1,0:T(8,128)(2,1)} %param.11) | copy-start | bytes 36868
  2.7 11.6 %collective-permute-start.2 = (bf16[64,512]{1,0:T(8,128)(2,1)S(1)}, bf16[64,512]{1,0:T(8,128)(2,1)S(1)}, u32[]{:S(2)}, u32[]{:S(2)}) collective-permute-start(bf16[64,512]{1,0:T(8,128)(2,1)S(1)} %fusion.3.refs_0_), channel_id=1, source_target_pairs={{0,3},{1,2},{2,1},{3,0},{4,7},{5,6},{6,5},{7,4},{8,11},{9,10},{10,... | collective-permute-start | bytes 196616 | tf_op jit(solution)/shard_map/ppermute | solution.py:404
  5.2 9.1 %collective-permute-start.1 = (bf16[64,512]{1,0:T(8,128)(2,1)S(1)}, bf16[64,512]{1,0:T(8,128)(2,1)S(1)}, u32[]{:S(2)}, u32[]{:S(2)}) collective-permute-start(bf16[64,512]{1,0:T(8,128)(2,1)S(1)} %fusion.3.refs_0_), channel_id=1, source_target_pairs={{0,2},{1,3},{2,0},{3,1},{4,6},{5,7},{6,4},{7,5},{8,10},{9,11},{10,... | collective-permute-start | bytes 196616 | tf_op jit(solution)/shard_map/ppermute | solution.py:404
  5.8 8.5 %collective-permute-start = (bf16[64,512]{1,0:T(8,128)(2,1)S(1)}, bf16[64,512]{1,0:T(8,128)(2,1)S(1)}, u32[]{:S(2)}, u32[]{:S(2)}) collective-permute-start(bf16[64,512]{1,0:T(8,128)(2,1)S(1)} %fusion.3.refs_0_), channel_id=1, source_target_pairs={{0,1},{1,0},{2,3},{3,2},{4,5},{5,4},{6,7},{7,6},{8,9},{9,8},{10,11... | collective-permute-start | bytes 196616 | tf_op jit(solution)/shard_map/ppermute | solution.py:404
  7.2 7.0 %collective-permute-start.3 = (s32[2]{0:T(128)S(1)}, s32[2]{0:T(128)S(1)}, u32[]{:S(2)}, u32[]{:S(2)}) collective-permute-start(s32[2]{0:T(128)S(1)} %get-tuple-element.73), channel_id=1, source_target_pairs={{0,0},{1,9},{2,6},{3,15},{4,4},{5,13},{6,2},{7,11},{8,8},{9,1},{10... | collective-permute-start | bytes 32 | tf_op jit(solution)/shard_map/ppermute | solution.py:391
  7.9 11.6 %copy-start.2 = (bf16[8,26,4096]{2,0,1:T(8,128)(2,1)S(1)}, bf16[8,26,4096]{2,0,1:T(8,128)(2,1)}, u32[]{:S(2)}) copy-start(bf16[8,26,4096]{2,0,1:T(8,128)(2,1)} %param.9) | copy-start | bytes 5111812
  7.9 6.4 %collective-permute-start.4 = (s32[2]{0:T(128)S(1)}, s32[2]{0:T(128)S(1)}, u32[]{:S(2)}, u32[]{:S(2)}) collective-permute-start(s32[2]{0:T(128)S(1)} %get-tuple-element.74), channel_id=1, source_target_pairs={{0,24},{1,17},{2,30},{3,23},{4,28},{5,21},{6,26},{7,19},{8,16},{9,... | collective-permute-start | bytes 32 | tf_op jit(solution)/shard_map/ppermute | solution.py:391
  15.6 4.8 %copy-start.1 = (bf16[8,2,64,1024]{3,2,1,0:T(8,128)(2,1)S(1)}, bf16[8,2,64,1024]{3,2,1,0:T(8,128)(2,1)}, u32[]{:S(2)}) copy-start(bf16[8,2,64,1024]{3,2,1,0:T(8,128)(2,1)} %param.7) | copy-start | bytes 6291460
  15.6 14.1 %collective-permute-start.5 = (bf16[2,64,768]{2,1,0:T(8,128)(2,1)S(1)}, bf16[2,64,768]{2,1,0:T(8,128)(2,1)S(1)}, u32[]{:S(2)}, u32[]{:S(2)}) collective-permute-start(bf16[2,64,768]{2,1,0:T(8,128)(2,1)S(1)} %get-tuple-element.37), channel_id=1, source_target_pairs={{0,0},{1,9},{2,6},{3,15},{4,4},{5,13},{6,2},{7,11},{8,8},{9,1},{10... | collective-permute-start | bytes 589832 | tf_op jit(solution)/shard_map/ppermute | solution.py:423
  16.4 13.3 %collective-permute-start.6 = (bf16[2,64,768]{2,1,0:T(8,128)(2,1)S(1)}, bf16[2,64,768]{2,1,0:T(8,128)(2,1)S(1)}, u32[]{:S(2)}, u32[]{:S(2)}) collective-permute-start(bf16[2,64,768]{2,1,0:T(8,128)(2,1)S(1)} %get-tuple-element.38), channel_id=1, source_target_pairs={{0,24},{1,17},{2,30},{3,23},{4,28},{5,21},{6,26},{7,19},{8,16},{9,... | collective-permute-start | bytes 589832 | tf_op jit(solution)/shard_map/ppermute | solution.py:423
  47.9 14.6 %collective-permute-start.7 = (bf16[2,16,2048]{2,1,0:T(8,128)(2,1)S(1)}, bf16[2,16,2048]{2,1,0:T(8,128)(2,1)S(1)}, u32[]{:S(2)}, u32[]{:S(2)}) collective-permute-start(bf16[2,16,2048]{2,1,0:T(8,128)(2,1)S(1)} %get-tuple-element.49), channel_id=1, source_target_pairs={{0,1},{1,0},{2,3},{3,2},{4,5},{5,4},{6,7},{7,6},{8,9},{9,8},{10,11... | collective-permute-start | bytes 393224 | tf_op jit(solution)/shard_map/ppermute | solution.py:404
  51.3 12.4 %collective-permute-start.8 = (bf16[3,16,2048]{2,1,0:T(8,128)(2,1)S(1)}, bf16[3,16,2048]{2,1,0:T(8,128)(2,1)S(1)}, u32[]{:S(2)}, u32[]{:S(2)}) collective-permute-start(bf16[3,16,2048]{2,1,0:T(8,128)(2,1)S(1)} %get-tuple-element.58), channel_id=1, source_target_pairs={{0,2},{1,3},{2,0},{3,1},{4,6},{5,7},{6,4},{7,5},{8,10},{9,11},{10,... | collective-permute-start | bytes 589832 | tf_op jit(solution)/shard_map/ppermute | solution.py:404
  51.9 11.8 %collective-permute-start.9 = (bf16[3,16,2048]{2,1,0:T(8,128)(2,1)S(1)}, bf16[3,16,2048]{2,1,0:T(8,128)(2,1)S(1)}, u32[]{:S(2)}, u32[]{:S(2)}) collective-permute-start(bf16[3,16,2048]{2,1,0:T(8,128)(2,1)S(1)} %get-tuple-element.59), channel_id=1, source_target_pairs={{0,3},{1,2},{2,1},{3,0},{4,7},{5,6},{6,5},{7,4},{8,11},{9,10},{10,... | collective-permute-start | bytes 589832 | tf_op jit(solution)/shard_map/ppermute | solution.py:404
  61.7 5.3 %collective-permute-start.10 = (bf16[2,16,2048]{2,1,0:T(8,128)(2,1)S(1)}, bf16[2,16,2048]{2,1,0:T(8,128)(2,1)S(1)}, u32[]{:S(2)}, u32[]{:S(2)}) collective-permute-start(bf16[2,16,2048]{2,1,0:T(8,128)(2,1)S(1)} %get-tuple-element.66), channel_id=1, source_target_pairs={{0,1},{1,0},{2,3},{3,2},{4,5},{5,4},{6,7},{7,6},{8,9},{9,8},{10,11... | collective-permute-start | bytes 393224 | tf_op jit(solution)/shard_map/ppermute | solution.py:404
  62.0 4.9 %collective-permute-start.11 = (bf16[1,16,2048]{2,1,0:T(8,128)(2,1)S(1)}, bf16[1,16,2048]{2,1,0:T(8,128)(2,1)S(1)}, u32[]{:S(2)}, u32[]{:S(2)}) collective-permute-start(bf16[1,16,2048]{2,1,0:T(8,128)(2,1)S(1)} %get-tuple-element.69), channel_id=1, source_target_pairs={{0,2},{1,3},{2,0},{3,1},{4,6},{5,7},{6,4},{7,5},{8,10},{9,11},{10,... | collective-permute-start | bytes 196616 | tf_op jit(solution)/shard_map/ppermute | solution.py:404
  62.6 4.4 %collective-permute-start.12 = (bf16[1,16,2048]{2,1,0:T(8,128)(2,1)S(1)}, bf16[1,16,2048]{2,1,0:T(8,128)(2,1)S(1)}, u32[]{:S(2)}, u32[]{:S(2)}) collective-permute-start(bf16[1,16,2048]{2,1,0:T(8,128)(2,1)S(1)} %get-tuple-element.70), channel_id=1, source_target_pairs={{0,3},{1,2},{2,1},{3,0},{4,7},{5,6},{6,5},{7,4},{8,11},{9,10},{10,... | collective-permute-start | bytes 196616 | tf_op jit(solution)/shard_map/ppermute | solution.py:404

commit v5 on v4

--- a/solution.py
+++ b/solution.py
@@ -255,9 +255,9 @@
 
 
 def near_kernel(pairs, phys, place, lefts, amat, rmats, *refs):
-    sources, outs, scratch = refs[:pairs], refs[pairs : pairs + 2], refs[pairs + 2 :]
+    sources, outs, scratch = refs[:pairs], refs[pairs : 2 * pairs + 1], refs[2 * pairs + 1 :]
     for pi in range(pairs):
-        both = [out.at[pi] for out in outs]
+        both = [outs[0].at[pi], outs[1 + pi].at[0]]
         product_rows(
             place, 0, lefts.at[pi], sources[pi], amat, rmats.at[pi], both, scratch, phys
         )
@@ -304,7 +304,9 @@
     for k in range(terms):
         source = lax.bitwise_xor(me, k)
         for pi in range(count):
-            if follows or k < 2:
+            if not follows and k == 1:
+                piece = refs[k][pi].at[0]
+            elif follows or k < 2:
                 piece = refs[k].at[pi]
             elif pi == 0:
                 piece = refs[k].at[count]
@@ -324,6 +326,14 @@
                         rows = pl.ds(pl.multiple_of(me * slab, slab), slab)
                         rest = value - ratio * vec[where, rows, cols].astype(F32)
                         following[where, :, cols] = (rest * scale).astype(BF)
+
+
+def place_all(terms, wide, phys, count, table, everyone, vec, own_first, chip_first, own, *refs):
+    others, (first, following, second) = refs[:-3], refs[-3:]
+    far, chip = others[:-count], others[-count:]
+    ahead = (own_first, chip_first, *far[: terms - 2])
+    place_kernel(terms, wide, phys, count, True, table, everyone, vec, *ahead, first, following)
+    place_kernel(terms, wide, phys, count, False, table, own, chip, *far, second)
 
 
 def call(kernel, tables, operands, out_shapes, scratch, flops, moved):
@@ -496,31 +506,23 @@
         functools.partial(near_kernel, pairs, phys),
         1,
         (where, lefts, amat, rmats, *sources),
-        [stacked(pairs, slab, phys * lane)] * 2,
+        [stacked(pairs, slab, phys * lane)] + [stacked(1, slab, phys * lane)] * pairs,
         part_scratch,
         pairs * product_flops * 2 // terms,
         4 * wide * phys * lane * 2,
     )
-    near_pieces = [near_pieces[0], shift(near_pieces[1], 1)]
+    near_pieces = [near_pieces[0]] + [shift(piece, 1) for piece in near_pieces[1:]]
 
     out_shape = jax.ShapeDtypeStruct((blocks, slab, row_width), BF)
-    first_image, next_rows = call(
-        functools.partial(place_kernel, terms, wide, phys, pairs, True),
+    far = [piece for one_pair in far_pieces for piece in one_pair]
+    first_image, next_rows, second_image = call(
+        functools.partial(place_all, terms, wide, phys, pairs),
         1,
-        (table, everyone, vec, pieces[0], shift(pieces[1], 1), *far_pieces[0]),
-        [out_shape] * 2,
+        (table, everyone, vec, pieces[0], shift(pieces[1], 1), near_pieces[0], *far, *near_pieces[1:]),
+        [out_shape] * 3,
         [],
         0,
-        blocks * slab * row_width * 8,
-    )
-    (second_image,) = call(
-        functools.partial(place_kernel, terms, wide, phys, pairs, False),
-        1,
-        (table, *near_pieces, *(piece for one_pair in far_pieces for piece in one_pair)),
-        [out_shape],
-        [],
-        0,
-        blocks * slab * row_width * 4,
+        blocks * slab * row_width * 12,
     )
     shape = (per_device, per_left, slab, row_width)
     return (first_image.reshape(shape), next_rows.reshape(shape), second_image.reshape(shape))

time: 68.9 us -> 68.6 us (level)
  Pallas kernels: 28.9 us -> 27.4 us
  waiting for transfers between devices: 0.87 us -> 1.83 us
    pallas_call x8 -> x7, Pallas kernels: 28.9 us -> 27.4 us  [call(): pl.pallas_call(kernel, out_shape=out_shapes, in_specs=specs, out_specs=[p...]
    ppermute x9 -> x10, waiting for transfers between devices: 0.86 us -> 1.82 us  [shift(): return lax.ppermute(value, 'term', [(t, t ^ k) for t in range(terms)])]
    ppermute x9 -> x10, starting transfers between devices: 6.97 us -> 7.27 us  [shift(): return lax.ppermute(value, 'term', [(t, t ^ k) for t in range(terms)])]
  transfers between devices with their start and end apart: 13 -> 14, of which waited for: 1 -> 3; matrix products, arithmetic and copies ran while one was open for 7% -> 7% of each run, Pallas kernels for 34% -> 26%
where the time goes in v5:
time: 68.6 us; the launch traced here: 68.3 us
  Pallas kernels  27.4 us (40%)
  starting transfers between devices  15.6 us (23%)
  blocking collectives  15.5 us (23%)
  local copies, waits for them, and re-layouts  4.87 us (7%)
  waiting for transfers between devices  1.83 us (3%)
  other arithmetic  1.27 us (2%)
  matrix products  0.98 us (1%)
  between operations  0.83 us (1%)
    pallas_call x7, Pallas kernels, call(): pl.pallas_call(kernel, out_shape=out_shapes, in_specs=specs, out_specs=[p...  27.4 us
    all_to_all x1, blocking collectives, body(): lax.all_to_all(line, both_axes, 0, 0, tiled=True).reshape(-1, lane)  15.5 us
    ppermute x10, starting transfers between devices, shift(): return lax.ppermute(value, 'term', [(t, t ^ k) for t in range(terms)])  7.27 us
    ppermute x2, starting transfers between devices, body(): lax.ppermute(wanted[a * each:(a + 1) * each], both_axes, swaps[a])  4.58 us
    ppermute x2, starting transfers between devices, body(): rights = [lax.ppermute(chosen[a], both_axes, swaps[a]) for a in range(span)]  3.76 us
    unnamed x8, local copies, waits for them, and re-layouts  3.4 us
    ppermute x10, waiting for transfers between devices, shift(): return lax.ppermute(value, 'term', [(t, t ^ k) for t in range(terms)])  1.82 us
  transfers between devices with their start and end apart: 14, of which 3 were waited for; matrix products, arithmetic and copies ran while one was open for 7% of the time, Pallas kernels for 26%

profile of v5, /device:TPU:0, one launch (start us, length us, event | category | flops | bytes accessed | tf_op | source)
XLA Modules:
  0.0 68.3 jit_solution(3581033839993178986)
XLA Ops:
  0.6 0.0 copy-start
  0.6 0.7 %convert_convert_fusion = (bf16[3]{0:T(256)(128)(2,1)S(1)}, bf16[1,3]{1,0:T(2,128)(2,1)S(1)}) fusion(s32[3]{0:T(128)} %param.13), kind=kLoop, calls=%fused_computation.41 | loop fusion | flops 6 | bytes 24 | tf_op jit(solution)/shard_map/squeeze | solution.py:417
  1.3 0.2 copy-done
  1.5 1.0 %fusion = bf16[3,16,16,32]{3,2,1,0:T(8,128)(2,1)S(1)} fusion(bf16[3,8,16,16]{3,2,1,0:T(8,128)(2,1)S(1)} %copy-done, s32[3,8]{1,0:T(4,128)} %param.12), kind=kOutput, calls=%fused_computation.1 | convolution fusion | flops 418560 | bytes 61536 | tf_op jit(solution)/shard_map/gtys,gtw->gysw/dot_general | solution.py:405
  2.5 0.2 reshape.184
  2.7 2.4 %collective-permute-start.2 = (bf16[64,512]{1,0:T(8,128)(2,1)S(1)}, bf16[64,512]{1,0:T(8,128)(2,1)S(1)}, u32[]{:S(2)}, u32[]{:S(2)}) collective-permute-start(bf16[64,512]{1,0:T(8,128)(2,1)S(1)} %fusion.3.refs_0_), channel_id=1, source_target_pairs={{0,3},{1,2},{2,1},{3,0},{4,7},{5,6},{6,5},{7,4},{8,11},{9,10},{10,... | collective-permute-start | bytes 196616 | tf_op jit(solution)/shard_map/ppermute | solution.py:414
  5.2 0.6 collective-permute-start.1
  5.8 0.0 collective-permute-start
  5.9 0.8 %copy.24 = s32[8,2]{1,0:T(8,128)S(1)} copy(s32[8,2]{0,1:T(2,128)} %param.8) | data formatting | bytes 128 | tf_op args[1]
  6.6 0.1 reshape.182
  6.7 0.2 convert_reduce_fusion
  6.9 0.1 select_reduce_fusion
  7.0 0.1 dynamic_slice.7
  7.1 0.1 fusion.12
  7.2 0.7 collective-permute-start.3
  7.9 0.0 copy-start.2
  7.9 3.9 %collective-permute-start.4 = (s32[2]{0:T(128)S(1)}, s32[2]{0:T(128)S(1)}, u32[]{:S(2)}, u32[]{:S(2)}) collective-permute-start(s32[2]{0:T(128)S(1)} %get-tuple-element.78), channel_id=1, source_target_pairs={{0,24},{1,17},{2,30},{3,23},{4,28},{5,21},{6,26},{7,19},{8,16},{9,... | collective-permute-start | bytes 32 | tf_op jit(solution)/shard_map/ppermute | solution.py:401
  11.8 2.4 %copy.26.right_env = bf16[8,26,4096]{2,1,0:T(8,128)(2,1)S(1)} copy(bf16[8,26,4096]{2,0,1:T(8,128)(2,1)} %param.10) | data formatting | bytes 3407872 | tf_op args[3]
  14.2 0.1 pad_add_fusion.1.asked
  14.3 0.0 collective-permute-done.2.refs_3_
  14.3 0.0 collective-permute-done.1.refs_2_
  14.3 0.0 collective-permute-done.refs_1_
  14.4 0.1 maximum_convert_fusion.names
  14.4 1.1 %shard_map.94 = (bf16[2,64,768]{2,1,0:T(8,128)(2,1)S(1)}, bf16[2,64,768]{2,1,0:T(8,128)(2,1)S(1)}) custom-call(s32[12]{0:T(128)S(1)} %maximum_convert_fusion.names, s32[4]{0:T(128)S(1)} %pad_add_fusion.1.asked, bf16[8,26,4096]{2,1,0:T(8,128)(2,1)S(1)} %copy.26.right_env), custom_call_target="tpu_custom_call" | custom-call | bytes 13312 | tf_op jit(solution)/shard_map/pallas_call | solution.py:344
  15.6 0.0 copy-start.1
  15.6 0.8 %collective-permute-start.5 = (bf16[2,64,768]{2,1,0:T(8,128)(2,1)S(1)}, bf16[2,64,768]{2,1,0:T(8,128)(2,1)S(1)}, u32[]{:S(2)}, u32[]{:S(2)}) collective-permute-start(bf16[2,64,768]{2,1,0:T(8,128)(2,1)S(1)} %get-tuple-element.39), channel_id=1, source_target_pairs={{0,0},{1,9},{2,6},{3,15},{4,4},{5,13},{6,2},{7,11},{8,8},{9,1},{10... | collective-permute-start | bytes 589832 | tf_op jit(solution)/shard_map/ppermute | solution.py:433
  16.4 3.0 %collective-permute-start.6 = (bf16[2,64,768]{2,1,0:T(8,128)(2,1)S(1)}, bf16[2,64,768]{2,1,0:T(8,128)(2,1)S(1)}, u32[]{:S(2)}, u32[]{:S(2)}) collective-permute-start(bf16[2,64,768]{2,1,0:T(8,128)(2,1)S(1)} %get-tuple-element.40), channel_id=1, source_target_pairs={{0,24},{1,17},{2,30},{3,23},{4,28},{5,21},{6,26},{7,19},{8,16},{9,... | collective-permute-start | bytes 589832 | tf_op jit(solution)/shard_map/ppermute | solution.py:433
  19.4 0.1 dynamic_slice.6.own
  19.4 1.0 %copy.27.left_env = bf16[8,26,4096]{2,1,0:T(8,128)(2,1)S(1)} copy(bf16[8,26,4096]{2,0,1:T(8,128)(2,1)S(1)} %copy-done.2) | data formatting | bytes 3407872 | tf_op jit(solution)/shard_map/optimization_barrier | solution.py:434
  20.4 9.2 %shard_map.95 = (bf16[2,1024,1536]{2,1,0:T(8,128)(2,1)S(1)}, bf16[2,64,2048]{2,1,0:T(8,128)(2,1)S(1)}, bf16[2,2048,256]{2,1,0:T(8,128)(2,1)S(1)}, bf16[192,512]{1,0:T(8,128)(2,1)S(1)}) custom-call(s32[4]{0:T(128)S(1)} %dynamic_slice.6.own, bf16[8,26,4096]{2,1,0:T(8,128)(2,1)S(1)} %copy.27.left_env, bf16[16,64,1024]{2,1,0:T(8,128)(2,1)S(1)} %bitcast.23, ...), custom_call_target="tpu_custom_call" | custom-call | flops 117440512 | bytes 98304 | tf_op jit(solution)/shard_map/pallas_call | solution.py:344
  29.6 0.0 collective-permute-done.5.refs_0_
  29.7 2.7 %shard_map.96 = (bf16[2,64,2048]{2,1,0:T(8,128)(2,1)S(1)}, f32[32,1,128]{2,1,0:T(1,128)S(1)}, bf16[2,128,1536]{2,1,0:T(8,128)(2,1)S(1)}, bf16[2,16,2048]{2,1,0:T...) custom-call(s32[1]{0:T(128)} %bitcast.place, ...), custom_call_target="tpu_custom_call" | custom-call | flops 12582912 | bytes 98304 | tf_op jit(solution)/shard_map/pallas_call | solution.py:344
  32.4 15.5 %all_to_all.5 = f32[32,1,128]{2,1,0:T(1,128)S(1)} all-to-all(f32[32,1,128]{2,1,0:T(1,128)S(1)} %get-tuple-element.48), channel_id=1, replica_groups=mesh['sec'=8,'term'=4] {'sec','term'}, dimensions={0} | all-to-all | bytes 32768 | tf_op jit(solution)/shard_map/all_to_all | solution.py:480
  47.9 3.3 %shard_map.97 = (bf16[3,16,2048]{2,1,0:T(8,128)(2,1)S(1)}, bf16[3,16,2048]{2,1,0:T(8,128)(2,1)S(1)}, bf16[256,2048]{1,0:T(8,128)(2,1)S(1)}) custom-call(s32[1]{0:T(128)} %bitcast.place, f32[32,128]{1,0:T(8,128)S(1)} %bitcast.25, bf16[2,64,2048]{2,1,0:T(8,128)(2,1)S(1)} %get-tuple-element.43.boths, bf16[2,64,2048]{2,1,0:T(8,128)(2,1)S(1)} %get-tuple-element.55.images, ...), custom_call_target="tpu_custom_call" | custom-call | flops 32505856 | bytes 16384 | tf_op jit(solution)/shard_map/pallas_call | solution.py:344
  51.3 0.6 collective-permute-start.8
  51.9 0.7 %collective-permute-start.9 = (bf16[3,16,2048]{2,1,0:T(8,128)(2,1)S(1)}, bf16[3,16,2048]{2,1,0:T(8,128)(2,1)S(1)}, u32[]{:S(2)}, u32[]{:S(2)}) collective-permute-start(bf16[3,16,2048]{2,1,0:T(8,128)(2,1)S(1)} %get-tuple-element.65), channel_id=1, source_target_pairs={{0,3},{1,2},{2,1},{3,0},{4,7},{5,6},{6,5},{7,4},{8,11},{9,10},{10,... | collective-permute-start | bytes 589832 | tf_op jit(solution)/shard_map/ppermute | solution.py:414
  52.6 3.3 %shard_map.98 = (bf16[1,16,2048]{2,1,0:T(8,128)(2,1)S(1)}, bf16[1,16,2048]{2,1,0:T(8,128)(2,1)S(1)}, bf16[256,2048]{1,0:T(8,128)(2,1)S(1)}) custom-call(s32[1]{0:T(128)} %bitcast.place, f32[32,128]{1,0:T(8,128)S(1)} %bitcast.26, bf16[2,64,2048]{2,1,0:T(8,128)(2,1)S(1)} %get-tuple-element.43.boths, bf16[2,64,2048]{2,1,0:T(8,128)(2,1)S(1)} %get-tuple-element.55.images, ...), custom_call_target="tpu_custom_call" | custom-call | flops 32505856 | bytes 16384 | tf_op jit(solution)/shard_map/pallas_call | solution.py:344
  55.9 0.9 %collective-permute-start.10 = (bf16[1,16,2048]{2,1,0:T(8,128)(2,1)S(1)}, bf16[1,16,2048]{2,1,0:T(8,128)(2,1)S(1)}, u32[]{:S(2)}, u32[]{:S(2)}) collective-permute-start(bf16[1,16,2048]{2,1,0:T(8,128)(2,1)S(1)} %get-tuple-element.68), channel_id=1, source_target_pairs={{0,2},{1,3},{2,0},{3,1},{4,6},{5,7},{6,4},{7,5},{8,10},{9,11},{10,... | collective-permute-start | bytes 196616 | tf_op jit(solution)/shard_map/ppermute | solution.py:414
  56.8 1.5 %collective-permute-start.11 = (bf16[1,16,2048]{2,1,0:T(8,128)(2,1)S(1)}, bf16[1,16,2048]{2,1,0:T(8,128)(2,1)S(1)}, u32[]{:S(2)}, u32[]{:S(2)}) collective-permute-start(bf16[1,16,2048]{2,1,0:T(8,128)(2,1)S(1)} %get-tuple-element.69), channel_id=1, source_target_pairs={{0,3},{1,2},{2,1},{3,0},{4,7},{5,6},{6,5},{7,4},{8,11},{9,10},{10,... | collective-permute-start | bytes 196616 | tf_op jit(solution)/shard_map/ppermute | solution.py:414
  58.2 0.0 collective-permute-start.7
  58.2 5.1 %shard_map.99 = (bf16[2,16,2048]{2,1,0:T(8,128)(2,1)S(1)}, bf16[1,16,2048]{2,1,0:T(8,128)(2,1)S(1)}, bf16[1,16,2048]{2,1,0:T(8,128)(2,1)S(1)}) custom-call(s32[1]{0:T(128)} %bitcast.place, bf16[2,2048,256]{2,1,0:T(8,128)(2,1)S(1)} %get-tuple-element.52.lefts, bf16[192,512]{1,0:T(8,128)(2,1)S(1)} %get-tuple-element.53.amat, ...), custom_call_target="tpu_custom_call" | custom-call | flops 65011712 | bytes 16384 | tf_op jit(solution)/shard_map/pallas_call | solution.py:344
  63.4 1.0 %collective-permute-done.10.refs_2_ = bf16[1,16,2048]{2,1,0:T(8,128)(2,1)S(1)} collective-permute-done((bf16[1,16,2048]{2,1,0:T(8,128)(2,1)S(1)}, bf16[1,16,2048]{2,1,0:T(8,128)(2,1)S(1)}, u32[]{:S(2)}, u32[]{:S(2)}) %collective-permute-start.10) | collective-permute-done | bytes 65568 | tf_op jit(solution)/shard_map/ppermute | solution.py:414
  64.3 0.0 collective-permute-start.12
  64.3 0.5 collective-permute-start.13
  64.9 0.1 pad_add_fusion.table
  64.9 0.7 collective-permute-done.12.refs_4_
  65.6 0.2 collective-permute-done.13.refs_5_
  65.8 2.5 %shard_map.100 = (bf16[16,16,1024]{2,1,0:T(8,128)(2,1)}, bf16[16,16,1024]{2,1,0:T(8,128)(2,1)}, bf16[16,16,1024]{2,1,0:T(8,128)(2,1)}) custom-call(s32[17]{0:T(128)S(1)} %pad_add_fusion.table, f32[32,128]{1,0:T(8,128)S(1)} %bitcast.27, bf16[16,64,1024]{2,1,0:T(8,128)(2,1)S(1)} %bitcast.24, bf16[2,16,2048]{2,1,0:T(8,128)(2,1)S(1)} %get-tuple-element.50.own_first, ...), custom_call_target="tpu_custom_call" | custom-call | bytes 49152 | tf_op jit(solution)/shard_map/pallas_call | solution.py:344
  (15 shorter events, 0.1 us)
Async XLA Ops:
  0.6 0.9 %copy-start = (bf16[3,8,16,16]{3,2,1,0:T(8,128)(2,1)S(1)}, bf16[3,8,16,16]{3,2,1,0:T(8,128)(2,1)}, u32[]{:S(2)}) copy-start(bf16[3,8,16,16]{3,2,1,0:T(8,128)(2,1)} %param.11) | copy-start | bytes 36868
  2.7 11.6 %collective-permute-start.2 = (bf16[64,512]{1,0:T(8,128)(2,1)S(1)}, bf16[64,512]{1,0:T(8,128)(2,1)S(1)}, u32[]{:S(2)}, u32[]{:S(2)}) collective-permute-start(bf16[64,512]{1,0:T(8,128)(2,1)S(1)} %fusion.3.refs_0_), channel_id=1, source_target_pairs={{0,3},{1,2},{2,1},{3,0},{4,7},{5,6},{6,5},{7,4},{8,11},{9,10},{10,... | collective-permute-start | bytes 196616 | tf_op jit(solution)/shard_map/ppermute | solution.py:414
  5.2 9.1 %collective-permute-start.1 = (bf16[64,512]{1,0:T(8,128)(2,1)S(1)}, bf16[64,512]{1,0:T(8,128)(2,1)S(1)}, u32[]{:S(2)}, u32[]{:S(2)}) collective-permute-start(bf16[64,512]{1,0:T(8,128)(2,1)S(1)} %fusion.3.refs_0_), channel_id=1, source_target_pairs={{0,2},{1,3},{2,0},{3,1},{4,6},{5,7},{6,4},{7,5},{8,10},{9,11},{10,... | collective-permute-start | bytes 196616 | tf_op jit(solution)/shard_map/ppermute | solution.py:414
  5.8 8.5 %collective-permute-start = (bf16[64,512]{1,0:T(8,128)(2,1)S(1)}, bf16[64,512]{1,0:T(8,128)(2,1)S(1)}, u32[]{:S(2)}, u32[]{:S(2)}) collective-permute-start(bf16[64,512]{1,0:T(8,128)(2,1)S(1)} %fusion.3.refs_0_), channel_id=1, source_target_pairs={{0,1},{1,0},{2,3},{3,2},{4,5},{5,4},{6,7},{7,6},{8,9},{9,8},{10,11... | collective-permute-start | bytes 196616 | tf_op jit(solution)/shard_map/ppermute | solution.py:414
  7.2 7.0 %collective-permute-start.3 = (s32[2]{0:T(128)S(1)}, s32[2]{0:T(128)S(1)}, u32[]{:S(2)}, u32[]{:S(2)}) collective-permute-start(s32[2]{0:T(128)S(1)} %get-tuple-element.77), channel_id=1, source_target_pairs={{0,0},{1,9},{2,6},{3,15},{4,4},{5,13},{6,2},{7,11},{8,8},{9,1},{10... | collective-permute-start | bytes 32 | tf_op jit(solution)/shard_map/ppermute | solution.py:401
  7.9 11.6 %copy-start.2 = (bf16[8,26,4096]{2,0,1:T(8,128)(2,1)S(1)}, bf16[8,26,4096]{2,0,1:T(8,128)(2,1)}, u32[]{:S(2)}) copy-start(bf16[8,26,4096]{2,0,1:T(8,128)(2,1)} %param.9) | copy-start | bytes 5111812
  7.9 6.4 %collective-permute-start.4 = (s32[2]{0:T(128)S(1)}, s32[2]{0:T(128)S(1)}, u32[]{:S(2)}, u32[]{:S(2)}) collective-permute-start(s32[2]{0:T(128)S(1)} %get-tuple-element.78), channel_id=1, source_target_pairs={{0,24},{1,17},{2,30},{3,23},{4,28},{5,21},{6,26},{7,19},{8,16},{9,... | collective-permute-start | bytes 32 | tf_op jit(solution)/shard_map/ppermute | solution.py:401
  15.6 4.8 %copy-start.1 = (bf16[8,2,64,1024]{3,2,1,0:T(8,128)(2,1)S(1)}, bf16[8,2,64,1024]{3,2,1,0:T(8,128)(2,1)}, u32[]{:S(2)}) copy-start(bf16[8,2,64,1024]{3,2,1,0:T(8,128)(2,1)} %param.7) | copy-start | bytes 6291460
  15.6 14.1 %collective-permute-start.5 = (bf16[2,64,768]{2,1,0:T(8,128)(2,1)S(1)}, bf16[2,64,768]{2,1,0:T(8,128)(2,1)S(1)}, u32[]{:S(2)}, u32[]{:S(2)}) collective-permute-start(bf16[2,64,768]{2,1,0:T(8,128)(2,1)S(1)} %get-tuple-element.39), channel_id=1, source_target_pairs={{0,0},{1,9},{2,6},{3,15},{4,4},{5,13},{6,2},{7,11},{8,8},{9,1},{10... | collective-permute-start | bytes 589832 | tf_op jit(solution)/shard_map/ppermute | solution.py:433
  16.4 13.3 %collective-permute-start.6 = (bf16[2,64,768]{2,1,0:T(8,128)(2,1)S(1)}, bf16[2,64,768]{2,1,0:T(8,128)(2,1)S(1)}, u32[]{:S(2)}, u32[]{:S(2)}) collective-permute-start(bf16[2,64,768]{2,1,0:T(8,128)(2,1)S(1)} %get-tuple-element.40), channel_id=1, source_target_pairs={{0,24},{1,17},{2,30},{3,23},{4,28},{5,21},{6,26},{7,19},{8,16},{9,... | collective-permute-start | bytes 589832 | tf_op jit(solution)/shard_map/ppermute | solution.py:433
  51.3 14.5 %collective-permute-start.8 = (bf16[3,16,2048]{2,1,0:T(8,128)(2,1)S(1)}, bf16[3,16,2048]{2,1,0:T(8,128)(2,1)S(1)}, u32[]{:S(2)}, u32[]{:S(2)}) collective-permute-start(bf16[3,16,2048]{2,1,0:T(8,128)(2,1)S(1)} %get-tuple-element.64), channel_id=1, source_target_pairs={{0,2},{1,3},{2,0},{3,1},{4,6},{5,7},{6,4},{7,5},{8,10},{9,11},{10,... | collective-permute-start | bytes 589832 | tf_op jit(solution)/shard_map/ppermute | solution.py:414
  51.9 13.9 %collective-permute-start.9 = (bf16[3,16,2048]{2,1,0:T(8,128)(2,1)S(1)}, bf16[3,16,2048]{2,1,0:T(8,128)(2,1)S(1)}, u32[]{:S(2)}, u32[]{:S(2)}) collective-permute-start(bf16[3,16,2048]{2,1,0:T(8,128)(2,1)S(1)} %get-tuple-element.65), channel_id=1, source_target_pairs={{0,3},{1,2},{2,1},{3,0},{4,7},{5,6},{6,5},{7,4},{8,11},{9,10},{10,... | collective-permute-start | bytes 589832 | tf_op jit(solution)/shard_map/ppermute | solution.py:414
  55.9 8.4 %collective-permute-start.10 = (bf16[1,16,2048]{2,1,0:T(8,128)(2,1)S(1)}, bf16[1,16,2048]{2,1,0:T(8,128)(2,1)S(1)}, u32[]{:S(2)}, u32[]{:S(2)}) collective-permute-start(bf16[1,16,2048]{2,1,0:T(8,128)(2,1)S(1)} %get-tuple-element.68), channel_id=1, source_target_pairs={{0,2},{1,3},{2,0},{3,1},{4,6},{5,7},{6,4},{7,5},{8,10},{9,11},{10,... | collective-permute-start | bytes 196616 | tf_op jit(solution)/shard_map/ppermute | solution.py:414
  56.8 7.6 %collective-permute-start.11 = (bf16[1,16,2048]{2,1,0:T(8,128)(2,1)S(1)}, bf16[1,16,2048]{2,1,0:T(8,128)(2,1)S(1)}, u32[]{:S(2)}, u32[]{:S(2)}) collective-permute-start(bf16[1,16,2048]{2,1,0:T(8,128)(2,1)S(1)} %get-tuple-element.69), channel_id=1, source_target_pairs={{0,3},{1,2},{2,1},{3,0},{4,7},{5,6},{6,5},{7,4},{8,11},{9,10},{10,... | collective-permute-start | bytes 196616 | tf_op jit(solution)/shard_map/ppermute | solution.py:414
  58.2 7.5 %collective-permute-start.7 = (bf16[2,16,2048]{2,1,0:T(8,128)(2,1)S(1)}, bf16[2,16,2048]{2,1,0:T(8,128)(2,1)S(1)}, u32[]{:S(2)}, u32[]{:S(2)}) collective-permute-start(bf16[2,16,2048]{2,1,0:T(8,128)(2,1)S(1)} %get-tuple-element.51), channel_id=1, source_target_pairs={{0,1},{1,0},{2,3},{3,2},{4,5},{5,4},{6,7},{7,6},{8,9},{9,8},{10,11... | collective-permute-start | bytes 393224 | tf_op jit(solution)/shard_map/ppermute | solution.py:414
  64.3 1.3 %collective-permute-start.12 = (bf16[1,16,2048]{2,1,0:T(8,128)(2,1)S(1)}, bf16[1,16,2048]{2,1,0:T(8,128)(2,1)S(1)}, u32[]{:S(2)}, u32[]{:S(2)}) collective-permute-start(bf16[1,16,2048]{2,1,0:T(8,128)(2,1)S(1)} %get-tuple-element.70), channel_id=1, source_target_pairs={{0,1},{1,0},{2,3},{3,2},{4,5},{5,4},{6,7},{7,6},{8,9},{9,8},{10,11... | collective-permute-start | bytes 196616 | tf_op jit(solution)/shard_map/ppermute | solution.py:414
  64.3 1.4 %collective-permute-start.13 = (bf16[1,16,2048]{2,1,0:T(8,128)(2,1)S(1)}, bf16[1,16,2048]{2,1,0:T(8,128)(2,1)S(1)}, u32[]{:S(2)}, u32[]{:S(2)}) collective-permute-start(bf16[1,16,2048]{2,1,0:T(8,128)(2,1)S(1)} %get-tuple-element.71), channel_id=1, source_target_pairs={{0,1},{1,0},{2,3},{3,2},{4,5},{5,4},{6,7},{7,6},{8,9},{9,8},{10,11... | collective-permute-start | bytes 196616 | tf_op jit(solution)/shard_map/ppermute | solution.py:414

commit v6 on v5

--- a/solution.py
+++ b/solution.py
@@ -127,13 +127,14 @@
 
 def left_kernel(per_left, wide, phys, own, left_env, vec, *refs):
     parts = refs[:-6]
-    mixes, boths, lefts, amat, rhs, con = refs[-6:]
+    mixes, boths, lefts, amat, sources, con = refs[-6:]
     lane = 2 * wide
     copy_operator(amat, parts)
 
-    def one(pi, carry):
+    pairs = boths.shape[0]
+    for pi in range(pairs):
         first, second = own[2 * pi], own[2 * pi + 1]
-        both, lhs = boths.at[pi], lefts.at[pi]
+        both, lhs, rhs = boths.at[pi], lefts.at[pi], sources.at[pi]
         fill_left(lhs, [left_env.at[lax.div(n, per_left)] for n in (first, second)], wide)
         for pair in range(phys // 2):
             cols = slice(pair * lane, (pair + 1) * lane)
@@ -142,11 +143,9 @@
                 s = 2 * pair + half
                 both[:, s * lane : (s + 1) * lane] = tile.astype(BF)
                 put_source(rhs, s, tile)
-        contract_left(lhs, 0, rhs, con)
+    for pi in range(pairs):
+        contract_left(lefts.at[pi], 0, sources.at[pi], con)
         mix(amat, con, mixes.at[pi], phys, lane)
-        return carry
-
-    lax.fori_loop(0, boths.shape[0], one, 0)
 
 
 def quarter_of(place, k, rows):
@@ -455,7 +454,7 @@
             stacked(pairs, rows, 4 * wide),
             stacked(groups * phys, phys * depth),
         ],
-        [rhs_scratch, con_scratch],
+        [pltpu.VMEM((pairs, 4 * wide, phys * lane), BF), con_scratch],
         pairs * (left_flops + mix_flops),
         pairs * wide * phys * groups * lane * 2,
     )

time: 68.6 us -> 68.5 us (level)
  transfers between devices with their start and end apart: 14 -> 14, of which waited for: 3 -> 3; matrix products, arithmetic and copies ran while one was open for 7% -> 7% of each run, Pallas kernels for 26% -> 25%
where the time goes in v6:
time: 68.5 us; the launch traced here: 68.3 us
  Pallas kernels  27.2 us (40%)
  starting transfers between devices  15.8 us (23%)
  blocking collectives  15.6 us (23%)
  local copies, waits for them, and re-layouts  4.87 us (7%)
  waiting for transfers between devices  1.83 us (3%)
  other arithmetic  1.27 us (2%)
  matrix products  0.98 us (1%)
  between operations  0.83 us (1%)
    pallas_call x7, Pallas kernels, call(): pl.pallas_call(kernel, out_shape=out_shapes, in_specs=specs, out_specs=[p...  27.2 us
    all_to_all x1, blocking collectives, body(): lax.all_to_all(line, both_axes, 0, 0, tiled=True).reshape(-1, lane)  15.6 us
    ppermute x10, starting transfers between devices, shift(): return lax.ppermute(value, 'term', [(t, t ^ k) for t in range(terms)])  7.27 us
    ppermute x2, starting transfers between devices, body(): lax.ppermute(wanted[a * each:(a + 1) * each], both_axes, swaps[a])  4.58 us
    ppermute x2, starting transfers between devices, body(): rights = [lax.ppermute(chosen[a], both_axes, swaps[a]) for a in range(span)]  3.94 us
    unnamed x8, local copies, waits for them, and re-layouts  3.4 us
    ppermute x10, waiting for transfers between devices, shift(): return lax.ppermute(value, 'term', [(t, t ^ k) for t in range(terms)])  1.82 us
  transfers between devices with their start and end apart: 14, of which 3 were waited for; matrix products, arithmetic and copies ran while one was open for 7% of the time, Pallas kernels for 25%

profile of v6, /device:TPU:0, one launch (start us, length us, event | category | flops | bytes accessed | tf_op | source)
XLA Modules:
  0.0 68.3 jit_solution(9082384273957281112)
XLA Ops:
  0.6 0.0 copy-start
  0.6 0.7 %convert_convert_fusion = (bf16[3]{0:T(256)(128)(2,1)S(1)}, bf16[1,3]{1,0:T(2,128)(2,1)S(1)}) fusion(s32[3]{0:T(128)} %param.13), kind=kLoop, calls=%fused_computation.41 | loop fusion | flops 6 | bytes 24 | tf_op jit(solution)/shard_map/squeeze | solution.py:416
  1.3 0.2 copy-done
  1.5 1.0 %fusion = bf16[3,16,16,32]{3,2,1,0:T(8,128)(2,1)S(1)} fusion(bf16[3,8,16,16]{3,2,1,0:T(8,128)(2,1)S(1)} %copy-done, s32[3,8]{1,0:T(4,128)} %param.12), kind=kOutput, calls=%fused_computation.1 | convolution fusion | flops 418560 | bytes 61536 | tf_op jit(solution)/shard_map/gtys,gtw->gysw/dot_general | solution.py:404
  2.5 0.2 reshape.184
  2.7 2.4 %collective-permute-start.2 = (bf16[64,512]{1,0:T(8,128)(2,1)S(1)}, bf16[64,512]{1,0:T(8,128)(2,1)S(1)}, u32[]{:S(2)}, u32[]{:S(2)}) collective-permute-start(bf16[64,512]{1,0:T(8,128)(2,1)S(1)} %fusion.3.refs_0_), channel_id=1, source_target_pairs={{0,3},{1,2},{2,1},{3,0},{4,7},{5,6},{6,5},{7,4},{8,11},{9,10},{10,... | collective-permute-start | bytes 196616 | tf_op jit(solution)/shard_map/ppermute | solution.py:413
  5.2 0.6 collective-permute-start.1
  5.8 0.0 collective-permute-start
  5.9 0.8 %copy.24 = s32[8,2]{1,0:T(8,128)S(1)} copy(s32[8,2]{0,1:T(2,128)} %param.8) | data formatting | bytes 128 | tf_op args[1]
  6.6 0.1 reshape.182
  6.7 0.2 convert_reduce_fusion
  6.9 0.1 select_reduce_fusion
  7.0 0.1 dynamic_slice.7
  7.1 0.1 fusion.12
  7.2 0.7 collective-permute-start.3
  7.9 0.0 copy-start.2
  7.9 3.9 %collective-permute-start.4 = (s32[2]{0:T(128)S(1)}, s32[2]{0:T(128)S(1)}, u32[]{:S(2)}, u32[]{:S(2)}) collective-permute-start(s32[2]{0:T(128)S(1)} %get-tuple-element.78), channel_id=1, source_target_pairs={{0,24},{1,17},{2,30},{3,23},{4,28},{5,21},{6,26},{7,19},{8,16},{9,... | collective-permute-start | bytes 32 | tf_op jit(solution)/shard_map/ppermute | solution.py:400
  11.8 2.4 %copy.26.right_env = bf16[8,26,4096]{2,1,0:T(8,128)(2,1)S(1)} copy(bf16[8,26,4096]{2,0,1:T(8,128)(2,1)} %param.10) | data formatting | bytes 3407872 | tf_op args[3]
  14.2 0.1 pad_add_fusion.1.asked
  14.3 0.0 collective-permute-done.2.refs_3_
  14.3 0.0 collective-permute-done.1.refs_2_
  14.3 0.0 collective-permute-done.refs_1_
  14.4 0.1 maximum_convert_fusion.names
  14.4 1.1 %shard_map.94 = (bf16[2,64,768]{2,1,0:T(8,128)(2,1)S(1)}, bf16[2,64,768]{2,1,0:T(8,128)(2,1)S(1)}) custom-call(s32[12]{0:T(128)S(1)} %maximum_convert_fusion.names, s32[4]{0:T(128)S(1)} %pad_add_fusion.1.asked, bf16[8,26,4096]{2,1,0:T(8,128)(2,1)S(1)} %copy.26.right_env), custom_call_target="tpu_custom_call" | custom-call | bytes 13312 | tf_op jit(solution)/shard_map/pallas_call | solution.py:343
  15.6 0.0 copy-start.1
  15.6 1.0 %collective-permute-start.5 = (bf16[2,64,768]{2,1,0:T(8,128)(2,1)S(1)}, bf16[2,64,768]{2,1,0:T(8,128)(2,1)S(1)}, u32[]{:S(2)}, u32[]{:S(2)}) collective-permute-start(bf16[2,64,768]{2,1,0:T(8,128)(2,1)S(1)} %get-tuple-element.39), channel_id=1, source_target_pairs={{0,0},{1,9},{2,6},{3,15},{4,4},{5,13},{6,2},{7,11},{8,8},{9,1},{10... | collective-permute-start | bytes 589832 | tf_op jit(solution)/shard_map/ppermute | solution.py:432
  16.6 3.0 %collective-permute-start.6 = (bf16[2,64,768]{2,1,0:T(8,128)(2,1)S(1)}, bf16[2,64,768]{2,1,0:T(8,128)(2,1)S(1)}, u32[]{:S(2)}, u32[]{:S(2)}) collective-permute-start(bf16[2,64,768]{2,1,0:T(8,128)(2,1)S(1)} %get-tuple-element.40), channel_id=1, source_target_pairs={{0,24},{1,17},{2,30},{3,23},{4,28},{5,21},{6,26},{7,19},{8,16},{9,... | collective-permute-start | bytes 589832 | tf_op jit(solution)/shard_map/ppermute | solution.py:432
  19.5 0.1 dynamic_slice.6.own
  19.6 1.0 %copy.27.left_env = bf16[8,26,4096]{2,1,0:T(8,128)(2,1)S(1)} copy(bf16[8,26,4096]{2,0,1:T(8,128)(2,1)S(1)} %copy-done.2) | data formatting | bytes 3407872 | tf_op jit(solution)/shard_map/optimization_barrier | solution.py:433
  20.6 9.0 %shard_map.95 = (bf16[2,1024,1536]{2,1,0:T(8,128)(2,1)S(1)}, bf16[2,64,2048]{2,1,0:T(8,128)(2,1)S(1)}, bf16[2,2048,256]{2,1,0:T(8,128)(2,1)S(1)}, bf16[192,512]{1,0:T(8,128)(2,1)S(1)}) custom-call(s32[4]{0:T(128)S(1)} %dynamic_slice.6.own, bf16[8,26,4096]{2,1,0:T(8,128)(2,1)S(1)} %copy.27.left_env, bf16[16,64,1024]{2,1,0:T(8,128)(2,1)S(1)} %bitcast.23, ...), custom_call_target="tpu_custom_call" | custom-call | flops 117440512 | bytes 98304 | tf_op jit(solution)/shard_map/pallas_call | solution.py:343
  29.6 0.0 collective-permute-done.6.refs_1_
  29.6 2.7 %shard_map.96 = (bf16[2,64,2048]{2,1,0:T(8,128)(2,1)S(1)}, f32[32,1,128]{2,1,0:T(1,128)S(1)}, bf16[2,128,1536]{2,1,0:T(8,128)(2,1)S(1)}, bf16[2,16,2048]{2,1,0:T...) custom-call(s32[1]{0:T(128)} %bitcast.place, ...), custom_call_target="tpu_custom_call" | custom-call | flops 12582912 | bytes 98304 | tf_op jit(solution)/shard_map/pallas_call | solution.py:343
  32.3 15.6 %all_to_all.5 = f32[32,1,128]{2,1,0:T(1,128)S(1)} all-to-all(f32[32,1,128]{2,1,0:T(1,128)S(1)} %get-tuple-element.48), channel_id=1, replica_groups=mesh['sec'=8,'term'=4] {'sec','term'}, dimensions={0} | all-to-all | bytes 32768 | tf_op jit(solution)/shard_map/all_to_all | solution.py:479
  47.9 3.3 %shard_map.97 = (bf16[3,16,2048]{2,1,0:T(8,128)(2,1)S(1)}, bf16[3,16,2048]{2,1,0:T(8,128)(2,1)S(1)}, bf16[256,2048]{1,0:T(8,128)(2,1)S(1)}) custom-call(s32[1]{0:T(128)} %bitcast.place, f32[32,128]{1,0:T(8,128)S(1)} %bitcast.25, bf16[2,64,2048]{2,1,0:T(8,128)(2,1)S(1)} %get-tuple-element.43.boths, bf16[2,64,2048]{2,1,0:T(8,128)(2,1)S(1)} %get-tuple-element.55.images, ...), custom_call_target="tpu_custom_call" | custom-call | flops 32505856 | bytes 16384 | tf_op jit(solution)/shard_map/pallas_call | solution.py:343
  51.2 0.6 collective-permute-start.8
  51.8 0.7 %collective-permute-start.9 = (bf16[3,16,2048]{2,1,0:T(8,128)(2,1)S(1)}, bf16[3,16,2048]{2,1,0:T(8,128)(2,1)S(1)}, u32[]{:S(2)}, u32[]{:S(2)}) collective-permute-start(bf16[3,16,2048]{2,1,0:T(8,128)(2,1)S(1)} %get-tuple-element.65), channel_id=1, source_target_pairs={{0,3},{1,2},{2,1},{3,0},{4,7},{5,6},{6,5},{7,4},{8,11},{9,10},{10,... | collective-permute-start | bytes 589832 | tf_op jit(solution)/shard_map/ppermute | solution.py:413
  52.5 3.3 %shard_map.98 = (bf16[1,16,2048]{2,1,0:T(8,128)(2,1)S(1)}, bf16[1,16,2048]{2,1,0:T(8,128)(2,1)S(1)}, bf16[256,2048]{1,0:T(8,128)(2,1)S(1)}) custom-call(s32[1]{0:T(128)} %bitcast.place, f32[32,128]{1,0:T(8,128)S(1)} %bitcast.26, bf16[2,64,2048]{2,1,0:T(8,128)(2,1)S(1)} %get-tuple-element.43.boths, bf16[2,64,2048]{2,1,0:T(8,128)(2,1)S(1)} %get-tuple-element.55.images, ...), custom_call_target="tpu_custom_call" | custom-call | flops 32505856 | bytes 16384 | tf_op jit(solution)/shard_map/pallas_call | solution.py:343
  55.9 0.9 %collective-permute-start.10 = (bf16[1,16,2048]{2,1,0:T(8,128)(2,1)S(1)}, bf16[1,16,2048]{2,1,0:T(8,128)(2,1)S(1)}, u32[]{:S(2)}, u32[]{:S(2)}) collective-permute-start(bf16[1,16,2048]{2,1,0:T(8,128)(2,1)S(1)} %get-tuple-element.68), channel_id=1, source_target_pairs={{0,2},{1,3},{2,0},{3,1},{4,6},{5,7},{6,4},{7,5},{8,10},{9,11},{10,... | collective-permute-start | bytes 196616 | tf_op jit(solution)/shard_map/ppermute | solution.py:413
  56.7 1.5 %collective-permute-start.11 = (bf16[1,16,2048]{2,1,0:T(8,128)(2,1)S(1)}, bf16[1,16,2048]{2,1,0:T(8,128)(2,1)S(1)}, u32[]{:S(2)}, u32[]{:S(2)}) collective-permute-start(bf16[1,16,2048]{2,1,0:T(8,128)(2,1)S(1)} %get-tuple-element.69), channel_id=1, source_target_pairs={{0,3},{1,2},{2,1},{3,0},{4,7},{5,6},{6,5},{7,4},{8,11},{9,10},{10,... | collective-permute-start | bytes 196616 | tf_op jit(solution)/shard_map/ppermute | solution.py:413
  58.2 5.1 %shard_map.99 = (bf16[2,16,2048]{2,1,0:T(8,128)(2,1)S(1)}, bf16[1,16,2048]{2,1,0:T(8,128)(2,1)S(1)}, bf16[1,16,2048]{2,1,0:T(8,128)(2,1)S(1)}) custom-call(s32[1]{0:T(128)} %bitcast.place, bf16[2,2048,256]{2,1,0:T(8,128)(2,1)S(1)} %get-tuple-element.52.lefts, bf16[192,512]{1,0:T(8,128)(2,1)S(1)} %get-tuple-element.53.amat, ...), custom_call_target="tpu_custom_call" | custom-call | flops 65011712 | bytes 16384 | tf_op jit(solution)/shard_map/pallas_call | solution.py:343
  63.3 1.0 %collective-permute-done.10.refs_2_ = bf16[1,16,2048]{2,1,0:T(8,128)(2,1)S(1)} collective-permute-done((bf16[1,16,2048]{2,1,0:T(8,128)(2,1)S(1)}, bf16[1,16,2048]{2,1,0:T(8,128)(2,1)S(1)}, u32[]{:S(2)}, u32[]{:S(2)}) %collective-permute-start.10) | collective-permute-done | bytes 65568 | tf_op jit(solution)/shard_map/ppermute | solution.py:413
  64.3 0.0 collective-permute-done.11.refs_3_
  64.3 0.5 collective-permute-start.13
  64.8 0.1 pad_add_fusion.table
  64.9 0.7 collective-permute-done.12.refs_4_
  65.5 0.2 collective-permute-done.13.refs_5_
  65.7 0.0 collective-permute-done.7.chip_first
  65.7 2.5 %shard_map.100 = (bf16[16,16,1024]{2,1,0:T(8,128)(2,1)}, bf16[16,16,1024]{2,1,0:T(8,128)(2,1)}, bf16[16,16,1024]{2,1,0:T(8,128)(2,1)}) custom-call(s32[17]{0:T(128)S(1)} %pad_add_fusion.table, f32[32,128]{1,0:T(8,128)S(1)} %bitcast.27, bf16[16,64,1024]{2,1,0:T(8,128)(2,1)S(1)} %bitcast.24, bf16[2,16,2048]{2,1,0:T(8,128)(2,1)S(1)} %get-tuple-element.50.own_first, ...), custom_call_target="tpu_custom_call" | custom-call | bytes 49152 | tf_op jit(solution)/shard_map/pallas_call | solution.py:343
  (15 shorter events, 0.1 us)
Async XLA Ops:
  0.6 0.9 %copy-start = (bf16[3,8,16,16]{3,2,1,0:T(8,128)(2,1)S(1)}, bf16[3,8,16,16]{3,2,1,0:T(8,128)(2,1)}, u32[]{:S(2)}) copy-start(bf16[3,8,16,16]{3,2,1,0:T(8,128)(2,1)} %param.11) | copy-start | bytes 36868
  2.7 11.6 %collective-permute-start.2 = (bf16[64,512]{1,0:T(8,128)(2,1)S(1)}, bf16[64,512]{1,0:T(8,128)(2,1)S(1)}, u32[]{:S(2)}, u32[]{:S(2)}) collective-permute-start(bf16[64,512]{1,0:T(8,128)(2,1)S(1)} %fusion.3.refs_0_), channel_id=1, source_target_pairs={{0,3},{1,2},{2,1},{3,0},{4,7},{5,6},{6,5},{7,4},{8,11},{9,10},{10,... | collective-permute-start | bytes 196616 | tf_op jit(solution)/shard_map/ppermute | solution.py:413
  5.2 9.1 %collective-permute-start.1 = (bf16[64,512]{1,0:T(8,128)(2,1)S(1)}, bf16[64,512]{1,0:T(8,128)(2,1)S(1)}, u32[]{:S(2)}, u32[]{:S(2)}) collective-permute-start(bf16[64,512]{1,0:T(8,128)(2,1)S(1)} %fusion.3.refs_0_), channel_id=1, source_target_pairs={{0,2},{1,3},{2,0},{3,1},{4,6},{5,7},{6,4},{7,5},{8,10},{9,11},{10,... | collective-permute-start | bytes 196616 | tf_op jit(solution)/shard_map/ppermute | solution.py:413
  5.8 8.5 %collective-permute-start = (bf16[64,512]{1,0:T(8,128)(2,1)S(1)}, bf16[64,512]{1,0:T(8,128)(2,1)S(1)}, u32[]{:S(2)}, u32[]{:S(2)}) collective-permute-start(bf16[64,512]{1,0:T(8,128)(2,1)S(1)} %fusion.3.refs_0_), channel_id=1, source_target_pairs={{0,1},{1,0},{2,3},{3,2},{4,5},{5,4},{6,7},{7,6},{8,9},{9,8},{10,11... | collective-permute-start | bytes 196616 | tf_op jit(solution)/shard_map/ppermute | solution.py:413
  7.2 7.0 %collective-permute-start.3 = (s32[2]{0:T(128)S(1)}, s32[2]{0:T(128)S(1)}, u32[]{:S(2)}, u32[]{:S(2)}) collective-permute-start(s32[2]{0:T(128)S(1)} %get-tuple-element.77), channel_id=1, source_target_pairs={{0,0},{1,9},{2,6},{3,15},{4,4},{5,13},{6,2},{7,11},{8,8},{9,1},{10... | collective-permute-start | bytes 32 | tf_op jit(solution)/shard_map/ppermute | solution.py:400
  7.9 11.7 %copy-start.2 = (bf16[8,26,4096]{2,0,1:T(8,128)(2,1)S(1)}, bf16[8,26,4096]{2,0,1:T(8,128)(2,1)}, u32[]{:S(2)}) copy-start(bf16[8,26,4096]{2,0,1:T(8,128)(2,1)} %param.9) | copy-start | bytes 5111812
  7.9 6.4 %collective-permute-start.4 = (s32[2]{0:T(128)S(1)}, s32[2]{0:T(128)S(1)}, u32[]{:S(2)}, u32[]{:S(2)}) collective-permute-start(s32[2]{0:T(128)S(1)} %get-tuple-element.78), channel_id=1, source_target_pairs={{0,24},{1,17},{2,30},{3,23},{4,28},{5,21},{6,26},{7,19},{8,16},{9,... | collective-permute-start | bytes 32 | tf_op jit(solution)/shard_map/ppermute | solution.py:400
  15.6 5.0 %copy-start.1 = (bf16[8,2,64,1024]{3,2,1,0:T(8,128)(2,1)S(1)}, bf16[8,2,64,1024]{3,2,1,0:T(8,128)(2,1)}, u32[]{:S(2)}) copy-start(bf16[8,2,64,1024]{3,2,1,0:T(8,128)(2,1)} %param.7) | copy-start | bytes 6291460
  15.6 14.0 %collective-permute-start.5 = (bf16[2,64,768]{2,1,0:T(8,128)(2,1)S(1)}, bf16[2,64,768]{2,1,0:T(8,128)(2,1)S(1)}, u32[]{:S(2)}, u32[]{:S(2)}) collective-permute-start(bf16[2,64,768]{2,1,0:T(8,128)(2,1)S(1)} %get-tuple-element.39), channel_id=1, source_target_pairs={{0,0},{1,9},{2,6},{3,15},{4,4},{5,13},{6,2},{7,11},{8,8},{9,1},{10... | collective-permute-start | bytes 589832 | tf_op jit(solution)/shard_map/ppermute | solution.py:432
  16.6 13.0 %collective-permute-start.6 = (bf16[2,64,768]{2,1,0:T(8,128)(2,1)S(1)}, bf16[2,64,768]{2,1,0:T(8,128)(2,1)S(1)}, u32[]{:S(2)}, u32[]{:S(2)}) collective-permute-start(bf16[2,64,768]{2,1,0:T(8,128)(2,1)S(1)} %get-tuple-element.40), channel_id=1, source_target_pairs={{0,24},{1,17},{2,30},{3,23},{4,28},{5,21},{6,26},{7,19},{8,16},{9,... | collective-permute-start | bytes 589832 | tf_op jit(solution)/shard_map/ppermute | solution.py:432
  51.2 14.5 %collective-permute-start.8 = (bf16[3,16,2048]{2,1,0:T(8,128)(2,1)S(1)}, bf16[3,16,2048]{2,1,0:T(8,128)(2,1)S(1)}, u32[]{:S(2)}, u32[]{:S(2)}) collective-permute-start(bf16[3,16,2048]{2,1,0:T(8,128)(2,1)S(1)} %get-tuple-element.64), channel_id=1, source_target_pairs={{0,2},{1,3},{2,0},{3,1},{4,6},{5,7},{6,4},{7,5},{8,10},{9,11},{10,... | collective-permute-start | bytes 589832 | tf_op jit(solution)/shard_map/ppermute | solution.py:413
  51.8 13.9 %collective-permute-start.9 = (bf16[3,16,2048]{2,1,0:T(8,128)(2,1)S(1)}, bf16[3,16,2048]{2,1,0:T(8,128)(2,1)S(1)}, u32[]{:S(2)}, u32[]{:S(2)}) collective-permute-start(bf16[3,16,2048]{2,1,0:T(8,128)(2,1)S(1)} %get-tuple-element.65), channel_id=1, source_target_pairs={{0,3},{1,2},{2,1},{3,0},{4,7},{5,6},{6,5},{7,4},{8,11},{9,10},{10,... | collective-permute-start | bytes 589832 | tf_op jit(solution)/shard_map/ppermute | solution.py:413
  55.9 8.4 %collective-permute-start.10 = (bf16[1,16,2048]{2,1,0:T(8,128)(2,1)S(1)}, bf16[1,16,2048]{2,1,0:T(8,128)(2,1)S(1)}, u32[]{:S(2)}, u32[]{:S(2)}) collective-permute-start(bf16[1,16,2048]{2,1,0:T(8,128)(2,1)S(1)} %get-tuple-element.68), channel_id=1, source_target_pairs={{0,2},{1,3},{2,0},{3,1},{4,6},{5,7},{6,4},{7,5},{8,10},{9,11},{10,... | collective-permute-start | bytes 196616 | tf_op jit(solution)/shard_map/ppermute | solution.py:413
  56.7 7.6 %collective-permute-start.11 = (bf16[1,16,2048]{2,1,0:T(8,128)(2,1)S(1)}, bf16[1,16,2048]{2,1,0:T(8,128)(2,1)S(1)}, u32[]{:S(2)}, u32[]{:S(2)}) collective-permute-start(bf16[1,16,2048]{2,1,0:T(8,128)(2,1)S(1)} %get-tuple-element.69), channel_id=1, source_target_pairs={{0,3},{1,2},{2,1},{3,0},{4,7},{5,6},{6,5},{7,4},{8,11},{9,10},{10,... | collective-permute-start | bytes 196616 | tf_op jit(solution)/shard_map/ppermute | solution.py:413
  58.2 7.5 %collective-permute-start.7 = (bf16[2,16,2048]{2,1,0:T(8,128)(2,1)S(1)}, bf16[2,16,2048]{2,1,0:T(8,128)(2,1)S(1)}, u32[]{:S(2)}, u32[]{:S(2)}) collective-permute-start(bf16[2,16,2048]{2,1,0:T(8,128)(2,1)S(1)} %get-tuple-element.51), channel_id=1, source_target_pairs={{0,1},{1,0},{2,3},{3,2},{4,5},{5,4},{6,7},{7,6},{8,9},{9,8},{10,11... | collective-permute-start | bytes 393224 | tf_op jit(solution)/shard_map/ppermute | solution.py:413
  64.3 1.3 %collective-permute-start.12 = (bf16[1,16,2048]{2,1,0:T(8,128)(2,1)S(1)}, bf16[1,16,2048]{2,1,0:T(8,128)(2,1)S(1)}, u32[]{:S(2)}, u32[]{:S(2)}) collective-permute-start(bf16[1,16,2048]{2,1,0:T(8,128)(2,1)S(1)} %get-tuple-element.70), channel_id=1, source_target_pairs={{0,1},{1,0},{2,3},{3,2},{4,5},{5,4},{6,7},{7,6},{8,9},{9,8},{10,11... | collective-permute-start | bytes 196616 | tf_op jit(solution)/shard_map/ppermute | solution.py:413
  64.3 1.4 %collective-permute-start.13 = (bf16[1,16,2048]{2,1,0:T(8,128)(2,1)S(1)}, bf16[1,16,2048]{2,1,0:T(8,128)(2,1)S(1)}, u32[]{:S(2)}, u32[]{:S(2)}) collective-permute-start(bf16[1,16,2048]{2,1,0:T(8,128)(2,1)S(1)} %get-tuple-element.71), channel_id=1, source_target_pairs={{0,1},{1,0},{2,3},{3,2},{4,5},{5,4},{6,7},{7,6},{8,9},{9,8},{10,11... | collective-permute-start | bytes 196616 | tf_op jit(solution)/shard_map/ppermute | solution.py:413

commit v7 on v6

--- a/solution.py
+++ b/solution.py
@@ -163,10 +163,11 @@
     at = lax.broadcasted_iota(jnp.int32, (1, lane), 1)
     row = jnp.zeros((1, lane), F32)
     for pi in range(pairs):
-        both, image = boths.at[pi], images.at[pi]
         fill_right(rmats.at[pi], tiles_of(rights, kinds[pi], lane), lane)
-        acc = accs.at[pi]
-        contract_right(mixes.at[pi], rmats.at[pi], acc)
+    for pi in range(pairs):
+        contract_right(mixes.at[pi], rmats.at[pi], accs.at[pi])
+    for pi in range(pairs):
+        both, image, acc = boths.at[pi], images.at[pi], accs.at[pi]
         norm = jnp.zeros((wide, lane), F32)
         corr = jnp.zeros((wide, lane), F32)
         for y in range(phys):

time: 68.5 us -> 68.5 us (level)
  no operation moved by 1% of the time
where the time goes in v7:
time: 68.5 us; the launch traced here: 68.3 us
  Pallas kernels  27.2 us (40%)
  starting transfers between devices  15.8 us (23%)
  blocking collectives  15.5 us (23%)
  local copies, waits for them, and re-layouts  4.87 us (7%)
  waiting for transfers between devices  1.83 us (3%)
  other arithmetic  1.27 us (2%)
  matrix products  0.98 us (1%)
  between operations  0.83 us (1%)
    pallas_call x7, Pallas kernels, call(): pl.pallas_call(kernel, out_shape=out_shapes, in_specs=specs, out_specs=[p...  27.2 us
    all_to_all x1, blocking collectives, body(): lax.all_to_all(line, both_axes, 0, 0, tiled=True).reshape(-1, lane)  15.5 us
    ppermute x10, starting transfers between devices, shift(): return lax.ppermute(value, 'term', [(t, t ^ k) for t in range(terms)])  7.27 us
    ppermute x2, starting transfers between devices, body(): lax.ppermute(wanted[a * each:(a + 1) * each], both_axes, swaps[a])  4.58 us
    ppermute x2, starting transfers between devices, body(): rights = [lax.ppermute(chosen[a], both_axes, swaps[a]) for a in range(span)]  3.94 us
    unnamed x8, local copies, waits for them, and re-layouts  3.4 us
    ppermute x10, waiting for transfers between devices, shift(): return lax.ppermute(value, 'term', [(t, t ^ k) for t in range(terms)])  1.82 us
  transfers between devices with their start and end apart: 14, of which 3 were waited for; matrix products, arithmetic and copies ran while one was open for 7% of the time, Pallas kernels for 25%

profile of v7, /device:TPU:0, one launch (start us, length us, event | category | flops | bytes accessed | tf_op | source)
XLA Modules:
  0.0 68.3 jit_solution(9082384273957281112)
XLA Ops:
  0.6 0.0 copy-start
  0.6 0.7 %convert_convert_fusion = (bf16[3]{0:T(256)(128)(2,1)S(1)}, bf16[1,3]{1,0:T(2,128)(2,1)S(1)}) fusion(s32[3]{0:T(128)} %param.13), kind=kLoop, calls=%fused_computation.41 | loop fusion | flops 6 | bytes 24 | tf_op jit(solution)/shard_map/squeeze | solution.py:417
  1.3 0.2 copy-done
  1.5 1.0 %fusion = bf16[3,16,16,32]{3,2,1,0:T(8,128)(2,1)S(1)} fusion(bf16[3,8,16,16]{3,2,1,0:T(8,128)(2,1)S(1)} %copy-done, s32[3,8]{1,0:T(4,128)} %param.12), kind=kOutput, calls=%fused_computation.1 | convolution fusion | flops 418560 | bytes 61536 | tf_op jit(solution)/shard_map/gtys,gtw->gysw/dot_general | solution.py:405
  2.5 0.2 reshape.184
  2.7 2.4 %collective-permute-start.2 = (bf16[64,512]{1,0:T(8,128)(2,1)S(1)}, bf16[64,512]{1,0:T(8,128)(2,1)S(1)}, u32[]{:S(2)}, u32[]{:S(2)}) collective-permute-start(bf16[64,512]{1,0:T(8,128)(2,1)S(1)} %fusion.3.refs_0_), channel_id=1, source_target_pairs={{0,3},{1,2},{2,1},{3,0},{4,7},{5,6},{6,5},{7,4},{8,11},{9,10},{10,... | collective-permute-start | bytes 196616 | tf_op jit(solution)/shard_map/ppermute | solution.py:414
  5.2 0.6 collective-permute-start.1
  5.8 0.0 collective-permute-start
  5.9 0.8 %copy.24 = s32[8,2]{1,0:T(8,128)S(1)} copy(s32[8,2]{0,1:T(2,128)} %param.8) | data formatting | bytes 128 | tf_op args[1]
  6.6 0.1 reshape.182
  6.7 0.2 convert_reduce_fusion
  6.9 0.1 select_reduce_fusion
  7.0 0.1 dynamic_slice.7
  7.1 0.1 fusion.12
  7.2 0.7 collective-permute-start.3
  7.9 0.0 copy-start.2
  7.9 3.9 %collective-permute-start.4 = (s32[2]{0:T(128)S(1)}, s32[2]{0:T(128)S(1)}, u32[]{:S(2)}, u32[]{:S(2)}) collective-permute-start(s32[2]{0:T(128)S(1)} %get-tuple-element.78), channel_id=1, source_target_pairs={{0,24},{1,17},{2,30},{3,23},{4,28},{5,21},{6,26},{7,19},{8,16},{9,... | collective-permute-start | bytes 32 | tf_op jit(solution)/shard_map/ppermute | solution.py:401
  11.8 2.4 %copy.26.right_env = bf16[8,26,4096]{2,1,0:T(8,128)(2,1)S(1)} copy(bf16[8,26,4096]{2,0,1:T(8,128)(2,1)} %param.10) | data formatting | bytes 3407872 | tf_op args[3]
  14.2 0.1 pad_add_fusion.1.asked
  14.3 0.0 collective-permute-done.2.refs_3_
  14.3 0.0 collective-permute-done.1.refs_2_
  14.3 0.0 collective-permute-done.refs_1_
  14.4 0.1 maximum_convert_fusion.names
  14.4 1.1 %shard_map.94 = (bf16[2,64,768]{2,1,0:T(8,128)(2,1)S(1)}, bf16[2,64,768]{2,1,0:T(8,128)(2,1)S(1)}) custom-call(s32[12]{0:T(128)S(1)} %maximum_convert_fusion.names, s32[4]{0:T(128)S(1)} %pad_add_fusion.1.asked, bf16[8,26,4096]{2,1,0:T(8,128)(2,1)S(1)} %copy.26.right_env), custom_call_target="tpu_custom_call" | custom-call | bytes 13312 | tf_op jit(solution)/shard_map/pallas_call | solution.py:344
  15.6 0.0 copy-start.1
  15.6 1.0 %collective-permute-start.5 = (bf16[2,64,768]{2,1,0:T(8,128)(2,1)S(1)}, bf16[2,64,768]{2,1,0:T(8,128)(2,1)S(1)}, u32[]{:S(2)}, u32[]{:S(2)}) collective-permute-start(bf16[2,64,768]{2,1,0:T(8,128)(2,1)S(1)} %get-tuple-element.39), channel_id=1, source_target_pairs={{0,0},{1,9},{2,6},{3,15},{4,4},{5,13},{6,2},{7,11},{8,8},{9,1},{10... | collective-permute-start | bytes 589832 | tf_op jit(solution)/shard_map/ppermute | solution.py:433
  16.6 3.0 %collective-permute-start.6 = (bf16[2,64,768]{2,1,0:T(8,128)(2,1)S(1)}, bf16[2,64,768]{2,1,0:T(8,128)(2,1)S(1)}, u32[]{:S(2)}, u32[]{:S(2)}) collective-permute-start(bf16[2,64,768]{2,1,0:T(8,128)(2,1)S(1)} %get-tuple-element.40), channel_id=1, source_target_pairs={{0,24},{1,17},{2,30},{3,23},{4,28},{5,21},{6,26},{7,19},{8,16},{9,... | collective-permute-start | bytes 589832 | tf_op jit(solution)/shard_map/ppermute | solution.py:433
  19.5 0.1 dynamic_slice.6.own
  19.6 1.0 %copy.27.left_env = bf16[8,26,4096]{2,1,0:T(8,128)(2,1)S(1)} copy(bf16[8,26,4096]{2,0,1:T(8,128)(2,1)S(1)} %copy-done.2) | data formatting | bytes 3407872 | tf_op jit(solution)/shard_map/optimization_barrier | solution.py:434
  20.6 9.0 %shard_map.95 = (bf16[2,1024,1536]{2,1,0:T(8,128)(2,1)S(1)}, bf16[2,64,2048]{2,1,0:T(8,128)(2,1)S(1)}, bf16[2,2048,256]{2,1,0:T(8,128)(2,1)S(1)}, bf16[192,512]{1,0:T(8,128)(2,1)S(1)}) custom-call(s32[4]{0:T(128)S(1)} %dynamic_slice.6.own, bf16[8,26,4096]{2,1,0:T(8,128)(2,1)S(1)} %copy.27.left_env, bf16[16,64,1024]{2,1,0:T(8,128)(2,1)S(1)} %bitcast.23, ...), custom_call_target="tpu_custom_call" | custom-call | flops 117440512 | bytes 98304 | tf_op jit(solution)/shard_map/pallas_call | solution.py:344
  29.6 0.0 collective-permute-done.6.refs_1_
  29.6 2.7 %shard_map.96 = (bf16[2,64,2048]{2,1,0:T(8,128)(2,1)S(1)}, f32[32,1,128]{2,1,0:T(1,128)S(1)}, bf16[2,128,1536]{2,1,0:T(8,128)(2,1)S(1)}, bf16[2,16,2048]{2,1,0:T...) custom-call(s32[1]{0:T(128)} %bitcast.place, ...), custom_call_target="tpu_custom_call" | custom-call | flops 12582912 | bytes 98304 | tf_op jit(solution)/shard_map/pallas_call | solution.py:344
  32.3 15.5 %all_to_all.5 = f32[32,1,128]{2,1,0:T(1,128)S(1)} all-to-all(f32[32,1,128]{2,1,0:T(1,128)S(1)} %get-tuple-element.48), channel_id=1, replica_groups=mesh['sec'=8,'term'=4] {'sec','term'}, dimensions={0} | all-to-all | bytes 32768 | tf_op jit(solution)/shard_map/all_to_all | solution.py:480
  47.9 3.3 %shard_map.97 = (bf16[3,16,2048]{2,1,0:T(8,128)(2,1)S(1)}, bf16[3,16,2048]{2,1,0:T(8,128)(2,1)S(1)}, bf16[256,2048]{1,0:T(8,128)(2,1)S(1)}) custom-call(s32[1]{0:T(128)} %bitcast.place, f32[32,128]{1,0:T(8,128)S(1)} %bitcast.25, bf16[2,64,2048]{2,1,0:T(8,128)(2,1)S(1)} %get-tuple-element.43.boths, bf16[2,64,2048]{2,1,0:T(8,128)(2,1)S(1)} %get-tuple-element.55.images, ...), custom_call_target="tpu_custom_call" | custom-call | flops 32505856 | bytes 16384 | tf_op jit(solution)/shard_map/pallas_call | solution.py:344
  51.2 0.6 collective-permute-start.8
  51.8 0.7 %collective-permute-start.9 = (bf16[3,16,2048]{2,1,0:T(8,128)(2,1)S(1)}, bf16[3,16,2048]{2,1,0:T(8,128)(2,1)S(1)}, u32[]{:S(2)}, u32[]{:S(2)}) collective-permute-start(bf16[3,16,2048]{2,1,0:T(8,128)(2,1)S(1)} %get-tuple-element.65), channel_id=1, source_target_pairs={{0,3},{1,2},{2,1},{3,0},{4,7},{5,6},{6,5},{7,4},{8,11},{9,10},{10,... | collective-permute-start | bytes 589832 | tf_op jit(solution)/shard_map/ppermute | solution.py:414
  52.5 3.3 %shard_map.98 = (bf16[1,16,2048]{2,1,0:T(8,128)(2,1)S(1)}, bf16[1,16,2048]{2,1,0:T(8,128)(2,1)S(1)}, bf16[256,2048]{1,0:T(8,128)(2,1)S(1)}) custom-call(s32[1]{0:T(128)} %bitcast.place, f32[32,128]{1,0:T(8,128)S(1)} %bitcast.26, bf16[2,64,2048]{2,1,0:T(8,128)(2,1)S(1)} %get-tuple-element.43.boths, bf16[2,64,2048]{2,1,0:T(8,128)(2,1)S(1)} %get-tuple-element.55.images, ...), custom_call_target="tpu_custom_call" | custom-call | flops 32505856 | bytes 16384 | tf_op jit(solution)/shard_map/pallas_call | solution.py:344
  55.8 0.9 %collective-permute-start.10 = (bf16[1,16,2048]{2,1,0:T(8,128)(2,1)S(1)}, bf16[1,16,2048]{2,1,0:T(8,128)(2,1)S(1)}, u32[]{:S(2)}, u32[]{:S(2)}) collective-permute-start(bf16[1,16,2048]{2,1,0:T(8,128)(2,1)S(1)} %get-tuple-element.68), channel_id=1, source_target_pairs={{0,2},{1,3},{2,0},{3,1},{4,6},{5,7},{6,4},{7,5},{8,10},{9,11},{10,... | collective-permute-start | bytes 196616 | tf_op jit(solution)/shard_map/ppermute | solution.py:414
  56.7 1.5 %collective-permute-start.11 = (bf16[1,16,2048]{2,1,0:T(8,128)(2,1)S(1)}, bf16[1,16,2048]{2,1,0:T(8,128)(2,1)S(1)}, u32[]{:S(2)}, u32[]{:S(2)}) collective-permute-start(bf16[1,16,2048]{2,1,0:T(8,128)(2,1)S(1)} %get-tuple-element.69), channel_id=1, source_target_pairs={{0,3},{1,2},{2,1},{3,0},{4,7},{5,6},{6,5},{7,4},{8,11},{9,10},{10,... | collective-permute-start | bytes 196616 | tf_op jit(solution)/shard_map/ppermute | solution.py:414
  58.2 0.0 collective-permute-start.7
  58.2 5.1 %shard_map.99 = (bf16[2,16,2048]{2,1,0:T(8,128)(2,1)S(1)}, bf16[1,16,2048]{2,1,0:T(8,128)(2,1)S(1)}, bf16[1,16,2048]{2,1,0:T(8,128)(2,1)S(1)}) custom-call(s32[1]{0:T(128)} %bitcast.place, bf16[2,2048,256]{2,1,0:T(8,128)(2,1)S(1)} %get-tuple-element.52.lefts, bf16[192,512]{1,0:T(8,128)(2,1)S(1)} %get-tuple-element.53.amat, ...), custom_call_target="tpu_custom_call" | custom-call | flops 65011712 | bytes 16384 | tf_op jit(solution)/shard_map/pallas_call | solution.py:344
  63.3 1.0 %collective-permute-done.10.refs_2_ = bf16[1,16,2048]{2,1,0:T(8,128)(2,1)S(1)} collective-permute-done((bf16[1,16,2048]{2,1,0:T(8,128)(2,1)S(1)}, bf16[1,16,2048]{2,1,0:T(8,128)(2,1)S(1)}, u32[]{:S(2)}, u32[]{:S(2)}) %collective-permute-start.10) | collective-permute-done | bytes 65568 | tf_op jit(solution)/shard_map/ppermute | solution.py:414
  64.3 0.5 collective-permute-start.13
  64.8 0.1 pad_add_fusion.table
  64.9 0.7 collective-permute-done.12.refs_4_
  65.5 0.2 collective-permute-done.13.refs_5_
  65.7 0.0 collective-permute-done.7.chip_first
  65.7 2.5 %shard_map.100 = (bf16[16,16,1024]{2,1,0:T(8,128)(2,1)}, bf16[16,16,1024]{2,1,0:T(8,128)(2,1)}, bf16[16,16,1024]{2,1,0:T(8,128)(2,1)}) custom-call(s32[17]{0:T(128)S(1)} %pad_add_fusion.table, f32[32,128]{1,0:T(8,128)S(1)} %bitcast.27, bf16[16,64,1024]{2,1,0:T(8,128)(2,1)S(1)} %bitcast.24, bf16[2,16,2048]{2,1,0:T(8,128)(2,1)S(1)} %get-tuple-element.50.own_first, ...), custom_call_target="tpu_custom_call" | custom-call | bytes 49152 | tf_op jit(solution)/shard_map/pallas_call | solution.py:344
  (15 shorter events, 0.1 us)
Async XLA Ops:
  0.6 0.9 %copy-start = (bf16[3,8,16,16]{3,2,1,0:T(8,128)(2,1)S(1)}, bf16[3,8,16,16]{3,2,1,0:T(8,128)(2,1)}, u32[]{:S(2)}) copy-start(bf16[3,8,16,16]{3,2,1,0:T(8,128)(2,1)} %param.11) | copy-start | bytes 36868
  2.7 11.6 %collective-permute-start.2 = (bf16[64,512]{1,0:T(8,128)(2,1)S(1)}, bf16[64,512]{1,0:T(8,128)(2,1)S(1)}, u32[]{:S(2)}, u32[]{:S(2)}) collective-permute-start(bf16[64,512]{1,0:T(8,128)(2,1)S(1)} %fusion.3.refs_0_), channel_id=1, source_target_pairs={{0,3},{1,2},{2,1},{3,0},{4,7},{5,6},{6,5},{7,4},{8,11},{9,10},{10,... | collective-permute-start | bytes 196616 | tf_op jit(solution)/shard_map/ppermute | solution.py:414
  5.2 9.1 %collective-permute-start.1 = (bf16[64,512]{1,0:T(8,128)(2,1)S(1)}, bf16[64,512]{1,0:T(8,128)(2,1)S(1)}, u32[]{:S(2)}, u32[]{:S(2)}) collective-permute-start(bf16[64,512]{1,0:T(8,128)(2,1)S(1)} %fusion.3.refs_0_), channel_id=1, source_target_pairs={{0,2},{1,3},{2,0},{3,1},{4,6},{5,7},{6,4},{7,5},{8,10},{9,11},{10,... | collective-permute-start | bytes 196616 | tf_op jit(solution)/shard_map/ppermute | solution.py:414
  5.8 8.5 %collective-permute-start = (bf16[64,512]{1,0:T(8,128)(2,1)S(1)}, bf16[64,512]{1,0:T(8,128)(2,1)S(1)}, u32[]{:S(2)}, u32[]{:S(2)}) collective-permute-start(bf16[64,512]{1,0:T(8,128)(2,1)S(1)} %fusion.3.refs_0_), channel_id=1, source_target_pairs={{0,1},{1,0},{2,3},{3,2},{4,5},{5,4},{6,7},{7,6},{8,9},{9,8},{10,11... | collective-permute-start | bytes 196616 | tf_op jit(solution)/shard_map/ppermute | solution.py:414
  7.2 7.0 %collective-permute-start.3 = (s32[2]{0:T(128)S(1)}, s32[2]{0:T(128)S(1)}, u32[]{:S(2)}, u32[]{:S(2)}) collective-permute-start(s32[2]{0:T(128)S(1)} %get-tuple-element.77), channel_id=1, source_target_pairs={{0,0},{1,9},{2,6},{3,15},{4,4},{5,13},{6,2},{7,11},{8,8},{9,1},{10... | collective-permute-start | bytes 32 | tf_op jit(solution)/shard_map/ppermute | solution.py:401
  7.9 11.7 %copy-start.2 = (bf16[8,26,4096]{2,0,1:T(8,128)(2,1)S(1)}, bf16[8,26,4096]{2,0,1:T(8,128)(2,1)}, u32[]{:S(2)}) copy-start(bf16[8,26,4096]{2,0,1:T(8,128)(2,1)} %param.9) | copy-start | bytes 5111812
  7.9 6.4 %collective-permute-start.4 = (s32[2]{0:T(128)S(1)}, s32[2]{0:T(128)S(1)}, u32[]{:S(2)}, u32[]{:S(2)}) collective-permute-start(s32[2]{0:T(128)S(1)} %get-tuple-element.78), channel_id=1, source_target_pairs={{0,24},{1,17},{2,30},{3,23},{4,28},{5,21},{6,26},{7,19},{8,16},{9,... | collective-permute-start | bytes 32 | tf_op jit(solution)/shard_map/ppermute | solution.py:401
  15.6 5.0 %copy-start.1 = (bf16[8,2,64,1024]{3,2,1,0:T(8,128)(2,1)S(1)}, bf16[8,2,64,1024]{3,2,1,0:T(8,128)(2,1)}, u32[]{:S(2)}) copy-start(bf16[8,2,64,1024]{3,2,1,0:T(8,128)(2,1)} %param.7) | copy-start | bytes 6291460
  15.6 14.0 %collective-permute-start.5 = (bf16[2,64,768]{2,1,0:T(8,128)(2,1)S(1)}, bf16[2,64,768]{2,1,0:T(8,128)(2,1)S(1)}, u32[]{:S(2)}, u32[]{:S(2)}) collective-permute-start(bf16[2,64,768]{2,1,0:T(8,128)(2,1)S(1)} %get-tuple-element.39), channel_id=1, source_target_pairs={{0,0},{1,9},{2,6},{3,15},{4,4},{5,13},{6,2},{7,11},{8,8},{9,1},{10... | collective-permute-start | bytes 589832 | tf_op jit(solution)/shard_map/ppermute | solution.py:433
  16.6 13.0 %collective-permute-start.6 = (bf16[2,64,768]{2,1,0:T(8,128)(2,1)S(1)}, bf16[2,64,768]{2,1,0:T(8,128)(2,1)S(1)}, u32[]{:S(2)}, u32[]{:S(2)}) collective-permute-start(bf16[2,64,768]{2,1,0:T(8,128)(2,1)S(1)} %get-tuple-element.40), channel_id=1, source_target_pairs={{0,24},{1,17},{2,30},{3,23},{4,28},{5,21},{6,26},{7,19},{8,16},{9,... | collective-permute-start | bytes 589832 | tf_op jit(solution)/shard_map/ppermute | solution.py:433
  51.2 14.5 %collective-permute-start.8 = (bf16[3,16,2048]{2,1,0:T(8,128)(2,1)S(1)}, bf16[3,16,2048]{2,1,0:T(8,128)(2,1)S(1)}, u32[]{:S(2)}, u32[]{:S(2)}) collective-permute-start(bf16[3,16,2048]{2,1,0:T(8,128)(2,1)S(1)} %get-tuple-element.64), channel_id=1, source_target_pairs={{0,2},{1,3},{2,0},{3,1},{4,6},{5,7},{6,4},{7,5},{8,10},{9,11},{10,... | collective-permute-start | bytes 589832 | tf_op jit(solution)/shard_map/ppermute | solution.py:414
  51.8 13.9 %collective-permute-start.9 = (bf16[3,16,2048]{2,1,0:T(8,128)(2,1)S(1)}, bf16[3,16,2048]{2,1,0:T(8,128)(2,1)S(1)}, u32[]{:S(2)}, u32[]{:S(2)}) collective-permute-start(bf16[3,16,2048]{2,1,0:T(8,128)(2,1)S(1)} %get-tuple-element.65), channel_id=1, source_target_pairs={{0,3},{1,2},{2,1},{3,0},{4,7},{5,6},{6,5},{7,4},{8,11},{9,10},{10,... | collective-permute-start | bytes 589832 | tf_op jit(solution)/shard_map/ppermute | solution.py:414
  55.8 8.4 %collective-permute-start.10 = (bf16[1,16,2048]{2,1,0:T(8,128)(2,1)S(1)}, bf16[1,16,2048]{2,1,0:T(8,128)(2,1)S(1)}, u32[]{:S(2)}, u32[]{:S(2)}) collective-permute-start(bf16[1,16,2048]{2,1,0:T(8,128)(2,1)S(1)} %get-tuple-element.68), channel_id=1, source_target_pairs={{0,2},{1,3},{2,0},{3,1},{4,6},{5,7},{6,4},{7,5},{8,10},{9,11},{10,... | collective-permute-start | bytes 196616 | tf_op jit(solution)/shard_map/ppermute | solution.py:414
  56.7 7.6 %collective-permute-start.11 = (bf16[1,16,2048]{2,1,0:T(8,128)(2,1)S(1)}, bf16[1,16,2048]{2,1,0:T(8,128)(2,1)S(1)}, u32[]{:S(2)}, u32[]{:S(2)}) collective-permute-start(bf16[1,16,2048]{2,1,0:T(8,128)(2,1)S(1)} %get-tuple-element.69), channel_id=1, source_target_pairs={{0,3},{1,2},{2,1},{3,0},{4,7},{5,6},{6,5},{7,4},{8,11},{9,10},{10,... | collective-permute-start | bytes 196616 | tf_op jit(solution)/shard_map/ppermute | solution.py:414
  58.2 7.5 %collective-permute-start.7 = (bf16[2,16,2048]{2,1,0:T(8,128)(2,1)S(1)}, bf16[2,16,2048]{2,1,0:T(8,128)(2,1)S(1)}, u32[]{:S(2)}, u32[]{:S(2)}) collective-permute-start(bf16[2,16,2048]{2,1,0:T(8,128)(2,1)S(1)} %get-tuple-element.51), channel_id=1, source_target_pairs={{0,1},{1,0},{2,3},{3,2},{4,5},{5,4},{6,7},{7,6},{8,9},{9,8},{10,11... | collective-permute-start | bytes 393224 | tf_op jit(solution)/shard_map/ppermute | solution.py:414
  64.3 1.3 %collective-permute-start.12 = (bf16[1,16,2048]{2,1,0:T(8,128)(2,1)S(1)}, bf16[1,16,2048]{2,1,0:T(8,128)(2,1)S(1)}, u32[]{:S(2)}, u32[]{:S(2)}) collective-permute-start(bf16[1,16,2048]{2,1,0:T(8,128)(2,1)S(1)} %get-tuple-element.70), channel_id=1, source_target_pairs={{0,1},{1,0},{2,3},{3,2},{4,5},{5,4},{6,7},{7,6},{8,9},{9,8},{10,11... | collective-permute-start | bytes 196616 | tf_op jit(solution)/shard_map/ppermute | solution.py:414
  64.3 1.4 %collective-permute-start.13 = (bf16[1,16,2048]{2,1,0:T(8,128)(2,1)S(1)}, bf16[1,16,2048]{2,1,0:T(8,128)(2,1)S(1)}, u32[]{:S(2)}, u32[]{:S(2)}) collective-permute-start(bf16[1,16,2048]{2,1,0:T(8,128)(2,1)S(1)} %get-tuple-element.71), channel_id=1, source_target_pairs={{0,1},{1,0},{2,3},{3,2},{4,5},{5,4},{6,7},{7,6},{8,9},{9,8},{10,11... | collective-permute-start | bytes 196616 | tf_op jit(solution)/shard_map/ppermute | solution.py:414
